TPU v7x, 32 devices: a whole 2x2x4 slice. The times are simulated.
32 devices in a mesh: seq: 4 (over y, x), fsdp: 8 (over z, core).
Axes of the slice: x: 2, y: 2, z: 4, core: 2. Of those that a mesh axis runs over, the one named last changes fastest.
Arguments:
- layer_in: float32 [2, 4, 1024, 2048], P(None, 'seq', 'fsdp'), may hold values from -6 to 6
- doc_ids: int32 [2, 4, 1024], P(None, 'seq'), may hold values from 0 to 3, as said below
- out_grad: float32 [2, 4, 1024, 2048], P(None, 'seq', 'fsdp'), may hold values from -6 to 6
- query_weight: float32 [2048, 2048], P(('seq', 'fsdp')), may hold values from -0.125 to 0.125
- query_bias: float32 [2048], P(('seq', 'fsdp')), may hold values from -3 to 3
- key_weight: float32 [2048, 2048], P(('seq', 'fsdp')), may hold values from -0.1875 to 0.1875
- value_weight: float32 [2048, 2048], P(('seq', 'fsdp')), may hold values from -0.125 to 0.125
- value_bias: float32 [2048], P(('seq', 'fsdp')), may hold values from -2 to 2
- output_weight: float32 [2048, 2048], P(('seq', 'fsdp')), may hold values from -2 to 2
- output_bias: float32 [2048], P(('seq', 'fsdp')), may hold values from -3 to 3
- first_gain: float32 [2048], P(('seq', 'fsdp')), may hold values from 0.25 to 1.75
- first_shift: float32 [2048], P(('seq', 'fsdp')), may hold values from -2 to 2
- up_weight: float32 [2048, 8192], P(('seq', 'fsdp')), may hold values from -0.125 to 0.125
- up_bias: float32 [8192], P(('seq', 'fsdp')), may hold values from -3 to 3
- down_weight: float32 [8192, 2048], P(('seq', 'fsdp')), may hold values from -0.0625 to 0.0625
- down_bias: float32 [2048], P(('seq', 'fsdp')), may hold values from -3 to 3
- second_gain: float32 [2048], P(('seq', 'fsdp')), may hold values from 0.25 to 1.75
- second_shift: float32 [2048], P(('seq', 'fsdp')), may hold values from -2 to 2
Outputs:
- layer_out: float32 [2, 4, 1024, 2048], P(None, 'seq', 'fsdp')
- input_grad: float32 [2, 4, 1024, 2048], P(None, 'seq', 'fsdp')
- query_weight_grad: float32 [2048, 2048], P(('seq', 'fsdp'))
- query_bias_grad: float32 [2048], P(('seq', 'fsdp'))
- key_weight_grad: float32 [2048, 2048], P(('seq', 'fsdp'))
- value_weight_grad: float32 [2048, 2048], P(('seq', 'fsdp'))
- value_bias_grad: float32 [2048], P(('seq', 'fsdp'))
- output_weight_grad: float32 [2048, 2048], P(('seq', 'fsdp'))
- output_bias_grad: float32 [2048], P(('seq', 'fsdp'))
- first_gain_grad: float32 [2048], P(('seq', 'fsdp'))
- first_shift_grad: float32 [2048], P(('seq', 'fsdp'))
- up_weight_grad: float32 [2048, 8192], P(('seq', 'fsdp'))
- up_bias_grad: float32 [8192], P(('seq', 'fsdp'))
- down_weight_grad: float32 [8192, 2048], P(('seq', 'fsdp'))
- down_bias_grad: float32 [2048], P(('seq', 'fsdp'))
- second_gain_grad: float32 [2048], P(('seq', 'fsdp'))
- second_shift_grad: float32 [2048], P(('seq', 'fsdp'))
Inputs may be any that keep to these rules, and one draw needn't show every extreme that they name: `doc_ids`: within a sequence the document numbers never fall, every one of the 4 numbers occurs, and each document holds 102 to 718 tokens; in every draw some sequence has a document of exactly 718 tokens.
All inputs are finite; a program needn't handle non-finite values.
Results may differ from a plain program's by a relative error of at most 0.015.
The roundings to bfloat16 on the way count: a program that leaves them out, or rounds other values in their place, can miss the bound.
Values may be sent and summed in bfloat16 or wider, within the bound.
No kernel may reach another device: no remote copies, remote signals or barrier semaphores. Data moves between devices by JAX's collectives and lax.ppermute only.
A program may use at most 512 MiB of HBM per device.

v0:
```python
from functools import reduce

import jax
import jax.numpy as jnp
from jax import lax
from jax.sharding import PartitionSpec as P

D = 2048
H = 16
DH = 128
MB = 2


norm_eps = 1e-06
masked_score = -1e30


def normalize_forward(summed, gain_vector, shift_vector):
    center = summed - jnp.mean(summed, axis=-1, keepdims=True)
    inverse = lax.rsqrt(jnp.mean(center * center, axis=-1, keepdims=True) + norm_eps)
    normed = center * inverse
    return (normed * gain_vector + shift_vector, normed, inverse)


def normalize_backward(grad_output, normed, inverse, gain_vector):
    grad_normed = grad_output * gain_vector
    centered = grad_normed - jnp.mean(grad_normed, axis=-1, keepdims=True)
    grad_input = inverse * (
        centered - normed * jnp.mean(grad_normed * normed, axis=-1, keepdims=True)
    )
    return (grad_input, jnp.sum(grad_output * normed, axis=0), jnp.sum(grad_output, axis=0))


def masked_scores(query_heads, key_heads, row_ids, all_ids, score_scale):
    scores = (
        jnp.einsum("thd,shd->hts", query_heads, key_heads, preferred_element_type=jnp.float32)
        * score_scale
    )
    same_doc = row_ids[:, None] == all_ids[None, :]
    return jnp.where(same_doc[None], scores, masked_score)


def matmul(left, right):
    return jnp.dot(left, right, preferred_element_type=jnp.float32)


def transposed(left, right):
    return jnp.einsum("ti,tj->ij", left, right, preferred_element_type=jnp.float32)


def against(left, right):
    return jnp.einsum("ti,ji->tj", left, right, preferred_element_type=jnp.float32)


def gelu_tanh(argument):
    return jax.nn.gelu(argument, approximate=True)


def column_sum(matrix):
    return jnp.sum(matrix.astype(jnp.float32), axis=0)


def weight_terms(factors, norm_terms):
    (
        rounded_in,
        grad_query,
        grad_key,
        grad_value,
        mixed_rows,
        grad_branch,
        hidden_low,
        grad_up,
        active_low,
        grad_down,
    ) = factors
    first_gain_part, first_shift_part, second_gain_part, second_shift_part = norm_terms
    return (
        transposed(rounded_in, grad_query),
        column_sum(grad_query),
        transposed(rounded_in, grad_key),
        transposed(rounded_in, grad_value),
        column_sum(grad_value),
        transposed(mixed_rows, grad_branch),
        column_sum(grad_branch),
        first_gain_part,
        first_shift_part,
        transposed(hidden_low, grad_up),
        column_sum(grad_up),
        transposed(active_low, grad_down),
        column_sum(grad_down),
        second_gain_part,
        second_shift_part,
    )


def shards(
    layer_in,
    doc_ids,
    out_grad,
    query_weight,
    query_bias,
    key_weight,
    value_weight,
    value_bias,
    output_weight,
    output_bias,
    first_gain,
    first_shift,
    up_weight,
    up_bias,
    down_weight,
    down_bias,
    second_gain,
    second_shift,
):
    low_type = jnp.bfloat16
    wide_type = jnp.float32
    local = (
        query_weight.astype(low_type),
        query_bias.astype(low_type),
        key_weight.astype(low_type),
        value_weight.astype(low_type),
        value_bias.astype(low_type),
        output_weight.astype(low_type),
        output_bias.astype(low_type),
        first_gain.astype(low_type),
        first_shift.astype(low_type),
        up_weight.astype(low_type),
        up_bias.astype(low_type),
        down_weight.astype(low_type),
        down_bias.astype(low_type),
        second_gain.astype(low_type),
        second_shift.astype(low_type),
    )
    tokens_here = layer_in.shape[2]
    start_row = lax.axis_index("fsdp") * tokens_here
    score_scale = DH ** (-0.5)
    outputs = []
    input_grads = []
    grad_total = None
    stored_factors = []
    stored_norms = []
    (
        query_matrix,
        query_offset,
        key_matrix,
        value_matrix,
        value_offset,
        output_matrix,
        output_offset,
        first_scale,
        first_offset,
        up_matrix,
        up_offset,
        down_matrix,
        down_offset,
        second_scale,
        second_offset,
    ) = (
        lax.all_gather(local[0], ("seq", "fsdp"), axis=0, tiled=True),
        lax.all_gather(local[1], ("seq", "fsdp"), axis=0, tiled=True),
        lax.all_gather(local[2], ("seq", "fsdp"), axis=0, tiled=True),
        lax.all_gather(local[3], ("seq", "fsdp"), axis=0, tiled=True),
        lax.all_gather(local[4], ("seq", "fsdp"), axis=0, tiled=True),
        lax.all_gather(local[5], ("seq", "fsdp"), axis=0, tiled=True),
        lax.all_gather(local[6], ("seq", "fsdp"), axis=0, tiled=True),
        lax.all_gather(local[7], ("seq", "fsdp"), axis=0, tiled=True),
        lax.all_gather(local[8], ("seq", "fsdp"), axis=0, tiled=True),
        lax.all_gather(local[9], ("seq", "fsdp"), axis=0, tiled=True),
        lax.all_gather(local[10], ("seq", "fsdp"), axis=0, tiled=True),
        lax.all_gather(local[11], ("seq", "fsdp"), axis=0, tiled=True),
        lax.all_gather(local[12], ("seq", "fsdp"), axis=0, tiled=True),
        lax.all_gather(local[13], ("seq", "fsdp"), axis=0, tiled=True),
        lax.all_gather(local[14], ("seq", "fsdp"), axis=0, tiled=True),
    )
    for portion in range(MB):
        inputs = layer_in[portion, 0]
        all_ids = doc_ids[portion, 0]
        row_ids = lax.dynamic_slice_in_dim(all_ids, start_row, tokens_here)
        rounded_in = inputs.astype(low_type)
        query_rows = (matmul(rounded_in, query_matrix) + query_offset.astype(wide_type)).astype(
            low_type
        )
        key_rows = matmul(rounded_in, key_matrix).astype(low_type)
        value_rows = (matmul(rounded_in, value_matrix) + value_offset.astype(wide_type)).astype(
            low_type
        )
        key_whole, value_whole = (
            lax.all_gather(key_rows, "fsdp", axis=0, tiled=True),
            lax.all_gather(value_rows, "fsdp", axis=0, tiled=True),
        )
        length = key_whole.shape[0]
        query_heads = query_rows.reshape(tokens_here, H, DH)
        key_heads = key_whole.reshape(length, H, DH)
        value_heads = value_whole.reshape(length, H, DH)
        scores = masked_scores(query_heads, key_heads, row_ids, all_ids, score_scale)
        row_max = jnp.max(scores, axis=-1, keepdims=True)
        log_total = row_max + jnp.log(jnp.sum(jnp.exp(scores - row_max), axis=-1, keepdims=True))
        attend_low = jnp.exp(scores - log_total).astype(low_type)
        mixed_rows = jnp.einsum(
            "hts,shd->thd", attend_low, value_heads, preferred_element_type=wide_type
        )
        mixed_rows = mixed_rows.reshape(tokens_here, D).astype(low_type)
        branch = matmul(mixed_rows, output_matrix) + output_offset.astype(wide_type)
        hidden, first_normed, first_inverse = normalize_forward(
            inputs + branch, first_scale.astype(wide_type), first_offset.astype(wide_type)
        )
        hidden_low = hidden.astype(low_type)
        up_rows = matmul(hidden_low, up_matrix) + up_offset.astype(wide_type)
        active, gelu_back = jax.vjp(gelu_tanh, up_rows)
        active_low = active.astype(low_type)
        down_rows = matmul(active_low, down_matrix) + down_offset.astype(wide_type)
        result, second_normed, second_inverse = normalize_forward(
            hidden + down_rows, second_scale.astype(wide_type), second_offset.astype(wide_type)
        )
        outputs.append(result)
        (
            query_back,
            key_back,
            value_back,
            output_back,
            first_back,
            up_back,
            down_back,
            second_back,
        ) = (
            query_matrix,
            key_matrix,
            value_matrix,
            output_matrix,
            first_scale,
            up_matrix,
            down_matrix,
            second_scale,
        )
        grad_output = out_grad[portion, 0]
        grad_second, second_gain_part, second_shift_part = normalize_backward(
            grad_output, second_normed, second_inverse, second_back.astype(wide_type)
        )
        grad_down = grad_second.astype(low_type)
        grad_active = against(grad_down, down_back)
        grad_up = gelu_back(grad_active)[0].astype(low_type)
        grad_hidden = grad_second + against(grad_up, up_back)
        grad_first, first_gain_part, first_shift_part = normalize_backward(
            grad_hidden, first_normed, first_inverse, first_back.astype(wide_type)
        )
        grad_branch = grad_first.astype(low_type)
        grad_mixed = against(grad_branch, output_back).astype(low_type)
        grad_heads = grad_mixed.reshape(tokens_here, H, DH)
        scores = masked_scores(query_heads, key_heads, row_ids, all_ids, score_scale)
        attend = jnp.exp(scores - log_total)
        grad_attend = jnp.einsum(
            "thd,shd->hts", grad_heads, value_heads, preferred_element_type=wide_type
        )
        row_dot = jnp.sum(attend * grad_attend, axis=-1, keepdims=True)
        grad_scores = (attend * (grad_attend - row_dot)).astype(low_type)
        grad_query = (
            jnp.einsum("hts,shd->thd", grad_scores, key_heads, preferred_element_type=wide_type)
            * score_scale
        )
        grad_query = grad_query.reshape(tokens_here, D).astype(low_type)
        key_part = (
            jnp.einsum("hts,thd->shd", grad_scores, query_heads, preferred_element_type=wide_type)
            * score_scale
        )
        value_part = jnp.einsum(
            "hts,thd->shd", attend.astype(low_type), grad_heads, preferred_element_type=wide_type
        )
        key_sum, value_sum = (
            lax.psum_scatter(
                key_part.reshape(length, D).astype(jnp.bfloat16),
                "fsdp",
                scatter_dimension=0,
                tiled=True,
            ).astype(jnp.float32),
            lax.psum_scatter(
                value_part.reshape(length, D).astype(jnp.bfloat16),
                "fsdp",
                scatter_dimension=0,
                tiled=True,
            ).astype(jnp.float32),
        )
        grad_key = key_sum.astype(low_type)
        grad_value = value_sum.astype(low_type)
        input_grads.append(
            grad_first
            + against(grad_query, query_back)
            + against(grad_key, key_back)
            + against(grad_value, value_back)
        )
        factors = (
            rounded_in,
            grad_query,
            grad_key,
            grad_value,
            mixed_rows,
            grad_branch,
            hidden_low,
            grad_up,
            active_low,
            grad_down,
        )
        norm_terms = (first_gain_part, first_shift_part, second_gain_part, second_shift_part)
        stored_factors.append(factors)
        stored_norms.append(norm_terms)
    joined = tuple(
        (jnp.concatenate([entry[index] for entry in stored_factors], axis=0) for index in range(10))
    )
    summed_norms = tuple(
        (reduce(jnp.add, [entry[index] for entry in stored_norms]) for index in range(4))
    )
    terms = weight_terms(joined, summed_norms)
    grad_total = (
        lax.psum_scatter(terms[0], ("seq", "fsdp"), scatter_dimension=0, tiled=True),
        lax.psum_scatter(terms[1], ("seq", "fsdp"), scatter_dimension=0, tiled=True),
        lax.psum_scatter(terms[2], ("seq", "fsdp"), scatter_dimension=0, tiled=True),
        lax.psum_scatter(terms[3], ("seq", "fsdp"), scatter_dimension=0, tiled=True),
        lax.psum_scatter(terms[4], ("seq", "fsdp"), scatter_dimension=0, tiled=True),
        lax.psum_scatter(terms[5], ("seq", "fsdp"), scatter_dimension=0, tiled=True),
        lax.psum_scatter(terms[6], ("seq", "fsdp"), scatter_dimension=0, tiled=True),
        lax.psum_scatter(terms[7], ("seq", "fsdp"), scatter_dimension=0, tiled=True),
        lax.psum_scatter(terms[8], ("seq", "fsdp"), scatter_dimension=0, tiled=True),
        lax.psum_scatter(terms[9], ("seq", "fsdp"), scatter_dimension=0, tiled=True),
        lax.psum_scatter(terms[10], ("seq", "fsdp"), scatter_dimension=0, tiled=True),
        lax.psum_scatter(terms[11], ("seq", "fsdp"), scatter_dimension=0, tiled=True),
        lax.psum_scatter(terms[12], ("seq", "fsdp"), scatter_dimension=0, tiled=True),
        lax.psum_scatter(terms[13], ("seq", "fsdp"), scatter_dimension=0, tiled=True),
        lax.psum_scatter(terms[14], ("seq", "fsdp"), scatter_dimension=0, tiled=True),
    )
    layer_out = jnp.stack(outputs)[:, None]
    input_grad = jnp.stack(input_grads)[:, None]
    return (
        layer_out,
        input_grad,
        grad_total[0],
        grad_total[1],
        grad_total[2],
        grad_total[3],
        grad_total[4],
        grad_total[5],
        grad_total[6],
        grad_total[7],
        grad_total[8],
        grad_total[9],
        grad_total[10],
        grad_total[11],
        grad_total[12],
        grad_total[13],
        grad_total[14],
    )


def solution(mesh):
    placed = (
        P(None, "seq", "fsdp", None),
        P(None, "seq", None),
        P(None, "seq", "fsdp", None),
        P(("seq", "fsdp"), None),
        P(("seq", "fsdp")),
        P(("seq", "fsdp"), None),
        P(("seq", "fsdp"), None),
        P(("seq", "fsdp")),
        P(("seq", "fsdp"), None),
        P(("seq", "fsdp")),
        P(("seq", "fsdp")),
        P(("seq", "fsdp")),
        P(("seq", "fsdp"), None),
        P(("seq", "fsdp")),
        P(("seq", "fsdp"), None),
        P(("seq", "fsdp")),
        P(("seq", "fsdp")),
        P(("seq", "fsdp")),
    )
    return jax.shard_map(
        shards,
        mesh=mesh,
        in_specs=placed,
        out_specs=(
            P(None, "seq", "fsdp", None),
            P(None, "seq", "fsdp", None),
            P(("seq", "fsdp"), None),
            P(("seq", "fsdp")),
            P(("seq", "fsdp"), None),
            P(("seq", "fsdp"), None),
            P(("seq", "fsdp")),
            P(("seq", "fsdp"), None),
            P(("seq", "fsdp")),
            P(("seq", "fsdp")),
            P(("seq", "fsdp")),
            P(("seq", "fsdp"), None),
            P(("seq", "fsdp")),
            P(("seq", "fsdp"), None),
            P(("seq", "fsdp")),
            P(("seq", "fsdp")),
            P(("seq", "fsdp")),
        ),
        check_vma=False,
    )
```

profile of v0, /device:TPU:0, one launch (start us, length us, event | category | flops | bytes accessed | tf_op | source)
XLA Modules:
  0.0 3573.6 jit_solution(3197997986055923323)
XLA Ops:
  14.5 77.2 %all-gather.18.cloned.1.call-done = bf16[2048,2048]{1,0:T(8,128)(2,1)} async-done(((bf16[64,2048]{1,0:T(8,128)(2,1)}), bf16[2048,2048]{1,0:T(8,128)(2,1)}) %all-gather.18.cloned.1.call-update) | async-done | bytes 8388624 | tf_op jit(solution)/shard_map/all_gather | solution.py:162
  104.9 40.1 %all-reduce.18 = (bf16[2048]{0:T(1024)(128)(2,1)S(1)}, bf16[2048]{0:T(1024)(128)(2,1)S(1)}, bf16[2048]{0:T(1024)(128)(2,1)S(1)}, bf16[2048]{0:T(1024)(128)(2,1)S...) all-reduce(bf16[2048]{0:T(1024)(128)(2,1)S(1)} %dynamic-update-slic, ...), channel_id=1, replica_groups=mesh['seq'=4,'fsdp'=8] {'seq','fsdp'}, use_global_device_ids=true, to_apply=%add | all-reduce | flops 16384 | bytes 65536
  145.0 26.3 all-gather.12.cloned.1.call-done
  187.3 50.1 %all-gather = bf16[32,1,256]{2,1,0:T(2,128)(2,1)S(1)} all-gather(bf16[1,1,256]{2,1,0:T(2,128)(2,1)S(1)} %reshape.277), channel_id=1, replica_groups=mesh['seq'=4,'fsdp'=8] {'seq','fsdp'}, dimensions={0}, use_global_device_ids=true | all-gather | bytes 16896 | tf_op jit(solution)/shard_map/all_gather | solution.py:170
  262.1 36.9 %all-gather.20.cloned.1.call-done = bf16[1024,2048]{1,0:T(8,128)(2,1)} async-done(((bf16[128,2048]{1,0:T(8,128)(2,1)}), bf16[1024,2048]{1,0:T(8,128)(2,1)}) %all-gather.20.cloned.1.call-update) | async-done | bytes 4194320 | tf_op jit(solution)/shard_map/all_gather | solution.py:189
  305.4 41.5 %all-gather.30.cloned.1.call-done = bf16[1024,2048]{1,0:T(8,128)(2,1)} async-done(((bf16[128,2048]{1,0:T(8,128)(2,1)}), bf16[1024,2048]{1,0:T(8,128)(2,1)}) %all-gather.30.cloned.1.call-update) | async-done | bytes 4194320 | tf_op jit(solution)/shard_map/all_gather | solution.py:189
  360.9 33.9 all-gather.28.cloned.1.call-done
  403.0 71.5 %all-gather.22.cloned.1.call-done = bf16[2048,2048]{1,0:T(8,128)(2,1)} async-done(((bf16[64,2048]{1,0:T(8,128)(2,1)}), bf16[2048,2048]{1,0:T(8,128)(2,1)}) %all-gather.22.cloned.1.call-update) | async-done | bytes 8388624 | tf_op jit(solution)/shard_map/all_gather | solution.py:165
  485.2 37.3 %all-gather.14.cloned.1.call-done = bf16[1024,2048]{1,0:T(8,128)(2,1)} async-done(((bf16[128,2048]{1,0:T(8,128)(2,1)}), bf16[1024,2048]{1,0:T(8,128)(2,1)}) %all-gather.14.cloned.1.call-update) | async-done | bytes 4194320 | tf_op jit(solution)/shard_map/all_gather | solution.py:190
  536.3 183.4 %all-gather.24.cloned.1.call-done = bf16[2048,8192]{1,0:T(8,128)(2,1)} async-done(((bf16[64,8192]{1,0:T(8,128)(2,1)}), bf16[2048,8192]{1,0:T(8,128)(2,1)}) %all-gather.24.cloned.1.call-update) | async-done | bytes 33554448 | tf_op jit(solution)/shard_map/all_gather | solution.py:169
  736.4 179.6 %all-gather.26.cloned.1.call-done = bf16[8192,2048]{1,0:T(8,128)(2,1)} async-done(((bf16[256,2048]{1,0:T(8,128)(2,1)}), bf16[8192,2048]{1,0:T(8,128)(2,1)}) %all-gather.26.cloned.1.call-update) | async-done | bytes 33554448 | tf_op jit(solution)/shard_map/all_gather | solution.py:171
  983.6 19.7 multiply_reduce_fusion.3
  1022.1 19.9 fusion.90
  1188.9 26.6 reduce-scatter.35.cloned.1.call-done
  1217.6 48.3 %reduce-scatter.31.cloned.1.call-done = bf16[128,2048]{1,0:T(8,128)(2,1)} async-done(((bf16[1024,2048]{1,0:T(8,128)(2,1)}), bf16[128,2048]{1,0:T(8,128)(2,1)}) %reduce-scatter.31.cloned.1.call-update) | async-done | bytes 524304
  1287.8 24.9 fusion.34
  1314.5 25.0 fusion.26
  1368.8 26.5 all-reduce.21.cloned.1.call-done
  1406.7 179.1 %reduce-scatter.19.cloned.1.call-done = f32[64,2048]{1,0:T(8,128)} async-done(((f32[2048,2048]{1,0:T(8,128)}), f32[64,2048]{1,0:T(8,128)}) %reduce-scatter.19.cloned.1.call-update) | async-done | bytes 524304 | tf_op jit(solution)/shard_map/reduce_scatter | solution.py:314
  1585.8 187.2 %reduce-scatter.25.cloned.1.call-done = f32[64,2048]{1,0:T(8,128)} async-done(((f32[2048,2048]{1,0:T(8,128)}), f32[64,2048]{1,0:T(8,128)}) %reduce-scatter.25.cloned.1.call-update) | async-done | bytes 524304 | tf_op jit(solution)/shard_map/reduce_scatter | solution.py:319
  1773.0 187.2 %reduce-scatter.21.cloned.1.call-done = f32[64,2048]{1,0:T(8,128)} async-done(((f32[2048,2048]{1,0:T(8,128)}), f32[64,2048]{1,0:T(8,128)}) %reduce-scatter.21.cloned.1.call-update) | async-done | bytes 524304 | tf_op jit(solution)/shard_map/reduce_scatter | solution.py:316
  1960.2 187.3 %reduce-scatter.23.cloned.1.call-done = f32[64,2048]{1,0:T(8,128)} async-done(((f32[2048,2048]{1,0:T(8,128)}), f32[64,2048]{1,0:T(8,128)}) %reduce-scatter.23.cloned.1.call-update) | async-done | bytes 524304 | tf_op jit(solution)/shard_map/reduce_scatter | solution.py:317
  2147.6 710.0 %reduce-scatter.27.cloned.1.call-done = f32[64,8192]{1,0:T(8,128)} async-done(((f32[2048,8192]{1,0:T(8,128)}), f32[64,8192]{1,0:T(8,128)}) %reduce-scatter.27.cloned.1.call-update) | async-done | bytes 2097168 | tf_op jit(solution)/shard_map/reduce_scatter | solution.py:323
  2857.6 709.0 %reduce-scatter.29.cloned.1.call-done = f32[256,2048]{1,0:T(8,128)} async-done(((f32[8192,2048]{1,0:T(8,128)}), f32[256,2048]{1,0:T(8,128)}) %reduce-scatter.29.cloned.1.call-update) | async-done | bytes 2097168 | tf_op jit(solution)/shard_map/reduce_scatter | solution.py:325
  (322 shorter events, 429.3 us)
Async XLA Ops:
  7.2 84.5 %all-gather.18.cloned.1.call-start = ((), (), s32[]{:S(2)}) async-start(), calls=%async_computation.13 | async-start | bytes 8650752 | tf_op jit(solution)/shard_map/all_gather | solution.py:162
  9.0 162.3 %all-gather.12.cloned.1.call-start = ((), (), s32[]{:S(2)}) async-start(), calls=%async_computation.10 | async-start | bytes 8650752 | tf_op jit(solution)/shard_map/all_gather | solution.py:163
  10.9 240.3 %all-gather.16.cloned.1.call-start = ((), (), s32[]{:S(2)}) async-start(), calls=%async_computation.12 | async-start | bytes 8650752 | tf_op jit(solution)/shard_map/all_gather | solution.py:160
  12.7 286.2 %all-gather.20.cloned.1.call-start = ((), (), s32[]{:S(2)}) async-start(), calls=%async_computation.14 | async-start | bytes 4718592 | tf_op jit(solution)/shard_map/all_gather | solution.py:189
  14.5 236.7 %copy-start.2 = (bf16[128,2048]{1,0:T(8,128)(2,1)}, bf16[128,2048]{1,0:T(8,128)(2,1)S(1)}, u32[]{:S(2)}) copy-start(bf16[128,2048]{1,0:T(8,128)(2,1)S(1)} %get-tuple-element.96) | copy-start | bytes 1572868
  14.5 242.3 %copy-start.4 = (bf16[128,2048]{1,0:T(8,128)(2,1)}, bf16[128,2048]{1,0:T(8,128)(2,1)S(1)}, u32[]{:S(2)}) copy-start(bf16[128,2048]{1,0:T(8,128)(2,1)S(1)} %get-tuple-element.97) | copy-start | bytes 1572868
  97.2 249.7 %all-gather.30.cloned.1.call-start = ((), (), s32[]{:S(2)}) async-start(), calls=%async_computation.19 | async-start | bytes 4718592 | tf_op jit(solution)/shard_map/all_gather | solution.py:189
  102.8 292.0 %all-gather.28.cloned.1.call-start = ((), (), s32[]{:S(2)}) async-start(), calls=%async_computation.18 | async-start | bytes 4718592 | tf_op jit(solution)/shard_map/all_gather | solution.py:190
  176.8 297.7 %all-gather.22.cloned.1.call-start = ((), (), s32[]{:S(2)}) async-start(), calls=%async_computation.15 | async-start | bytes 8650752 | tf_op jit(solution)/shard_map/all_gather | solution.py:165
  177.6 344.9 %all-gather.14.cloned.1.call-start = ((), (), s32[]{:S(2)}) async-start(), calls=%async_computation.11 | async-start | bytes 4718592 | tf_op jit(solution)/shard_map/all_gather | solution.py:190
  183.3 536.4 %all-gather.24.cloned.1.call-start = ((), (), s32[]{:S(2)}) async-start(), calls=%async_computation.16 | async-start | bytes 34603008 | tf_op jit(solution)/shard_map/all_gather | solution.py:169
  184.4 731.6 %all-gather.26.cloned.1.call-start = ((), (), s32[]{:S(2)}) async-start(), calls=%async_computation.17 | async-start | bytes 34603008 | tf_op jit(solution)/shard_map/all_gather | solution.py:171
  187.2 963.6 %reduce-scatter.37.cloned.1.call-start = ((), (), s32[]{:S(2)}) async-start(), calls=%async_computation.29 | async-start | bytes 4718592
  536.2 393.7 %copy-start.41 = (bf16[128,2048]{1,0:T(8,128)(2,1)}, bf16[128,2048]{1,0:T(8,128)(2,1)S(1)}, u32[]{:S(2)}) copy-start(bf16[128,2048]{1,0:T(8,128)(2,1)S(1)} %get-tuple-element.101) | copy-start | bytes 1572868
  1066.4 98.7 %reduce-scatter.33.cloned.1.call-start = ((), (), s32[]{:S(2)}) async-start(), calls=%async_computation.27 | async-start | bytes 4718592
  1087.7 127.8 %reduce-scatter.35.cloned.1.call-start = ((), (), s32[]{:S(2)}) async-start(), calls=%async_computation.28 | async-start | bytes 4718592
  1111.3 154.6 %reduce-scatter.31.cloned.1.call-start = ((), (), s32[]{:S(2)}) async-start(), calls=%async_computation.26 | async-start | bytes 4718592
  1134.8 260.5 %all-reduce.21.cloned.1.call-start = ((), (), s32[]{:S(2)}) async-start(), calls=%async_computation.30 | async-start | bytes 196608
  1169.3 416.5 %reduce-scatter.19.cloned.1.call-start = ((), (), s32[]{:S(2)}) async-start(), calls=%async_computation.20 | async-start | bytes 17301504 | tf_op jit(solution)/shard_map/reduce_scatter | solution.py:314
  1179.1 593.9 %reduce-scatter.25.cloned.1.call-start = ((), (), s32[]{:S(2)}) async-start(), calls=%async_computation.23 | async-start | bytes 17301504 | tf_op jit(solution)/shard_map/reduce_scatter | solution.py:319
  1188.8 771.4 %reduce-scatter.21.cloned.1.call-start = ((), (), s32[]{:S(2)}) async-start(), calls=%async_computation.21 | async-start | bytes 17301504 | tf_op jit(solution)/shard_map/reduce_scatter | solution.py:316
  1277.3 870.3 %reduce-scatter.23.cloned.1.call-start = ((), (), s32[]{:S(2)}) async-start(), calls=%async_computation.22 | async-start | bytes 17301504 | tf_op jit(solution)/shard_map/reduce_scatter | solution.py:317
  1286.7 1570.9 %reduce-scatter.27.cloned.1.call-start = ((), (), s32[]{:S(2)}) async-start(), calls=%async_computation.24 | async-start | bytes 69206016 | tf_op jit(solution)/shard_map/reduce_scatter | solution.py:323
  1312.7 2253.9 %reduce-scatter.29.cloned.1.call-start = ((), (), s32[]{:S(2)}) async-start(), calls=%async_computation.25 | async-start | bytes 69206016 | tf_op jit(solution)/shard_map/reduce_scatter | solution.py:325
  (60 other events, 1012.5 us)
Sparse Core Ops, SparseCore 0:
  11.6 80.0 all-gather.17
  95.3 76.0 all-gather.11
  174.9 76.2 all-gather.15
  253.2 45.7 all-gather.19
  301.0 45.8 all-gather.29
  348.9 45.8 all-gather.27
  398.4 76.1 all-gather.21
  476.7 45.7 all-gather.13
  526.0 193.5 all-gather.23
  723.0 192.9 all-gather.25
  1066.5 48.1 reduce-scatter.36
  1116.9 48.1 reduce-scatter.32
  1167.4 48.1 reduce-scatter.34
  1217.7 48.1 reduce-scatter.30
  1272.1 123.1 all-reduce.20
  1398.1 187.6 reduce-scatter.18
  1588.6 184.3 reduce-scatter.24
  1775.8 184.3 reduce-scatter.20
  1963.2 184.3 reduce-scatter.22
  2150.5 707.0 reduce-scatter.26
  2860.6 705.9 reduce-scatter.28
where the time goes:
time: 3580 us; the launch traced here: 3570 us
  waiting for transfers between devices  2970 us (83%)
  matrix products  372 us (10%)
  blocking collectives  90.2 us (3%)
  local copies, waits for them, and re-layouts  73.9 us (2%)
  other arithmetic  45.7 us (1%)
    reduce_scatter x1, waiting for transfers between devices, shards(): lax.psum_scatter(terms[9], ('seq', 'fsdp'), scatter_dimension=0, tiled=True)  710 us
    reduce_scatter x1, waiting for transfers between devices, shards(): lax.psum_scatter(terms[11], ('seq', 'fsdp'), scatter_dimension=0, tiled=T...  709 us
    reduce_scatter x1, waiting for transfers between devices, shards(): lax.psum_scatter(terms[3], ('seq', 'fsdp'), scatter_dimension=0, tiled=True)  187 us
    reduce_scatter x1, waiting for transfers between devices, shards(): lax.psum_scatter(terms[2], ('seq', 'fsdp'), scatter_dimension=0, tiled=True)  187 us
    reduce_scatter x1, waiting for transfers between devices, shards(): lax.psum_scatter(terms[5], ('seq', 'fsdp'), scatter_dimension=0, tiled=True)  187 us
    all_gather x1, waiting for transfers between devices, shards(): lax.all_gather(local[9], ('seq', 'fsdp'), axis=0, tiled=True)  183 us
    all_gather x1, waiting for transfers between devices, shards(): lax.all_gather(local[11], ('seq', 'fsdp'), axis=0, tiled=True)  180 us
    reduce_scatter x1, waiting for transfers between devices, shards(): lax.psum_scatter(terms[0], ('seq', 'fsdp'), scatter_dimension=0, tiled=True)  179 us
  transfers between devices with their start and end apart: 21, of which 20 were waited for; matrix products, arithmetic and copies ran while one was open for 9% of the time, Pallas kernels for 0%

commit v1 on v0

v1 whole, which is shorter than its diff:
```python
import functools

import jax
import jax.numpy as jnp
from jax import lax
from jax.experimental import pallas as pl
from jax.experimental.pallas import tpu as pltpu
from jax.sharding import Mesh
from jax.sharding import PartitionSpec as P

D = 2048
H = 16
DH = 128
MB = 2
CORES = 2

low = jnp.bfloat16
wide = jnp.float32
norm_eps = 1e-06
masked_score = -1e30
score_scale = DH ** (-0.5)
ALL = ("seq", "z", "c")


def normalize_forward(summed, gain_vector, shift_vector):
    center = summed - jnp.mean(summed, axis=-1, keepdims=True)
    inverse = lax.rsqrt(jnp.mean(center * center, axis=-1, keepdims=True) + norm_eps)
    normed = center * inverse
    return (normed * gain_vector + shift_vector, normed, inverse)


def normalize_backward(grad_output, normed, inverse, gain_vector):
    grad_normed = grad_output * gain_vector
    centered = grad_normed - jnp.mean(grad_normed, axis=-1, keepdims=True)
    grad_input = inverse * (
        centered - normed * jnp.mean(grad_normed * normed, axis=-1, keepdims=True)
    )
    return (grad_input, jnp.sum(grad_output * normed, axis=0), jnp.sum(grad_output, axis=0))


def matmul(left, right):
    return jnp.dot(left, right, preferred_element_type=wide)


def transposed(left, right):
    return jnp.einsum("ti,tj->ij", left, right, preferred_element_type=wide)


def against(left, right):
    return jnp.einsum("ti,ji->tj", left, right, preferred_element_type=wide)


def column_sum(matrix):
    return jnp.sum(matrix.astype(wide), axis=0)


def gelu_both(u):
    root = (2.0 / jnp.pi) ** 0.5
    cubic = 0.044715
    square = u * u
    bend = jnp.tanh(root * (u + cubic * u * square))
    half = 0.5 * (1.0 + bend)
    slope = half + 0.5 * u * (1.0 - bend * bend) * (root * (1.0 + 3.0 * cubic * square))
    return u * half, slope


def nt(left, right):
    return lax.dot_general(left, right, (((1,), (1,)), ((), ())), preferred_element_type=wide)


def tn(left, right):
    return lax.dot_general(left, right, (((0,), (0,)), ((), ())), preferred_element_type=wide)


def attend_kernel(rows, q_ref, k_ref, v_ref, row_ref, col_ref, o_ref, total_ref):
    keys = k_ref[...]
    values = v_ref[...]
    cols = col_ref[...]
    for start in range(0, q_ref.shape[0], rows):
        here = pl.ds(start, rows)
        scores = nt(q_ref[here, :], keys) * score_scale
        scores = jnp.where(row_ref[here, :] == cols, scores, masked_score)
        top = jnp.max(scores, axis=-1, keepdims=True)
        raised = jnp.exp(scores - top)
        total = jnp.sum(raised, axis=-1, keepdims=True)
        probs = (raised * (1.0 / total)).astype(low)
        o_ref[here, :] = jnp.dot(probs, values, preferred_element_type=wide).astype(low)
        total_ref[0, here, :] = top + jnp.log(total)


def attend_back_kernel(
    rows, q_ref, k_ref, v_ref, g_ref, total_ref, row_ref, col_ref, dq_ref, dk_ref, dv_ref, ka, va
):
    keys = k_ref[...]
    values = v_ref[...]
    cols = col_ref[...]
    for start in range(0, q_ref.shape[0], rows):
        here = pl.ds(start, rows)
        queries = q_ref[here, :]
        grads = g_ref[here, :]
        scores = nt(queries, keys) * score_scale
        scores = jnp.where(row_ref[here, :] == cols, scores, masked_score)
        probs = jnp.exp(scores - total_ref[0, here, :])
        grad_probs = nt(grads, values)
        row_dot = jnp.sum(probs * grad_probs, axis=-1, keepdims=True)
        grad_scores = (probs * (grad_probs - row_dot)).astype(low)
        dq_ref[here, :] = (
            jnp.dot(grad_scores, keys, preferred_element_type=wide) * score_scale
        ).astype(low)
        dk_part = tn(grad_scores, queries)
        dv_part = tn(probs.astype(low), grads)
        if start == 0:
            ka[...] = dk_part
            va[...] = dv_part
        else:
            ka[...] += dk_part
            va[...] += dv_part
    dk_ref[...] = (ka[...] * score_scale).astype(low)
    dv_ref[...] = va[...].astype(low)


def attend(qkv, row_ids, col_ids, heads):
    length = qkv.shape[0]
    rows = min(256, length)
    block = lambda part: pl.BlockSpec((length, DH), lambda h: (0, part * heads + h))
    return pl.pallas_call(
        functools.partial(attend_kernel, rows),
        grid=(heads,),
        in_specs=[
            block(0),
            block(1),
            block(2),
            pl.BlockSpec((length, 1), lambda h: (0, 0)),
            pl.BlockSpec((1, length), lambda h: (0, 0)),
        ],
        out_specs=[
            pl.BlockSpec((length, DH), lambda h: (0, h)),
            pl.BlockSpec((1, length, 1), lambda h: (h, 0, 0)),
        ],
        out_shape=[
            jax.ShapeDtypeStruct((length, heads * DH), low),
            jax.ShapeDtypeStruct((heads, length, 1), wide),
        ],
        cost_estimate=pl.CostEstimate(
            flops=4 * heads * length * length * DH,
            bytes_accessed=8 * heads * length * DH,
            transcendentals=heads * length * length,
        ),
        compiler_params=pltpu.CompilerParams(vmem_limit_bytes=40 * 2**20),
        name="attend",
    )(qkv, qkv, qkv, row_ids, col_ids)


def attend_back(qkv, grad_mixed, totals, row_ids, col_ids, heads):
    length = qkv.shape[0]
    rows = min(256, length)
    block = lambda part: pl.BlockSpec((length, DH), lambda h: (0, part * heads + h))
    out = pl.BlockSpec((length, DH), lambda h: (0, h))
    shape = jax.ShapeDtypeStruct((length, heads * DH), low)
    return pl.pallas_call(
        functools.partial(attend_back_kernel, rows),
        grid=(heads,),
        in_specs=[
            block(0),
            block(1),
            block(2),
            out,
            pl.BlockSpec((1, length, 1), lambda h: (h, 0, 0)),
            pl.BlockSpec((length, 1), lambda h: (0, 0)),
            pl.BlockSpec((1, length), lambda h: (0, 0)),
        ],
        out_specs=[out, out, out],
        out_shape=[shape, shape, shape],
        scratch_shapes=[pltpu.VMEM((length, DH), wide), pltpu.VMEM((length, DH), wide)],
        cost_estimate=pl.CostEstimate(
            flops=10 * heads * length * length * DH,
            bytes_accessed=16 * heads * length * DH,
            transcendentals=heads * length * length,
        ),
        compiler_params=pltpu.CompilerParams(vmem_limit_bytes=48 * 2**20),
        name="attend_back",
    )(qkv, qkv, qkv, grad_mixed, totals, row_ids, col_ids)


def swap(value, axis, size, bit):
    return lax.ppermute(value, axis, [(i, i ^ bit) for i in range(size)])


def exchange(value, axis, size):
    here = lax.axis_index(axis)
    pick = lambda i: lax.dynamic_index_in_dim(value, i, 0, keepdims=True)
    result = value
    for k in range(1, size):
        came = swap(pick(here ^ k), axis, size, k)
        result = lax.dynamic_update_slice_in_dim(result, came, here ^ k, 0)
    return result


def bits(size):
    step = 1
    while step < size:
        yield step
        step *= 2


def sum_all(value, sizes):
    for axis in ("c", "z", "seq"):
        for bit in bits(sizes[axis]):
            value = value + swap(value, axis, sizes[axis], bit)
    return value


ENDS = [(0, 1), (1, 0), (2, 3), (3, 2)]
MIDDLE = [(1, 2), (2, 1)]
OUTWARD = [(1, 0), (2, 3)]
INWARD = [(0, 1), (3, 2)]


def gather_slots(own, axis, size):
    if size != 4:
        whole = lax.all_gather(own, axis, axis=0)
        return [whole[i] for i in range(size)]
    send = lambda value, pairs: lax.ppermute(value, axis, pairs)
    if axis == "z":
        inner = (lax.axis_index(axis) == 1) | (lax.axis_index(axis) == 2)
        first = send(own, ENDS)
        third_in = send(own, MIDDLE)
        second_in = send(first, MIDDLE)
        second_out = send(third_in, OUTWARD)
        third_out = send(second_in, OUTWARD)
        return [
            own,
            first,
            jnp.where(inner, second_in, second_out),
            jnp.where(inner, third_in, third_out),
        ]
    half = own.shape[0] // 2
    first = swap(own, axis, 4, 1)
    second = swap(own, axis, 4, 2)
    third_top = swap(first[:half], axis, 4, 2)
    third_end = swap(second[half:], axis, 4, 1)
    return [own, first, second, jnp.concatenate([third_top, third_end], axis=0)]


def scatter_slots(parts, axis, size):
    if size != 4:
        return lax.psum_scatter(jnp.stack(parts), axis, scatter_dimension=0, tiled=False).astype(
            wide
        )
    send = lambda value, pairs: lax.ppermute(value, axis, pairs)
    add = lambda a, b: (a.astype(wide) + b.astype(wide)).astype(low)
    own, first, second, third = parts
    if axis == "z":
        second_full = add(second, send(third, INWARD))
        third_full = add(third, send(second, INWARD))
        first_full = add(first, send(second_full, MIDDLE))
        from_middle = send(third_full, MIDDLE)
        from_end = send(first_full, ENDS)
        return own.astype(wide) + from_middle.astype(wide) + from_end.astype(wide)
    half = own.shape[0] // 2
    top = swap(third[:half], axis, 4, 2)
    end = swap(third[half:], axis, 4, 1)
    first_full = jnp.concatenate([add(first[:half], top), first[half:]], axis=0)
    second_full = jnp.concatenate([second[:half], add(second[half:], end)], axis=0)
    from_first = swap(first_full, axis, 4, 1)
    from_second = swap(second_full, axis, 4, 2)
    return own.astype(wide) + from_first.astype(wide) + from_second.astype(wide)


def slot_order(axis, size):
    order = jnp.arange(size)
    return order ^ lax.axis_index(axis) if size == 4 else order


def split_slots(value, size):
    step = value.shape[0] // size
    return [value[i * step : (i + 1) * step] for i in range(size)]


def shards(
    sizes,
    layer_in,
    doc_ids,
    out_grad,
    query_weight,
    query_bias,
    key_weight,
    value_weight,
    value_bias,
    output_weight,
    output_bias,
    first_gain,
    first_shift,
    up_weight,
    up_bias,
    down_weight,
    down_bias,
    second_gain,
    second_shift,
):
    S, Z, C = sizes["seq"], sizes["z"], sizes["c"]
    F = Z * C
    devices = S * F
    s, z, c = (lax.axis_index(a) for a in ALL)
    mine = (s * Z + z) * C + c
    rows = query_weight.shape[0]
    hidden_units = up_weight.shape[1]
    share = hidden_units // devices
    slice_width = hidden_units // S
    heads = H // Z
    tokens = layer_in.shape[2]
    whole_heads = rows * C == DH

    def to_core(value):
        keep = lax.dynamic_index_in_dim(value, c, 0, keepdims=False)[0]
        give = lax.dynamic_index_in_dim(value, 1 - c, 0, keepdims=False)[0]
        return jnp.concatenate([keep, swap(give, "c", C, 1)], axis=0)

    def from_core(value):
        keep, give = value[:tokens], value[tokens:]
        came = swap(give, "c", C, 1)
        first = jnp.where(c == 0, keep, came)
        second = jnp.where(c == 0, came, keep)
        return jnp.stack([first, second])[:, None]

    inputs = to_core(layer_in)
    rounded_in = inputs.astype(low)
    x_slots = gather_slots(rounded_in, "z", Z)

    packed = jnp.concatenate(
        [
            v.astype(low)
            for v in (
                query_bias,
                value_bias,
                output_bias,
                first_gain,
                first_shift,
                down_bias,
                second_gain,
                second_shift,
                up_bias,
            )
        ]
    )[None]
    vectors = sum_all(
        lax.dynamic_update_slice_in_dim(
            jnp.zeros((devices, packed.shape[1]), low), packed, mine, 0
        ),
        sizes,
    ).astype(wide)
    vector = lambda i: vectors[:, i * rows : (i + 1) * rows].reshape(D)
    by_head = lambda v: lax.dynamic_index_in_dim(v.reshape(heads, Z, DH), z, 1, keepdims=False)
    query_offset, value_offset = by_head(vector(0)), by_head(vector(1))
    (
        output_offset,
        first_scale,
        first_offset,
        down_offset,
        second_scale,
        second_offset,
    ) = (vector(i) for i in range(2, 8))
    up_offset = lax.dynamic_index_in_dim(
        vectors[:, 8 * rows :].reshape(S, slice_width), s, 0, keepdims=False
    )
    qkv_offset = jnp.concatenate(
        [query_offset.reshape(-1), jnp.zeros((heads * DH,), wide), value_offset.reshape(-1)]
    )

    width = 3 * heads * DH
    qkv_local = jnp.stack(
        [query_weight.astype(low), key_weight.astype(low), value_weight.astype(low)], axis=1
    )
    qkv_local = qkv_local.reshape(rows, 3, heads, Z, DH).transpose(3, 0, 1, 2, 4)
    qkv_local = exchange(qkv_local.reshape(Z, rows, width), "z", Z)
    qkv_matrix = lax.all_gather(qkv_local, ("seq", "c"), axis=0, tiled=False)
    qkv_matrix = qkv_matrix.reshape(S, C, Z, rows, width).transpose(0, 2, 1, 3, 4).reshape(D, width)
    if whole_heads:
        output_matrix = lax.all_gather(
            output_weight.astype(low), ("seq", "c"), axis=0, tiled=True
        )
    else:
        output_matrix = lax.all_gather(output_weight.astype(low), ALL, axis=0, tiled=True)
        output_matrix = lax.dynamic_index_in_dim(
            output_matrix.reshape(heads, Z, DH, D), z, 1, keepdims=False
        ).reshape(heads * DH, D)
    up_local = up_weight.astype(low).reshape(rows, S, slice_width).transpose(1, 0, 2)
    up_local = exchange(up_local, "seq", S)
    up_matrix = lax.all_gather(up_local, ("z", "c"), axis=0, tiled=False)
    up_matrix = up_matrix.transpose(1, 0, 2, 3).reshape(D, slice_width)
    down_matrix = lax.all_gather(down_weight.astype(low), ("z", "c"), axis=0, tiled=True)

    ids = lax.dynamic_index_in_dim(doc_ids, c, 0, keepdims=False)[0].reshape(Z, C, tokens)
    ids = jnp.where(c == 0, ids, ids[:, ::-1])
    ids = ids[slot_order("z", Z)].reshape(-1)
    row_ids, col_ids = ids[:, None], ids[None, :]

    x_all = jnp.concatenate(x_slots, axis=0)
    qkv = (matmul(x_all, qkv_matrix) + qkv_offset).astype(low)
    mixed, totals = attend(qkv, row_ids, col_ids, heads)
    branch_parts = split_slots(matmul(mixed, output_matrix).astype(low), Z)
    branch = scatter_slots(branch_parts, "z", Z) + output_offset
    hidden, first_normed, first_inverse = normalize_forward(
        inputs + branch, first_scale, first_offset
    )
    hidden_low = hidden.astype(low)

    h_slots = gather_slots(hidden_low, "seq", S)
    actives, slopes, downs = [], [], []
    for h_slot in h_slots:
        active, slope = gelu_both(matmul(h_slot, up_matrix) + up_offset)
        active = active.astype(low)
        actives.append(active)
        slopes.append(slope)
        downs.append(matmul(active, down_matrix).astype(low))
    down = scatter_slots(downs, "seq", S) + down_offset
    result, second_normed, second_inverse = normalize_forward(
        hidden + down, second_scale, second_offset
    )
    layer_out = from_core(result)

    grad_output = to_core(out_grad)
    grad_second, second_gain_part, second_shift_part = normalize_backward(
        grad_output, second_normed, second_inverse, second_scale
    )
    grad_down = grad_second.astype(low)
    g_slots = gather_slots(grad_down, "seq", S)
    grad_ups, hidden_parts = [], []
    for g_slot, slope in zip(g_slots, slopes, strict=True):
        grad_up = (against(g_slot, down_matrix) * slope).astype(low)
        grad_ups.append(grad_up)
        hidden_parts.append(against(grad_up, up_matrix).astype(low))
    grad_hidden = grad_second + scatter_slots(hidden_parts, "seq", S)

    joined = lambda values: jnp.concatenate(values, axis=0)
    down_term = transposed(joined(actives), joined(g_slots)).astype(low)
    down_weight_grad = lax.psum_scatter(
        down_term, ("z", "c"), scatter_dimension=0, tiled=True
    ).astype(wide)
    grad_up_all = joined(grad_ups)
    up_term = transposed(joined(h_slots), grad_up_all).astype(low)
    up_term = up_term.reshape(S, F, rows, slice_width).transpose(1, 0, 2, 3)
    up_mine = lax.psum_scatter(
        up_term.reshape(D, slice_width), ("z", "c"), scatter_dimension=0, tiled=True
    )
    up_mine = exchange(up_mine.reshape(S, rows, slice_width), "seq", S)
    up_weight_grad = up_mine.transpose(1, 0, 2).reshape(rows, hidden_units).astype(wide)

    grad_first, first_gain_part, first_shift_part = normalize_backward(
        grad_hidden, first_normed, first_inverse, first_scale
    )
    grad_branch = grad_first.astype(low)
    b_all = joined(gather_slots(grad_branch, "z", Z))
    grad_mixed = against(b_all, output_matrix).astype(low)
    grad_query, grad_key, grad_value = attend_back(
        qkv, grad_mixed, totals, row_ids, col_ids, heads
    )
    grad_qkv = jnp.concatenate([grad_query, grad_key, grad_value], axis=1)
    in_parts = split_slots(against(grad_qkv, qkv_matrix).astype(low), Z)
    input_grad = from_core(grad_first + scatter_slots(in_parts, "z", Z))

    qkv_term = transposed(x_all, grad_qkv).astype(low)
    qkv_term = qkv_term.reshape(S, Z, C, rows, width).transpose(0, 2, 1, 3, 4)
    qkv_mine = lax.psum_scatter(
        qkv_term.reshape(D, width), ("seq", "c"), scatter_dimension=0, tiled=True
    )
    qkv_mine = exchange(qkv_mine.reshape(Z, rows, width), "z", Z).reshape(Z, rows, 3, heads, DH)
    qkv_grads = qkv_mine.transpose(2, 1, 3, 0, 4).reshape(3, rows, D).astype(wide)
    output_term = transposed(mixed, b_all).astype(low)
    if whole_heads:
        output_weight_grad = lax.psum_scatter(
            output_term, ("seq", "c"), scatter_dimension=0, tiled=True
        ).astype(wide)
    else:
        output_term = lax.dynamic_update_slice_in_dim(
            jnp.zeros((heads, Z, DH, D), low), output_term.reshape(heads, 1, DH, D), z, 1
        )
        output_weight_grad = lax.psum_scatter(
            output_term.reshape(D, D), ALL, scatter_dimension=0, tiled=True
        ).astype(wide)

    spread = lambda v: lax.dynamic_update_slice_in_dim(
        jnp.zeros((heads, Z, DH), wide), v.reshape(heads, 1, DH), z, 1
    ).reshape(devices, rows)
    up_part = lax.dynamic_update_slice_in_dim(
        jnp.zeros((S, slice_width), wide), column_sum(grad_up_all)[None], s, 0
    ).reshape(devices, share)
    terms = [
        spread(column_sum(grad_query)),
        spread(column_sum(grad_value)),
        column_sum(grad_branch).reshape(devices, rows),
        first_gain_part.reshape(devices, rows),
        first_shift_part.reshape(devices, rows),
        column_sum(grad_down).reshape(devices, rows),
        second_gain_part.reshape(devices, rows),
        second_shift_part.reshape(devices, rows),
        up_part,
    ]
    sums = lax.dynamic_index_in_dim(
        sum_all(jnp.concatenate(terms, axis=1), sizes), mine, 0, keepdims=False
    )
    vec = lambda i: sums[i * rows : (i + 1) * rows]
    return (
        layer_out,
        input_grad,
        qkv_grads[0],
        vec(0),
        qkv_grads[1],
        qkv_grads[2],
        vec(1),
        output_weight_grad,
        vec(2),
        vec(3),
        vec(4),
        up_weight_grad,
        sums[8 * rows :],
        down_weight_grad,
        vec(5),
        vec(6),
        vec(7),
    )


def solution(mesh):
    sizes = {"seq": mesh.shape["seq"], "z": mesh.shape["fsdp"] // CORES, "c": CORES}
    inner = Mesh(mesh.devices.reshape(tuple(sizes[a] for a in ALL)), ALL)
    token = P(None, "seq", ("z", "c"), None)
    matrix = P(ALL, None)
    vector = P(ALL)
    return jax.shard_map(
        functools.partial(shards, sizes),
        mesh=inner,
        in_specs=(
            token,
            P(None, "seq", None),
            token,
            matrix,
            vector,
            matrix,
            matrix,
            vector,
            matrix,
            vector,
            vector,
            vector,
            matrix,
            vector,
            matrix,
            vector,
            vector,
            vector,
        ),
        out_specs=(
            token,
            token,
            matrix,
            vector,
            matrix,
            matrix,
            vector,
            matrix,
            vector,
            vector,
            vector,
            matrix,
            vector,
            matrix,
            vector,
            vector,
            vector,
        ),
        check_vma=False,
    )
```

time: 3580 us -> 1040 us (0.29)
  waiting for transfers between devices: 2970 us -> 534 us
  matrix products: 372 us -> 147 us
  starting transfers between devices: 1.86 us -> 154 us
  blocking collectives: 90.2 us -> 0 us
    reduce_scatter x6 -> x4, waiting for transfers between devices: 2160 us -> 8.56 us  [the longest x1 8.56 us: shards(): lax.psum_scatter(down_term, ('z', 'c'), scatter_dimension=0, tiled=True)]
    all_gather x10 -> x4, waiting for transfers between devices: 701 us -> 0.03 us  [the longest x1 0.02 us: shards(): up_matrix = lax.all_gather(up_local, ('z', 'c'), axis=0, tiled=False)]
    ppermute x0 -> x62, waiting for transfers between devices: none -> 525 us  [the longest x42 190 us: swap(): return lax.ppermute(value, axis, [(i, i ^ bit) for i in range(size)])]
    dot_general x42 -> x24, matrix products: 372 us -> 147 us  [the longest x10 55.4 us: matmul(): return jnp.dot(left, right, preferred_element_type=wide)]
    ppermute x0 -> x62, starting transfers between devices: none -> 154 us  [the longest x10 100 us: scatter_slots(): send = lambda value, pairs: lax.ppermute(value, axis, pairs)]
    unnamed x26 -> x8, waiting for transfers between devices: 114 us -> 0.13 us
    all_gather x1 -> x0, blocking collectives: 50.1 us -> none  [shards(): lax.all_gather(local[10], ('seq', 'fsdp'), axis=0, tiled=True)]
    unnamed x1 -> x0, blocking collectives: 40.1 us -> none
  transfers between devices with their start and end apart: 21 -> 70, of which waited for: 20 -> 38; matrix products, arithmetic and copies ran while one was open for 9% -> 25% of each run, Pallas kernels for 0% -> 3%
where the time goes in v1:
time: 1040 us; the launch traced here: 1030 us
  waiting for transfers between devices  534 us (51%)
  starting transfers between devices  154 us (15%)
  matrix products  147 us (14%)
  local copies, waits for them, and re-layouts  93.6 us (9%)
  other arithmetic  54.1 us (5%)
  Pallas kernels  30.1 us (3%)
  between operations  16.6 us (2%)
    ppermute x42, waiting for transfers between devices, swap(): return lax.ppermute(value, axis, [(i, i ^ bit) for i in range(size)])  190 us
    ppermute x10, waiting for transfers between devices, gather_slots(): send = lambda value, pairs: lax.ppermute(value, axis, pairs)  168 us
    ppermute x10, waiting for transfers between devices, scatter_slots(): send = lambda value, pairs: lax.ppermute(value, axis, pairs)  167 us
    ppermute x10, starting transfers between devices, scatter_slots(): send = lambda value, pairs: lax.ppermute(value, axis, pairs)  100 us
    dot_general x10, matrix products, matmul(): return jnp.dot(left, right, preferred_element_type=wide)  55.4 us
    dot_general x10, matrix products, against(): return jnp.einsum('ti,ji->tj', left, right, preferred_element_type=wide)  52.5 us
    ppermute x42, starting transfers between devices, swap(): return lax.ppermute(value, axis, [(i, i ^ bit) for i in range(size)])  43.5 us
    dot_general x4, matrix products, transposed(): return jnp.einsum('ti,tj->ij', left, right, preferred_element_type=wide)  38.8 us
  transfers between devices with their start and end apart: 70, of which 38 were waited for; matrix products, arithmetic and copies ran while one was open for 25% of the time, Pallas kernels for 3%

profile of v1, /device:TPU:0, one launch (start us, length us, event | category | flops | bytes accessed | tf_op | source)
XLA Modules:
  0.0 1029.2 jit_solution(17207972814662938966)
XLA Ops:
  18.8 14.5 %collective-permute-done.7 = bf16[1,64,1536]{2,1,0:T(8,128)(2,1)S(1)} collective-permute-done((bf16[1,64,1536]{2,1,0:T(8,128)(2,1)S(1)}, bf16[1,64,1536]{2,1,0:T(8,128)(2,1)S(1)}, u32[]{:S(2)}, u32[]{:S(2)}) %collective-permute-start.7) | collective-permute-done | bytes 196640 | tf_op jit(solution)/shard_map/ppermute | solution.py:186
  82.5 22.4 %collective-permute-done.1 = bf16[256,2048]{1,0:T(8,128)(2,1)} collective-permute-done((bf16[256,2048]{1,0:T(8,128)(2,1)S(1)}, bf16[256,2048]{1,0:T(8,128)(2,1)}, u32[]{:S(2)}, u32[]{:S(2)}) %collective-permute-start.1) | collective-permute-done | bytes 1048608 | tf_op jit(solution)/shard_map/ppermute | solution.py:223
  115.9 22.4 %collective-permute-done.11 = bf16[32,768]{1,0:T(8,128)(2,1)S(1)} collective-permute-done((bf16[32,768]{1,0:T(8,128)(2,1)S(1)}, bf16[32,768]{1,0:T(8,128)(2,1)S(1)}, u32[]{:S(2)}, u32[]{:S(2)}) %collective-permute-start.11) | collective-permute-done | bytes 49184 | tf_op jit(solution)/shard_map/ppermute | solution.py:186
  146.9 39.2 %collective-permute-done.4 = bf16[256,2048]{1,0:T(8,128)(2,1)S(1)} collective-permute-done((bf16[256,2048]{1,0:T(8,128)(2,1)}, bf16[256,2048]{1,0:T(8,128)(2,1)S(1)}, u32[]{:S(2)}, u32[]{:S(2)}) %collective-permute-start.4) | collective-permute-done | bytes 1048608 | tf_op jit(solution)/shard_map/ppermute | solution.py:223
  187.2 44.7 %collective-permute-done.5 = bf16[256,2048]{1,0:T(8,128)(2,1)} collective-permute-done((bf16[256,2048]{1,0:T(8,128)(2,1)}, bf16[256,2048]{1,0:T(8,128)(2,1)}, u32[]{:S(2)}, u32[]{:S(2)}) %collective-permute-start.5) | collective-permute-done | bytes 1048608 | tf_op jit(solution)/shard_map/ppermute | solution.py:223
  237.9 10.8 %add_convert_fusion.q_ref.k_ref.v_ref = bf16[1024,1536]{1,0:T(8,128)(2,1)S(1)} fusion(bf16[2048,1536]{1,0:T(8,128)(2,1)S(1)} %bitcast.157, f32[1536]{0:T(1024)S(1)} %pad_maximum_fusion.14, bf16[256,2048]{1,0:T(8,128)(2,1)S(1)} %copy-done.35, bf16[256,2048]{1,0:T(8,128)(2,1)S(1)} %copy-done.33, bf16[256,2048]{1,0:T(8,128)(2,1)} %collective-permute-done.1, ...), kind=kOutput, calls=%fused_computation.5 | convolution fusion | flops 6462373888 | bytes 13637632 | tf_op jit(solution)/shard_map/dot_general | solution.py:42
  248.8 11.8 %attend.1 = (bf16[1024,512]{1,0:T(8,128)(2,1)S(1)}, f32[4,1024,1]{2,1,0:T(8,128)S(1)}) custom-call(bf16[1024,1536]{1,0:T(8,128)(2,1)S(1)} %add_convert_fusion.q_ref.k_ref.v_ref, bf16[1024,1536]{1,0:T(8,128)(2,1)S(1)} %add_convert_fusion.q_ref.k_ref.v_ref, bf16[1024,1536]{1,0:T(8,128)(2,1)S(1)} %add_convert_fusion.q_ref.k_ref.v_ref, ...), custom_call_target="tpu_custom_call" | custom-call | flops 2147483648 | bytes 4194304 | tf_op jit(solution)/shard_map/attend/pallas_call | solution.py:126
  270.5 44.5 %collective-permute-done.14 = bf16[256,2048]{1,0:T(8,128)(2,1)S(1)} collective-permute-done((bf16[256,2048]{1,0:T(8,128)(2,1)S(1)}, bf16[256,2048]{1,0:T(8,128)(2,1)S(1)}, u32[]{:S(2)}, u32[]{:S(2)}) %collective-permute-start.14) | collective-permute-done | bytes 1048608 | tf_op jit(solution)/shard_map/ppermute | solution.py:250
  315.0 40.3 %collective-permute-done.16 = bf16[256,2048]{1,0:T(8,128)(2,1)S(1)} collective-permute-done((bf16[256,2048]{1,0:T(8,128)(2,1)S(1)}, bf16[256,2048]{1,0:T(8,128)(2,1)S(1)}, u32[]{:S(2)}, u32[]{:S(2)}) %collective-permute-start.16) | collective-permute-done | bytes 1048608 | tf_op jit(solution)/shard_map/ppermute | solution.py:250
  361.3 28.4 %collective-permute-start.18 = (bf16[256,2048]{1,0:T(8,128)(2,1)}, bf16[256,2048]{1,0:T(8,128)(2,1)}, u32[]{:S(2)}, u32[]{:S(2)}) collective-permute-start(bf16[256,2048]{1,0:T(8,128)(2,1)} %add_convert_fusion.4), channel_id=1, source_target_pairs={{0,2},{2,0},{4,6},{6,4},{1,3},{3,1},{5,7},{7,5},{8,10},{10,8},{12,... | collective-permute-start | bytes 3145736 | tf_op jit(solution)/shard_map/ppermute | solution.py:250
  389.9 13.2 %collective-permute-done.18 = bf16[256,2048]{1,0:T(8,128)(2,1)} collective-permute-done((bf16[256,2048]{1,0:T(8,128)(2,1)}, bf16[256,2048]{1,0:T(8,128)(2,1)}, u32[]{:S(2)}, u32[]{:S(2)}) %collective-permute-start.18) | collective-permute-done | bytes 1048608 | tf_op jit(solution)/shard_map/ppermute | solution.py:250
  504.5 18.8 %collective-permute-done.34 = bf16[256,2048]{1,0:T(8,128)(2,1)S(1)} collective-permute-done((bf16[256,2048]{1,0:T(8,128)(2,1)S(1)}, bf16[256,2048]{1,0:T(8,128)(2,1)S(1)}, u32[]{:S(2)}, u32[]{:S(2)}) %collective-permute-start.34) | collective-permute-done | bytes 1048608 | tf_op jit(solution)/shard_map/ppermute | solution.py:186
  593.3 18.3 %collective-permute-done.40 = bf16[256,2048]{1,0:T(8,128)(2,1)S(1)} collective-permute-done((bf16[256,2048]{1,0:T(8,128)(2,1)S(1)}, bf16[256,2048]{1,0:T(8,128)(2,1)S(1)}, u32[]{:S(2)}, u32[]{:S(2)}) %collective-permute-start.40) | collective-permute-done | bytes 1048608 | tf_op jit(solution)/shard_map/ppermute | solution.py:223
  615.0 20.8 %collective-permute-done.43 = bf16[256,2048]{1,0:T(8,128)(2,1)S(1)} collective-permute-done((bf16[256,2048]{1,0:T(8,128)(2,1)S(1)}, bf16[256,2048]{1,0:T(8,128)(2,1)S(1)}, u32[]{:S(2)}, u32[]{:S(2)}) %collective-permute-start.43) | collective-permute-done | bytes 1048608 | tf_op jit(solution)/shard_map/ppermute | solution.py:223
  635.8 22.4 %collective-permute-done.44 = bf16[256,2048]{1,0:T(8,128)(2,1)S(1)} collective-permute-done((bf16[256,2048]{1,0:T(8,128)(2,1)S(1)}, bf16[256,2048]{1,0:T(8,128)(2,1)S(1)}, u32[]{:S(2)}, u32[]{:S(2)}) %collective-permute-start.44) | collective-permute-done | bytes 1048608 | tf_op jit(solution)/shard_map/ppermute | solution.py:223
  668.7 18.3 %attend_back.1 = (bf16[1024,512]{1,0:T(8,128)(2,1)S(1)}, bf16[1024,512]{1,0:T(8,128)(2,1)S(1)}, bf16[1024,512]{1,0:T(8,128)(2,1)S(1)}) custom-call(bf16[1024,1536]{1,0:T(8,128)(2,1)} %copy-done.2, bf16[1024,1536]{1,0:T(8,128)(2,1)} %copy-done.2, bf16[1024,1536]{1,0:T(8,128)(2,1)} %copy-done.2, bf16[1024,512]{1,0:T(8,128)(2,1)S(1)} %convolution_convert_fusion.14.g_ref, ...), custom_call_target="tpu_custom_call" | custom-call | flops 5368709120 | bytes 8388608 | tf_op jit(solution)/shard_map/attend_back/pallas_call | solution.py:160
  709.6 13.5 %convolution_convert_fusion.1 = bf16[2048,2048]{1,0:T(8,128)(2,1)} fusion(bf16[1024,2048]{1,0:T(8,128)(2,1)} %constant_dynamic-update-slice_fusion.3, bf16[256,2048]{1,0:T(8,128)(2,1)S(1)} %copy-done.45, bf16[256,2048]{1,0:T(8,128)(2,1)S(1)} %copy-done.41, bf16[256,2048]{1,0:T(8,128)(2,1)S(1)} %copy-done.43, bf16[256,2048]{1,0:T(8,128)(2,1)S(1)} %copy-done.47), kind=kOutput, calls=%fused_computation.3 | convolution fusion | flops 8610906112 | bytes 16777216 | tf_op jit(solution)/shard_map/ti,tj->ij/dot_general | solution.py:46
  737.3 13.4 %convolution_convert_fusion = bf16[2048,2048]{1,0:T(8,128)(2,1)} fusion(bf16[1024,2048]{1,0:T(8,128)(2,1)} %constant_dynamic-update-slice_fusion.8, bf16[256,2048]{1,0:T(8,128)(2,1)S(1)} %copy-done.76, bf16[256,2048]{1,0:T(8,128)(2,1)S(1)} %copy-done.74, bf16[256,2048]{1,0:T(8,128)(2,1)S(1)} %copy-done.72, bf16[256,2048]{1,0:T(8,128)(2,1)S(1)} %copy-done.69), kind=kOutput, calls=%fused_computation.2 | convolution fusion | flops 8610906112 | bytes 16777216 | tf_op jit(solution)/shard_map/ti,tj->ij/dot_general | solution.py:46
  750.7 9.9 convolution_convert_fusion.3
  763.9 29.7 %collective-permute-done.45 = bf16[256,2048]{1,0:T(8,128)(2,1)S(1)} collective-permute-done((bf16[256,2048]{1,0:T(8,128)(2,1)S(1)}, bf16[256,2048]{1,0:T(8,128)(2,1)S(1)}, u32[]{:S(2)}, u32[]{:S(2)}) %collective-permute-start.45) | collective-permute-done | bytes 1048608 | tf_op jit(solution)/shard_map/ppermute | solution.py:250
  793.7 39.4 %collective-permute-done.47 = bf16[256,2048]{1,0:T(8,128)(2,1)S(1)} collective-permute-done((bf16[256,2048]{1,0:T(8,128)(2,1)S(1)}, bf16[256,2048]{1,0:T(8,128)(2,1)S(1)}, u32[]{:S(2)}, u32[]{:S(2)}) %collective-permute-start.47) | collective-permute-done | bytes 1048608 | tf_op jit(solution)/shard_map/ppermute | solution.py:250
  841.7 59.7 %collective-permute-start.49 = (bf16[256,2048]{1,0:T(8,128)(2,1)}, bf16[256,2048]{1,0:T(8,128)(2,1)}, u32[]{:S(2)}, u32[]{:S(2)}) collective-permute-start(bf16[256,2048]{1,0:T(8,128)(2,1)} %add_convert_fusion.1), channel_id=1, source_target_pairs={{0,2},{2,0},{4,6},{6,4},{1,3},{3,1},{5,7},{7,5},{8,10},{10,8},{12,... | collective-permute-start | bytes 3145736 | tf_op jit(solution)/shard_map/ppermute | solution.py:250
  909.6 10.3 collective-permute-done.55
  963.7 31.5 %collective-permute-done.52 = bf16[1,64,1536]{2,1,0:T(8,128)(2,1)S(1)} collective-permute-done((bf16[1,64,1536]{2,1,0:T(8,128)(2,1)S(1)}, bf16[1,64,1536]{2,1,0:T(8,128)(2,1)S(1)}, u32[]{:S(2)}, u32[]{:S(2)}) %collective-permute-start.52) | collective-permute-done | bytes 196640 | tf_op jit(solution)/shard_map/ppermute | solution.py:186
  (505 shorter events, 414.5 us)
Async XLA Ops:
  7.2 227.0 %all-gather.5.cloned.1.call-start = ((), (), s32[]{:S(2)}) async-start(), calls=%async_computation.4 | async-start | bytes 7077888 | tf_op jit(solution)/shard_map/all_gather | solution.py:376
  34.3 229.2 %all-gather.7.cloned.1.call-start = ((), (), s32[]{:S(2)}) async-start(), calls=%async_computation.5 | async-start | bytes 2359296 | tf_op jit(solution)/shard_map/all_gather | solution.py:379
  35.1 377.0 %all-gather.9.cloned.1.call-start = ((), (), s32[]{:S(2)}) async-start(), calls=%async_computation.6 | async-start | bytes 9437184 | tf_op jit(solution)/shard_map/all_gather | solution.py:389
  73.7 363.6 %all-gather.11.cloned.1.call-start = ((), (), s32[]{:S(2)}) async-start(), calls=%async_computation.7 | async-start | bytes 9437184 | tf_op jit(solution)/shard_map/all_gather | solution.py:391
  80.8 862.6 %reduce-scatter.7.cloned.1.call-start = ((), (), s32[]{:S(2)}) async-start(), calls=%async_computation.9 | async-start | bytes 2359296 | tf_op jit(solution)/shard_map/reduce_scatter | solution.py:471
  80.8 33.7 %collective-permute-start.3 = (bf16[256,2048]{1,0:T(8,128)(2,1)S(1)}, bf16[256,2048]{1,0:T(8,128)(2,1)}, u32[]{:S(2)}, u32[]{:S(2)}) collective-permute-start(bf16[256,2048]{1,0:T(8,128)(2,1)S(1)} %fusion.14), channel_id=1, source_target_pairs={{2,4},{4,2},{3,5},{5,3},{10,12},{12,10},{11,13},{13,11},{18,20},{2... | collective-permute-start | bytes 3145736 | tf_op jit(solution)/shard_map/ppermute | solution.py:223
  104.9 38.4 %collective-permute-start.2 = (bf16[256,2048]{1,0:T(8,128)(2,1)}, bf16[256,2048]{1,0:T(8,128)(2,1)}, u32[]{:S(2)}, u32[]{:S(2)}) collective-permute-start(bf16[256,2048]{1,0:T(8,128)(2,1)} %collective-permute-done.1), channel_id=1, source_target_pairs={{2,4},{4,2},{3,5},{5,3},{10,12},{12,10},{11,13},{13,11},{18,20},{2... | collective-permute-start | bytes 3145736 | tf_op jit(solution)/shard_map/ppermute | solution.py:223
  114.6 71.5 %collective-permute-start.4 = (bf16[256,2048]{1,0:T(8,128)(2,1)}, bf16[256,2048]{1,0:T(8,128)(2,1)S(1)}, u32[]{:S(2)}, u32[]{:S(2)}) collective-permute-start(bf16[256,2048]{1,0:T(8,128)(2,1)} %collective-permute-done.3), channel_id=1, source_target_pairs={{2,0},{4,6},{3,1},{5,7},{10,8},{12,14},{11,9},{13,15},{18,16},{20,... | collective-permute-start | bytes 3145736 | tf_op jit(solution)/shard_map/ppermute | solution.py:223
  143.3 88.5 %collective-permute-start.5 = (bf16[256,2048]{1,0:T(8,128)(2,1)}, bf16[256,2048]{1,0:T(8,128)(2,1)}, u32[]{:S(2)}, u32[]{:S(2)}) collective-permute-start(bf16[256,2048]{1,0:T(8,128)(2,1)} %collective-permute-done.2), channel_id=1, source_target_pairs={{2,0},{4,6},{3,1},{5,7},{10,8},{12,14},{11,9},{13,15},{18,16},{20,... | collective-permute-start | bytes 3145736 | tf_op jit(solution)/shard_map/ppermute | solution.py:223
  267.6 47.4 %collective-permute-start.14 = (bf16[256,2048]{1,0:T(8,128)(2,1)S(1)}, bf16[256,2048]{1,0:T(8,128)(2,1)S(1)}, u32[]{:S(2)}, u32[]{:S(2)}) collective-permute-start(bf16[256,2048]{1,0:T(8,128)(2,1)S(1)} %get-tuple-element.138), channel_id=1, source_target_pairs={{0,2},{6,4},{1,3},{7,5},{8,10},{14,12},{9,11},{15,13},{16,18},{22,... | collective-permute-start | bytes 3145736 | tf_op jit(solution)/shard_map/ppermute | solution.py:250
  269.1 86.2 %collective-permute-start.16 = (bf16[256,2048]{1,0:T(8,128)(2,1)S(1)}, bf16[256,2048]{1,0:T(8,128)(2,1)S(1)}, u32[]{:S(2)}, u32[]{:S(2)}) collective-permute-start(bf16[256,2048]{1,0:T(8,128)(2,1)S(1)} %get-tuple-element.139), channel_id=1, source_target_pairs={{0,2},{6,4},{1,3},{7,5},{8,10},{14,12},{9,11},{15,13},{16,18},{22,... | collective-permute-start | bytes 3145736 | tf_op jit(solution)/shard_map/ppermute | solution.py:250
  361.3 41.8 %collective-permute-start.18 = (bf16[256,2048]{1,0:T(8,128)(2,1)}, bf16[256,2048]{1,0:T(8,128)(2,1)}, u32[]{:S(2)}, u32[]{:S(2)}) collective-permute-start(bf16[256,2048]{1,0:T(8,128)(2,1)} %add_convert_fusion.4), channel_id=1, source_target_pairs={{0,2},{2,0},{4,6},{6,4},{1,3},{3,1},{5,7},{7,5},{8,10},{10,8},{12,... | collective-permute-start | bytes 3145736 | tf_op jit(solution)/shard_map/ppermute | solution.py:250
  411.9 85.7 %collective-permute-start.31 = (f32[128,2048]{1,0:T(8,128)}, f32[128,2048]{1,0:T(8,128)S(1)}, u32[]{:S(2)}, u32[]{:S(2)}) collective-permute-start(f32[128,2048]{1,0:T(8,128)} %get-tuple-element.146), channel_id=1, source_target_pairs={{0,1},{1,0},{2,3},{3,2},{4,5},{5,4},{6,7},{7,6},{8,9},{9,8},{10,11... | collective-permute-start | bytes 3145736 | tf_op jit(solution)/shard_map/ppermute | solution.py:186
  613.7 44.6 %collective-permute-start.44 = (bf16[256,2048]{1,0:T(8,128)(2,1)S(1)}, bf16[256,2048]{1,0:T(8,128)(2,1)S(1)}, u32[]{:S(2)}, u32[]{:S(2)}) collective-permute-start(bf16[256,2048]{1,0:T(8,128)(2,1)S(1)} %collective-permute-done.41), channel_id=1, source_target_pairs={{2,0},{4,6},{3,1},{5,7},{10,8},{12,14},{11,9},{13,15},{18,16},{20,... | collective-permute-start | bytes 3145736 | tf_op jit(solution)/shard_map/ppermute | solution.py:223
  662.9 284.7 %reduce-scatter.5.cloned.1.call-start = ((), (), s32[]{:S(2)}) async-start(), calls=%async_computation.8 | async-start | bytes 7077888 | tf_op jit(solution)/shard_map/reduce_scatter | solution.py:464
  700.7 261.1 %reduce-scatter.9.cloned.1.call-start = ((), (), s32[]{:S(2)}) async-start(), calls=%async_computation.10 | async-start | bytes 9437184 | tf_op jit(solution)/shard_map/reduce_scatter | solution.py:443
  731.6 281.2 %reduce-scatter.11.cloned.1.call-start = ((), (), s32[]{:S(2)}) async-start(), calls=%async_computation.11 | async-start | bytes 9437184 | tf_op jit(solution)/shard_map/reduce_scatter | solution.py:437
  760.9 32.8 %collective-permute-start.45 = (bf16[256,2048]{1,0:T(8,128)(2,1)S(1)}, bf16[256,2048]{1,0:T(8,128)(2,1)S(1)}, u32[]{:S(2)}, u32[]{:S(2)}) collective-permute-start(bf16[256,2048]{1,0:T(8,128)(2,1)S(1)} %get-tuple-element.134), channel_id=1, source_target_pairs={{0,2},{6,4},{1,3},{7,5},{8,10},{14,12},{9,11},{15,13},{16,18},{22,... | collective-permute-start | bytes 3145736 | tf_op jit(solution)/shard_map/ppermute | solution.py:250
  762.4 70.6 %collective-permute-start.47 = (bf16[256,2048]{1,0:T(8,128)(2,1)S(1)}, bf16[256,2048]{1,0:T(8,128)(2,1)S(1)}, u32[]{:S(2)}, u32[]{:S(2)}) collective-permute-start(bf16[256,2048]{1,0:T(8,128)(2,1)S(1)} %get-tuple-element.135), channel_id=1, source_target_pairs={{0,2},{6,4},{1,3},{7,5},{8,10},{14,12},{9,11},{15,13},{16,18},{22,... | collective-permute-start | bytes 3145736 | tf_op jit(solution)/shard_map/ppermute | solution.py:250
  837.0 93.9 %collective-permute-start.46 = (bf16[256,2048]{1,0:T(8,128)(2,1)}, bf16[256,2048]{1,0:T(8,128)(2,1)}, u32[]{:S(2)}, u32[]{:S(2)}) collective-permute-start(bf16[256,2048]{1,0:T(8,128)(2,1)} %get-tuple-element.132), channel_id=1, source_target_pairs={{2,4},{4,2},{3,5},{5,3},{10,12},{12,10},{11,13},{13,11},{18,20},{2... | collective-permute-start | bytes 3145736 | tf_op jit(solution)/shard_map/ppermute | solution.py:250
  841.7 89.2 %collective-permute-start.49 = (bf16[256,2048]{1,0:T(8,128)(2,1)}, bf16[256,2048]{1,0:T(8,128)(2,1)}, u32[]{:S(2)}, u32[]{:S(2)}) collective-permute-start(bf16[256,2048]{1,0:T(8,128)(2,1)} %add_convert_fusion.1), channel_id=1, source_target_pairs={{0,2},{2,0},{4,6},{6,4},{1,3},{3,1},{5,7},{7,5},{8,10},{10,8},{12,... | collective-permute-start | bytes 3145736 | tf_op jit(solution)/shard_map/ppermute | solution.py:250
  959.9 35.3 %collective-permute-start.53 = (bf16[1,64,1536]{2,1,0:T(8,128)(2,1)S(1)}, bf16[1,64,1536]{2,1,0:T(8,128)(2,1)S(1)}, u32[]{:S(2)}, u32[]{:S(2)}) collective-permute-start(bf16[1,64,1536]{2,1,0:T(8,128)(2,1)S(1)} %get-tuple-element.163), channel_id=1, source_target_pairs={{0,6},{2,4},{4,2},{6,0},{1,7},{3,5},{5,3},{7,1},{8,14},{10,12},{12... | collective-permute-start | bytes 589832 | tf_op jit(solution)/shard_map/ppermute | solution.py:186
  961.6 33.6 %collective-permute-start.52 = (bf16[1,64,1536]{2,1,0:T(8,128)(2,1)S(1)}, bf16[1,64,1536]{2,1,0:T(8,128)(2,1)S(1)}, u32[]{:S(2)}, u32[]{:S(2)}) collective-permute-start(bf16[1,64,1536]{2,1,0:T(8,128)(2,1)S(1)} %get-tuple-element.164), channel_id=1, source_target_pairs={{0,4},{2,6},{4,0},{6,2},{1,5},{3,7},{5,1},{7,3},{8,12},{10,14},{12... | collective-permute-start | bytes 589832 | tf_op jit(solution)/shard_map/ppermute | solution.py:186
  962.8 33.0 %collective-permute-start.59 = (bf16[1,64,2048]{2,1,0:T(8,128)(2,1)S(1)}, bf16[1,64,2048]{2,1,0:T(8,128)(2,1)S(1)}, u32[]{:S(2)}, u32[]{:S(2)}) collective-permute-start(bf16[1,64,2048]{2,1,0:T(8,128)(2,1)S(1)} %constant_dynamic-slice_fusion.3), channel_id=1, source_target_pairs={{0,8},{8,0},{16,24},{24,16},{1,9},{9,1},{17,25},{25,17},{2,10},{10... | collective-permute-start | bytes 786440 | tf_op jit(solution)/shard_map/ppermute | solution.py:186
  (127 other events, 2195.9 us)
Sparse Core Ops, SparseCore 0:
  34.4 53.1 all-gather.4
  90.1 27.8 all-gather.6
  120.2 113.2 all-gather.8
  235.0 119.1 all-gather.10
  663.0 41.5 reduce-scatter.6
  708.1 61.7 reduce-scatter.4
  772.2 114.2 reduce-scatter.8
  888.8 123.9 reduce-scatter.10

commit v2 on v1

--- a/solution.py
+++ b/solution.py
@@ -186,14 +186,24 @@
     return lax.ppermute(value, axis, [(i, i ^ bit) for i in range(size)])
 
 
+def together(*values):
+    return lax.optimization_barrier(values)
+
+
+def trade(value, axis, size):
+    here = lax.axis_index(axis)
+    pick = lambda i: lax.dynamic_index_in_dim(value, i, 0, keepdims=False)
+    return [pick(here)] + [swap(pick(here ^ k), axis, size, k) for k in range(1, size)]
+
+
+def ordered(came, axis):
+    here = lax.axis_index(axis)
+    size = len(came)
+    return jnp.stack([lax.select_n(here, *(came[i ^ k] for k in range(size))) for i in range(size)])
+
+
 def exchange(value, axis, size):
-    here = lax.axis_index(axis)
-    pick = lambda i: lax.dynamic_index_in_dim(value, i, 0, keepdims=True)
-    result = value
-    for k in range(1, size):
-        came = swap(pick(here ^ k), axis, size, k)
-        result = lax.dynamic_update_slice_in_dim(result, came, here ^ k, 0)
-    return result
+    return ordered(trade(value, axis, size), axis)
 
 
 def bits(size):
@@ -203,8 +213,8 @@
         step *= 2
 
 
-def sum_all(value, sizes):
-    for axis in ("c", "z", "seq"):
+def sum_over(value, axes, sizes):
+    for axis in axes:
         for bit in bits(sizes[axis]):
             value = value + swap(value, axis, sizes[axis], bit)
     return value
@@ -216,24 +226,51 @@
 INWARD = [(0, 1), (3, 2)]
 
 
+def send(value, pairs):
+    return lax.ppermute(value, "z", pairs)
+
+
+def add(left, right):
+    return (left.astype(wide) + right.astype(wide)).astype(low)
+
+
+def spread_1(own):
+    return own, send(own, ENDS), send(own, MIDDLE)
+
+
+def spread_2(own, first, third):
+    return own, first, send(first, MIDDLE), send(third, OUTWARD), third
+
+
+def spread_3(own, first, second_in, second_out, third_in):
+    inner = (lax.axis_index("z") == 1) | (lax.axis_index("z") == 2)
+    third_out = send(second_in, OUTWARD)
+    return [
+        own,
+        first,
+        jnp.where(inner, second_in, second_out),
+        jnp.where(inner, third_in, third_out),
+    ]
+
+
+def sum_1(own, first, second, third):
+    second_came = send(second, INWARD)
+    first_came = send(add(second, send(third, INWARD)), MIDDLE)
+    second_came, first_came = together(second_came, first_came)
+    return own, add(first, first_came), add(third, second_came)
+
+
+def sum_2(own, first, third):
+    from_end, from_middle = send(first, ENDS), send(third, MIDDLE)
+    return own.astype(wide) + from_middle.astype(wide) + from_end.astype(wide)
+
+
 def gather_slots(own, axis, size):
     if size != 4:
         whole = lax.all_gather(own, axis, axis=0)
         return [whole[i] for i in range(size)]
-    send = lambda value, pairs: lax.ppermute(value, axis, pairs)
     if axis == "z":
-        inner = (lax.axis_index(axis) == 1) | (lax.axis_index(axis) == 2)
-        first = send(own, ENDS)
-        third_in = send(own, MIDDLE)
-        second_in = send(first, MIDDLE)
-        second_out = send(third_in, OUTWARD)
-        third_out = send(second_in, OUTWARD)
-        return [
-            own,
-            first,
-            jnp.where(inner, second_in, second_out),
-            jnp.where(inner, third_in, third_out),
-        ]
+        return spread_3(*spread_2(*spread_1(own)))
     half = own.shape[0] // 2
     first = swap(own, axis, 4, 1)
     second = swap(own, axis, 4, 2)
@@ -247,16 +284,9 @@
         return lax.psum_scatter(jnp.stack(parts), axis, scatter_dimension=0, tiled=False).astype(
             wide
         )
-    send = lambda value, pairs: lax.ppermute(value, axis, pairs)
-    add = lambda a, b: (a.astype(wide) + b.astype(wide)).astype(low)
+    if axis == "z":
+        return sum_2(*sum_1(*parts))
     own, first, second, third = parts
-    if axis == "z":
-        second_full = add(second, send(third, INWARD))
-        third_full = add(third, send(second, INWARD))
-        first_full = add(first, send(second_full, MIDDLE))
-        from_middle = send(third_full, MIDDLE)
-        from_end = send(first_full, ENDS)
-        return own.astype(wide) + from_middle.astype(wide) + from_end.astype(wide)
     half = own.shape[0] // 2
     top = swap(third[:half], axis, 4, 2)
     end = swap(third[half:], axis, 4, 1)
@@ -299,59 +329,89 @@
     second_shift,
 ):
     S, Z, C = sizes["seq"], sizes["z"], sizes["c"]
-    F = Z * C
-    devices = S * F
+    devices = S * Z * C
     s, z, c = (lax.axis_index(a) for a in ALL)
-    mine = (s * Z + z) * C + c
     rows = query_weight.shape[0]
     hidden_units = up_weight.shape[1]
     share = hidden_units // devices
-    slice_width = hidden_units // S
+    slice_width = hidden_units // Z
     heads = H // Z
     tokens = layer_in.shape[2]
-    whole_heads = rows * C == DH
+    whole_heads = rows * C == DH and H == S * Z
+    cross = lambda value: swap(value, "c", C, 1)
+    pick = lambda value, axis, i: lax.dynamic_index_in_dim(value, i, axis, keepdims=False)
+
+    def place(value, axis, size, i):
+        shape = list(value.shape)
+        shape.insert(axis, size)
+        start = [0] * len(shape)
+        start[axis] = i
+        return lax.dynamic_update_slice(
+            jnp.zeros(shape, value.dtype), jnp.expand_dims(value, axis), start
+        )
 
     def to_core(value):
-        keep = lax.dynamic_index_in_dim(value, c, 0, keepdims=False)[0]
-        give = lax.dynamic_index_in_dim(value, 1 - c, 0, keepdims=False)[0]
-        return jnp.concatenate([keep, swap(give, "c", C, 1)], axis=0)
+        return jnp.concatenate([pick(value, 0, c)[0], cross(pick(value, 0, 1 - c)[0])], axis=0)
 
     def from_core(value):
-        keep, give = value[:tokens], value[tokens:]
-        came = swap(give, "c", C, 1)
+        keep, came = value[:tokens], cross(value[tokens:])
         first = jnp.where(c == 0, keep, came)
         second = jnp.where(c == 0, came, keep)
         return jnp.stack([first, second])[:, None]
 
-    inputs = to_core(layer_in)
-    rounded_in = inputs.astype(low)
-    x_slots = gather_slots(rounded_in, "z", Z)
-
-    packed = jnp.concatenate(
-        [
-            v.astype(low)
-            for v in (
-                query_bias,
-                value_bias,
-                output_bias,
-                first_gain,
-                first_shift,
-                down_bias,
-                second_gain,
-                second_shift,
-                up_bias,
-            )
-        ]
-    )[None]
-    vectors = sum_all(
-        lax.dynamic_update_slice_in_dim(
-            jnp.zeros((devices, packed.shape[1]), low), packed, mine, 0
-        ),
-        sizes,
-    ).astype(wide)
+    def gather_rows(local):
+        whole = lax.all_gather(
+            local.reshape(-1, local.shape[2]), ("seq", "c"), axis=0, tiled=False
+        )
+        return whole.reshape(S, C, *local.shape).transpose(0, 2, 1, 3, 4)
+
+    def by_owner(term):
+        return term.reshape(S, Z, C, rows, -1).transpose(0, 2, 1, 3, 4).reshape(D, -1)
+
+    width = 3 * heads * DH
+    qkv_local = jnp.stack(
+        [query_weight.astype(low), key_weight.astype(low), value_weight.astype(low)], axis=1
+    )
+    qkv_local = qkv_local.reshape(rows, 3, heads, Z, DH).transpose(3, 0, 1, 2, 4)
+    own_vectors = [query_bias, value_bias, output_bias, first_gain, first_shift]
+    own_vectors += [down_bias, second_gain, second_shift, up_bias]
+    own_vectors = jnp.concatenate([v.astype(low) for v in own_vectors])
+    extra = jnp.pad(own_vectors[None], ((0, 7), (0, width - own_vectors.shape[0])))
+    qkv_local = jnp.concatenate(
+        [qkv_local.reshape(Z, rows, width), jnp.broadcast_to(extra, (Z, 8, width))], axis=1
+    )
+    rounded_in, qkv_local = together(to_core(layer_in.astype(low)), qkv_local)
+    gathered = gather_rows(exchange(qkv_local, "z", Z))
+    if Z == 4:
+        x_blocks, gathered = together(spread_2(*spread_1(rounded_in)), gathered)
+        x_slots = spread_3(*x_blocks)
+    else:
+        x_slots = gather_slots(rounded_in, "z", Z)
+    qkv_matrix = gathered[:, :, :, :rows].reshape(D, width)
+    vectors = gathered[:, :, :, rows].reshape(devices, width)[:, : own_vectors.shape[0]]
+    vectors = vectors.astype(wide)
+
+    if whole_heads:
+        output_matrix = lax.all_gather(
+            output_weight.astype(low), ("seq", "c"), axis=0, tiled=True
+        )
+    else:
+        output_matrix = lax.all_gather(output_weight.astype(low), ALL, axis=0, tiled=True)
+        output_matrix = pick(output_matrix.reshape(heads, Z, DH, D), 1, z).reshape(heads * DH, D)
+    down_matrix = lax.all_gather(down_weight.astype(low), ("seq", "c"), axis=0, tiled=True)
+
+    up_local = up_weight.astype(low).reshape(rows, S, Z, C * share).transpose(2, 0, 1, 3)
+    up_local = up_local.reshape(Z, rows, slice_width)
+    x_slots, up_local, layer_in, out_grad, qkv_matrix, vectors = together(
+        x_slots, up_local, layer_in, out_grad, qkv_matrix, vectors
+    )
+    inputs, grad_output = to_core(layer_in), to_core(out_grad)
+    up_came = trade(up_local, "z", Z)
+
     vector = lambda i: vectors[:, i * rows : (i + 1) * rows].reshape(D)
-    by_head = lambda v: lax.dynamic_index_in_dim(v.reshape(heads, Z, DH), z, 1, keepdims=False)
-    query_offset, value_offset = by_head(vector(0)), by_head(vector(1))
+    query_offset, value_offset = (
+        pick(vector(i).reshape(heads, Z, DH), 1, z).reshape(heads * DH) for i in range(2)
+    )
     (
         output_offset,
         first_scale,
@@ -360,37 +420,11 @@
         second_scale,
         second_offset,
     ) = (vector(i) for i in range(2, 8))
-    up_offset = lax.dynamic_index_in_dim(
-        vectors[:, 8 * rows :].reshape(S, slice_width), s, 0, keepdims=False
-    )
-    qkv_offset = jnp.concatenate(
-        [query_offset.reshape(-1), jnp.zeros((heads * DH,), wide), value_offset.reshape(-1)]
-    )
-
-    width = 3 * heads * DH
-    qkv_local = jnp.stack(
-        [query_weight.astype(low), key_weight.astype(low), value_weight.astype(low)], axis=1
-    )
-    qkv_local = qkv_local.reshape(rows, 3, heads, Z, DH).transpose(3, 0, 1, 2, 4)
-    qkv_local = exchange(qkv_local.reshape(Z, rows, width), "z", Z)
-    qkv_matrix = lax.all_gather(qkv_local, ("seq", "c"), axis=0, tiled=False)
-    qkv_matrix = qkv_matrix.reshape(S, C, Z, rows, width).transpose(0, 2, 1, 3, 4).reshape(D, width)
-    if whole_heads:
-        output_matrix = lax.all_gather(
-            output_weight.astype(low), ("seq", "c"), axis=0, tiled=True
-        )
-    else:
-        output_matrix = lax.all_gather(output_weight.astype(low), ALL, axis=0, tiled=True)
-        output_matrix = lax.dynamic_index_in_dim(
-            output_matrix.reshape(heads, Z, DH, D), z, 1, keepdims=False
-        ).reshape(heads * DH, D)
-    up_local = up_weight.astype(low).reshape(rows, S, slice_width).transpose(1, 0, 2)
-    up_local = exchange(up_local, "seq", S)
-    up_matrix = lax.all_gather(up_local, ("z", "c"), axis=0, tiled=False)
-    up_matrix = up_matrix.transpose(1, 0, 2, 3).reshape(D, slice_width)
-    down_matrix = lax.all_gather(down_weight.astype(low), ("z", "c"), axis=0, tiled=True)
-
-    ids = lax.dynamic_index_in_dim(doc_ids, c, 0, keepdims=False)[0].reshape(Z, C, tokens)
+    up_offset = vectors[:, 8 * rows :].reshape(S, Z, C, share)
+    up_offset = pick(up_offset, 1, z).reshape(slice_width)
+    qkv_offset = jnp.concatenate([query_offset, jnp.zeros((heads * DH,), wide), value_offset])
+
+    ids = pick(doc_ids, 0, c)[0].reshape(Z, C, tokens)
     ids = jnp.where(c == 0, ids, ids[:, ::-1])
     ids = ids[slot_order("z", Z)].reshape(-1)
     row_ids, col_ids = ids[:, None], ids[None, :]
@@ -398,6 +432,8 @@
     x_all = jnp.concatenate(x_slots, axis=0)
     qkv = (matmul(x_all, qkv_matrix) + qkv_offset).astype(low)
     mixed, totals = attend(qkv, row_ids, col_ids, heads)
+    up_came, mixed = together(up_came, mixed)
+    up_matrix = gather_rows(ordered(up_came, "z")).reshape(D, slice_width)
     branch_parts = split_slots(matmul(mixed, output_matrix).astype(low), Z)
     branch = scatter_slots(branch_parts, "z", Z) + output_offset
     hidden, first_normed, first_inverse = normalize_forward(
@@ -405,119 +441,147 @@
     )
     hidden_low = hidden.astype(low)
 
-    h_slots = gather_slots(hidden_low, "seq", S)
-    actives, slopes, downs = [], [], []
-    for h_slot in h_slots:
+    def forward(h_slot):
         active, slope = gelu_both(matmul(h_slot, up_matrix) + up_offset)
         active = active.astype(low)
-        actives.append(active)
-        slopes.append(slope)
-        downs.append(matmul(active, down_matrix).astype(low))
-    down = scatter_slots(downs, "seq", S) + down_offset
+        return active, slope, lax.optimization_barrier(matmul(active, down_matrix).astype(low))
+
+    if Z == 4:
+        h_blocks, up_matrix, down_matrix = together(
+            spread_1(hidden_low), up_matrix, down_matrix
+        )
+        h_blocks, done_0 = together(spread_2(*h_blocks), forward(hidden_low))
+        h_slots, done_1 = together(spread_3(*h_blocks), forward(h_blocks[1]))
+        done = [done_0, done_1, forward(h_slots[2]), forward(h_slots[3])]
+    else:
+        h_slots = gather_slots(hidden_low, "z", Z)
+        done = [forward(h_slot) for h_slot in h_slots]
+    actives, slopes, downs = zip(*done, strict=True)
+    down = scatter_slots(downs, "z", Z) + down_offset
     result, second_normed, second_inverse = normalize_forward(
         hidden + down, second_scale, second_offset
     )
-    layer_out = from_core(result)
-
-    grad_output = to_core(out_grad)
+
     grad_second, second_gain_part, second_shift_part = normalize_backward(
         grad_output, second_normed, second_inverse, second_scale
     )
     grad_down = grad_second.astype(low)
-    g_slots = gather_slots(grad_down, "seq", S)
+    g_slots = gather_slots(grad_down, "z", Z)
     grad_ups, hidden_parts = [], []
     for g_slot, slope in zip(g_slots, slopes, strict=True):
         grad_up = (against(g_slot, down_matrix) * slope).astype(low)
         grad_ups.append(grad_up)
-        hidden_parts.append(against(grad_up, up_matrix).astype(low))
-    grad_hidden = grad_second + scatter_slots(hidden_parts, "seq", S)
+        hidden_parts.append(lax.optimization_barrier(against(grad_up, up_matrix).astype(low)))
 
     joined = lambda values: jnp.concatenate(values, axis=0)
+    grad_up_all = joined(grad_ups)
     down_term = transposed(joined(actives), joined(g_slots)).astype(low)
-    down_weight_grad = lax.psum_scatter(
-        down_term, ("z", "c"), scatter_dimension=0, tiled=True
-    ).astype(wide)
-    grad_up_all = joined(grad_ups)
     up_term = transposed(joined(h_slots), grad_up_all).astype(low)
-    up_term = up_term.reshape(S, F, rows, slice_width).transpose(1, 0, 2, 3)
-    up_mine = lax.psum_scatter(
-        up_term.reshape(D, slice_width), ("z", "c"), scatter_dimension=0, tiled=True
-    )
-    up_mine = exchange(up_mine.reshape(S, rows, slice_width), "seq", S)
-    up_weight_grad = up_mine.transpose(1, 0, 2).reshape(rows, hidden_units).astype(wide)
+    if Z == 4:
+        hidden_parts, down_term = together(sum_1(*hidden_parts), down_term)
+        hidden_sum = sum_2(*hidden_parts)
+    else:
+        hidden_sum = scatter_slots(hidden_parts, "z", Z)
+    down_mine = lax.psum_scatter(down_term, ("seq", "c"), scatter_dimension=0, tiled=True)
+    grad_hidden = grad_second + hidden_sum
 
     grad_first, first_gain_part, first_shift_part = normalize_backward(
         grad_hidden, first_normed, first_inverse, first_scale
     )
     grad_branch = grad_first.astype(low)
-    b_all = joined(gather_slots(grad_branch, "z", Z))
+    terms = [
+        column_sum(grad_branch),
+        first_gain_part,
+        first_shift_part,
+        column_sum(grad_down),
+        second_gain_part,
+        second_shift_part,
+    ]
+    terms = jnp.concatenate([v.reshape(devices, rows) for v in terms], axis=1).astype(low)
+    below = -(-terms.size // D // 8) * 8
+    terms = jnp.pad(terms.reshape(-1), (0, below * D - terms.size)).reshape(below, D)
+    sent = jnp.concatenate([grad_branch, terms], axis=0)
+    if Z == 4:
+        b_blocks, up_term = together(spread_1(sent), by_owner(up_term))
+        b_slots = spread_3(*spread_2(*b_blocks))
+    else:
+        b_slots, up_term = gather_slots(sent, "z", Z), by_owner(up_term)
+    up_mine = lax.psum_scatter(up_term, ("seq", "c"), scatter_dimension=0, tiled=True)
+    b_all = joined([v[:-below] for v in b_slots])
+    term_sums = sum(v[-below:].astype(wide) for v in b_slots)
+    term_sums = term_sums.reshape(-1)[: 6 * D].reshape(S, Z, C, 6 * rows)
+    term_sums = pick(term_sums, 1, z)
     grad_mixed = against(b_all, output_matrix).astype(low)
     grad_query, grad_key, grad_value = attend_back(
         qkv, grad_mixed, totals, row_ids, col_ids, heads
     )
     grad_qkv = jnp.concatenate([grad_query, grad_key, grad_value], axis=1)
     in_parts = split_slots(against(grad_qkv, qkv_matrix).astype(low), Z)
-    input_grad = from_core(grad_first + scatter_slots(in_parts, "z", Z))
-
-    qkv_term = transposed(x_all, grad_qkv).astype(low)
-    qkv_term = qkv_term.reshape(S, Z, C, rows, width).transpose(0, 2, 1, 3, 4)
-    qkv_mine = lax.psum_scatter(
-        qkv_term.reshape(D, width), ("seq", "c"), scatter_dimension=0, tiled=True
-    )
-    qkv_mine = exchange(qkv_mine.reshape(Z, rows, width), "z", Z).reshape(Z, rows, 3, heads, DH)
-    qkv_grads = qkv_mine.transpose(2, 1, 3, 0, 4).reshape(3, rows, D).astype(wide)
-    output_term = transposed(mixed, b_all).astype(low)
+    in_parts, grad_qkv_late, mixed_late, down_mine, term_sums = together(
+        in_parts, grad_qkv, mixed, down_mine, term_sums
+    )
+    if Z == 4:
+        in_parts, up_mine = together(sum_1(*in_parts), up_mine)
+        in_sum = sum_2(*in_parts)
+    else:
+        in_sum = scatter_slots(in_parts, "z", Z)
+    layer_out = from_core(result)
+    input_grad = from_core(grad_first + in_sum)
+    down_weight_grad = down_mine.astype(wide)
+    up_mine = exchange(up_mine.reshape(Z, rows, slice_width), "z", Z)
+    up_mine = up_mine.reshape(Z, rows, S, C * share)
+    up_weight_grad = up_mine.transpose(1, 2, 0, 3).reshape(rows, hidden_units).astype(wide)
+
+    def in_plane(term, rest):
+        term = term.reshape(S, -1, C, rows, rest)
+        both = add(pick(term, 2, c), cross(pick(term, 2, 1 - c))).reshape(S, -1, rest)
+        parts = [both[i] for i in range(S)] if S != 4 else [pick(both, 0, s ^ k) for k in range(S)]
+        return scatter_slots(parts, "seq", S)
+
+    output_term = transposed(mixed_late, b_all).astype(low)
     if whole_heads:
-        output_weight_grad = lax.psum_scatter(
-            output_term, ("seq", "c"), scatter_dimension=0, tiled=True
-        ).astype(wide)
-    else:
-        output_term = lax.dynamic_update_slice_in_dim(
-            jnp.zeros((heads, Z, DH, D), low), output_term.reshape(heads, 1, DH, D), z, 1
-        )
+        output_weight_grad = in_plane(output_term, D)
+    else:
+        output_term = place(output_term.reshape(heads, DH, D), 1, Z, z)
         output_weight_grad = lax.psum_scatter(
             output_term.reshape(D, D), ALL, scatter_dimension=0, tiled=True
         ).astype(wide)
-
-    spread = lambda v: lax.dynamic_update_slice_in_dim(
-        jnp.zeros((heads, Z, DH), wide), v.reshape(heads, 1, DH), z, 1
-    ).reshape(devices, rows)
-    up_part = lax.dynamic_update_slice_in_dim(
-        jnp.zeros((S, slice_width), wide), column_sum(grad_up_all)[None], s, 0
-    ).reshape(devices, share)
-    terms = [
-        spread(column_sum(grad_query)),
-        spread(column_sum(grad_value)),
-        column_sum(grad_branch).reshape(devices, rows),
-        first_gain_part.reshape(devices, rows),
-        first_shift_part.reshape(devices, rows),
-        column_sum(grad_down).reshape(devices, rows),
-        second_gain_part.reshape(devices, rows),
-        second_shift_part.reshape(devices, rows),
-        up_part,
-    ]
-    sums = lax.dynamic_index_in_dim(
-        sum_all(jnp.concatenate(terms, axis=1), sizes), mine, 0, keepdims=False
-    )
+    qkv_mine = in_plane(transposed(x_all, grad_qkv_late).astype(low), width).astype(low)
+    qkv_mine = exchange(qkv_mine.reshape(Z, rows, width), "z", Z)
+    qkv_grads = qkv_mine.reshape(Z, rows, 3, heads, DH).transpose(2, 1, 3, 0, 4)
+    qkv_grads = qkv_grads.reshape(3, rows, D).astype(wide)
+
+    sums = sum_over(term_sums, ("c", "seq"), sizes)
+    sums = pick(pick(sums, 0, s), 0, c)
     vec = lambda i: sums[i * rows : (i + 1) * rows]
+    up_bias_grad = sum_over(column_sum(grad_up_all).reshape(S, C, share), ("c", "seq"), sizes)
+    up_bias_grad = pick(pick(up_bias_grad, 0, s), 0, c)
+    biases = column_sum(grad_qkv_late).reshape(3, heads * DH)
+    biases = jnp.stack([biases[0], biases[2]])
+    biases = sum_over(biases, ("c", "seq"), sizes)
+    if whole_heads:
+        biases = pick(pick(biases.reshape(2, S, C, rows), 1, s), 1, c)
+    else:
+        biases = lax.all_gather(biases.reshape(2, heads, DH), "z", axis=2, tiled=False)
+        biases = pick(biases.reshape(2, devices, rows), 1, (s * Z + z) * C + c)
     return (
         layer_out,
         input_grad,
         qkv_grads[0],
-        vec(0),
+        biases[0],
         qkv_grads[1],
         qkv_grads[2],
+        biases[1],
+        output_weight_grad,
+        vec(0),
         vec(1),
-        output_weight_grad,
         vec(2),
+        up_weight_grad,
+        up_bias_grad,
+        down_weight_grad,
         vec(3),
         vec(4),
-        up_weight_grad,
-        sums[8 * rows :],
-        down_weight_grad,
         vec(5),
-        vec(6),
-        vec(7),
     )
 
 

time: 1040 us -> 873 us (0.84)
  waiting for transfers between devices: 534 us -> 385 us
  other arithmetic: 54.1 us -> 99.1 us
  starting transfers between devices: 154 us -> 126 us
  local copies, waits for them, and re-layouts: 93.6 us -> 74.2 us
  matrix products: 147 us -> 135 us
    ppermute x42 -> x36, waiting for transfers between devices: 190 us -> 41.5 us  [swap(): return lax.ppermute(value, axis, [(i, i ^ bit) for i in range(size)])]
    ppermute x20 -> x40, starting transfers between devices: 110 us -> 87.5 us  [send(): return lax.ppermute(value, 'z', pairs)]
    convert_element_type x22 -> x32, other arithmetic: 15.2 us -> 36.1 us  [the longest x15 25.2 us: add(): return (left.astype(wide) + right.astype(wide)).astype(low)]
    unnamed x173 -> x163, local copies, waits for them, and re-layouts: 23.1 us -> 7.12 us
    dynamic_update_slice x15 -> x0, local copies, waits for them, and re-layouts: 15.3 us -> none  [the longest x11 14.8 us: exchange(): result = lax.dynamic_update_slice_in_dim(result, came, here ^ k, 0)]
    all_gather x3, waiting for transfers between devices: 0.02 us -> 13.6 us  [the longest x1 13.5 us: shards(): lax.all_gather(down_weight.astype(low), ('seq', 'c'), axis=0, tiled=True)]
    ppermute x20 -> x40, waiting for transfers between devices: 335 us -> 329 us  [send(): return lax.ppermute(value, 'z', pairs)]
    ppermute x42 -> x36, starting transfers between devices: 43.5 us -> 38.7 us  [swap(): return lax.ppermute(value, axis, [(i, i ^ bit) for i in range(size)])]
  transfers between devices with their start and end apart: 70 -> 82, of which waited for: 38 -> 34; matrix products, arithmetic and copies ran while one was open for 25% -> 29% of each run, Pallas kernels for 3% -> 3%
where the time goes in v2:
time: 873 us; the launch traced here: 866 us
  waiting for transfers between devices  385 us (44%)
  matrix products  135 us (15%)
  starting transfers between devices  126 us (14%)
  other arithmetic  99.1 us (11%)
  local copies, waits for them, and re-layouts  74.2 us (8%)
  Pallas kernels  30.3 us (3%)
  between operations  16.4 us (2%)
    ppermute x40, waiting for transfers between devices, send(): return lax.ppermute(value, 'z', pairs)  329 us
    ppermute x40, starting transfers between devices, send(): return lax.ppermute(value, 'z', pairs)  87.5 us
    dot_general x10, matrix products, against(): return jnp.einsum('ti,ji->tj', left, right, preferred_element_type=wide)  50.1 us
    dot_general x10, matrix products, matmul(): return jnp.dot(left, right, preferred_element_type=wide)  48 us
    ppermute x36, waiting for transfers between devices, swap(): return lax.ppermute(value, axis, [(i, i ^ bit) for i in range(size)])  41.5 us
    ppermute x36, starting transfers between devices, swap(): return lax.ppermute(value, axis, [(i, i ^ bit) for i in range(size)])  38.7 us
    dot_general x4, matrix products, transposed(): return jnp.einsum('ti,tj->ij', left, right, preferred_element_type=wide)  36.7 us
    convert_element_type x15, other arithmetic, add(): return (left.astype(wide) + right.astype(wide)).astype(low)  25.2 us
  transfers between devices with their start and end apart: 82, of which 34 were waited for; matrix products, arithmetic and copies ran while one was open for 29% of the time, Pallas kernels for 3%

profile of v2, /device:TPU:0, one launch (start us, length us, event | category | flops | bytes accessed | tf_op | source)
XLA Modules:
  0.0 865.8 jit_solution(17431845131668797617)
XLA Ops:
  44.8 20.8 %collective-permute-done.1 = bf16[256,2048]{1,0:T(8,128)(2,1)} collective-permute-done((bf16[256,2048]{1,0:T(8,128)(2,1)S(1)}, bf16[256,2048]{1,0:T(8,128)(2,1)}, u32[]{:S(2)}, u32[]{:S(2)}) %collective-permute-start.1) | collective-permute-done | bytes 1048608 | tf_op jit(solution)/shard_map/ppermute | solution.py:230
  77.2 16.3 %collective-permute-done.4 = bf16[256,2048]{1,0:T(8,128)(2,1)} collective-permute-done((bf16[256,2048]{1,0:T(8,128)(2,1)}, bf16[256,2048]{1,0:T(8,128)(2,1)}, u32[]{:S(2)}, u32[]{:S(2)}) %collective-permute-start.4) | collective-permute-done | bytes 1048608 | tf_op jit(solution)/shard_map/ppermute | solution.py:230
  106.6 11.6 %collective-permute-done.8 = bf16[256,2048]{1,0:T(8,128)(2,1)} collective-permute-done((bf16[256,2048]{1,0:T(8,128)(2,1)}, bf16[256,2048]{1,0:T(8,128)(2,1)}, u32[]{:S(2)}, u32[]{:S(2)}) %collective-permute-start.8) | collective-permute-done | bytes 1048608 | tf_op jit(solution)/shard_map/ppermute | solution.py:230
  137.4 11.7 %attend.1 = (bf16[1024,512]{1,0:T(8,128)(2,1)S(1)}, f32[4,1024,1]{2,1,0:T(8,128)S(1)}) custom-call(bf16[1024,1536]{1,0:T(8,128)(2,1)S(1)} %add_convert_fusion.q_ref.k_ref.v_ref, bf16[1024,1536]{1,0:T(8,128)(2,1)S(1)} %add_convert_fusion.q_ref.k_ref.v_ref, bf16[1024,1536]{1,0:T(8,128)(2,1)S(1)} %add_convert_fusion.q_ref.k_ref.v_ref, ...), custom_call_target="tpu_custom_call" | custom-call | flops 2147483648 | bytes 4194304 | tf_op jit(solution)/shard_map/attend/pallas_call | solution.py:126
  161.7 22.2 %collective-permute-done.14 = bf16[256,2048]{1,0:T(8,128)(2,1)S(1)} collective-permute-done((bf16[256,2048]{1,0:T(8,128)(2,1)S(1)}, bf16[256,2048]{1,0:T(8,128)(2,1)S(1)}, u32[]{:S(2)}, u32[]{:S(2)}) %collective-permute-start.14) | collective-permute-done | bytes 1048608 | tf_op jit(solution)/shard_map/ppermute | solution.py:230
  186.2 16.6 %collective-permute-done.13 = bf16[256,2048]{1,0:T(8,128)(2,1)S(1)} collective-permute-done((bf16[256,2048]{1,0:T(8,128)(2,1)S(1)}, bf16[256,2048]{1,0:T(8,128)(2,1)S(1)}, u32[]{:S(2)}, u32[]{:S(2)}) %collective-permute-start.13) | collective-permute-done | bytes 1048608 | tf_op jit(solution)/shard_map/ppermute | solution.py:230
  212.9 18.4 %collective-permute-done.17 = bf16[256,2048]{1,0:T(8,128)(2,1)} collective-permute-done((bf16[256,2048]{1,0:T(8,128)(2,1)}, bf16[256,2048]{1,0:T(8,128)(2,1)}, u32[]{:S(2)}, u32[]{:S(2)}) %collective-permute-start.17) | collective-permute-done | bytes 1048608 | tf_op jit(solution)/shard_map/ppermute | solution.py:230
  248.0 13.5 %all-gather.11.cloned.1.call-done = bf16[2048,2048]{1,0:T(8,128)(2,1)} async-done(((bf16[256,2048]{1,0:T(8,128)(2,1)}), bf16[2048,2048]{1,0:T(8,128)(2,1)}) %all-gather.11.cloned.1.call-update) | async-done | bytes 8388624 | tf_op jit(solution)/shard_map/all_gather | solution.py:401
  275.7 15.5 %collective-permute-done.21 = bf16[256,2048]{1,0:T(8,128)(2,1)S(1)} collective-permute-done((bf16[256,2048]{1,0:T(8,128)(2,1)}, bf16[256,2048]{1,0:T(8,128)(2,1)S(1)}, u32[]{:S(2)}, u32[]{:S(2)}) %collective-permute-start.21) | collective-permute-done | bytes 1048608 | tf_op jit(solution)/shard_map/ppermute | solution.py:230
  301.4 22.4 %collective-permute-done.22 = bf16[256,2048]{1,0:T(8,128)(2,1)S(1)} collective-permute-done((bf16[256,2048]{1,0:T(8,128)(2,1)S(1)}, bf16[256,2048]{1,0:T(8,128)(2,1)S(1)}, u32[]{:S(2)}, u32[]{:S(2)}) %collective-permute-start.22) | collective-permute-done | bytes 1048608 | tf_op jit(solution)/shard_map/ppermute | solution.py:230
  342.4 15.6 %collective-permute-done.24 = bf16[256,2048]{1,0:T(8,128)(2,1)S(1)} collective-permute-done((bf16[256,2048]{1,0:T(8,128)(2,1)S(1)}, bf16[256,2048]{1,0:T(8,128)(2,1)S(1)}, u32[]{:S(2)}, u32[]{:S(2)}) %collective-permute-start.24) | collective-permute-done | bytes 1048608 | tf_op jit(solution)/shard_map/ppermute | solution.py:230
  359.1 18.8 %collective-permute-done.23 = bf16[256,2048]{1,0:T(8,128)(2,1)S(1)} collective-permute-done((bf16[256,2048]{1,0:T(8,128)(2,1)S(1)}, bf16[256,2048]{1,0:T(8,128)(2,1)S(1)}, u32[]{:S(2)}, u32[]{:S(2)}) %collective-permute-start.23) | collective-permute-done | bytes 1048608 | tf_op jit(solution)/shard_map/ppermute | solution.py:230
  392.2 15.1 %collective-permute-done.27 = bf16[256,2048]{1,0:T(8,128)(2,1)} collective-permute-done((bf16[256,2048]{1,0:T(8,128)(2,1)}, bf16[256,2048]{1,0:T(8,128)(2,1)}, u32[]{:S(2)}, u32[]{:S(2)}) %collective-permute-start.27) | collective-permute-done | bytes 1048608 | tf_op jit(solution)/shard_map/ppermute | solution.py:230
  425.1 12.7 %collective-permute-done.30 = bf16[256,2048]{1,0:T(8,128)(2,1)S(1)} collective-permute-done((bf16[256,2048]{1,0:T(8,128)(2,1)S(1)}, bf16[256,2048]{1,0:T(8,128)(2,1)S(1)}, u32[]{:S(2)}, u32[]{:S(2)}) %collective-permute-start.30) | collective-permute-done | bytes 1048608 | tf_op jit(solution)/shard_map/ppermute | solution.py:230
  464.6 20.9 %collective-permute-done.35 = bf16[256,2048]{1,0:T(8,128)(2,1)S(1)} collective-permute-done((bf16[256,2048]{1,0:T(8,128)(2,1)S(1)}, bf16[256,2048]{1,0:T(8,128)(2,1)S(1)}, u32[]{:S(2)}, u32[]{:S(2)}) %collective-permute-start.35) | collective-permute-done | bytes 1048608 | tf_op jit(solution)/shard_map/ppermute | solution.py:230
  510.1 10.7 %collective-permute-done.36 = bf16[256,2048]{1,0:T(8,128)(2,1)S(1)} collective-permute-done((bf16[256,2048]{1,0:T(8,128)(2,1)S(1)}, bf16[256,2048]{1,0:T(8,128)(2,1)S(1)}, u32[]{:S(2)}, u32[]{:S(2)}) %collective-permute-start.36) | collective-permute-done | bytes 1048608 | tf_op jit(solution)/shard_map/ppermute | solution.py:230
  525.0 11.4 %convolution_convert_fusion.2 = bf16[2048,2048]{1,0:T(8,128)(2,1)} fusion(bf16[256,2048]{1,0:T(8,128)(2,1)S(1)} %copy-done.71, bf16[256,2048]{1,0:T(8,128)(2,1)S(1)} %copy-done.73, bf16[256,2048]{1,0:T(8,128)(2,1)S(1)} %copy-done.69, bf16[256,2048]{1,0:T(8,128)(2,1)S(1)} %copy-done.67, bf16[256,2048]{1,0:T(8,128)(2,1)S(1)} %broadcast_select_fusion.2, ...), kind=kOutput, calls=%fused_computation.4 | convolution fusion | flops 8627683328 | bytes 16777216 | tf_op jit(solution)/shard_map/ti,tj->ij/dot_general | solution.py:46
  553.5 14.5 %collective-permute-done.39 = bf16[256,2048]{1,0:T(8,128)(2,1)} collective-permute-done((bf16[256,2048]{1,0:T(8,128)(2,1)}, bf16[256,2048]{1,0:T(8,128)(2,1)}, u32[]{:S(2)}, u32[]{:S(2)}) %collective-permute-start.39) | collective-permute-done | bytes 1048608 | tf_op jit(solution)/shard_map/ppermute | solution.py:230
  579.9 13.7 %convolution_convert_fusion.1 = bf16[2048,2048]{1,0:T(8,128)(2,1)} fusion(bf16[256,2048]{1,0:T(8,128)(2,1)S(1)} %copy-done.33, bf16[256,2048]{1,0:T(8,128)(2,1)S(1)} %copy-done.31, bf16[256,2048]{1,0:T(8,128)(2,1)} %collective-permute-done.18, bf16[256,2048]{1,0:T(8,128)(2,1)} %fusion.27, bf16[256,2048]{1,0:T(8,128)(2,1)} %copy-done.42, ...), kind=kOutput, calls=%fused_computation.3 | convolution fusion | flops 8627683328 | bytes 16777216 | tf_op jit(solution)/shard_map/ti,tj->ij/dot_general | solution.py:46
  622.4 13.0 %collective-permute-done.43 = bf16[264,2048]{1,0:T(8,128)(2,1)} collective-permute-done((bf16[264,2048]{1,0:T(8,128)(2,1)}, bf16[264,2048]{1,0:T(8,128)(2,1)}, u32[]{:S(2)}, u32[]{:S(2)}) %collective-permute-start.43) | collective-permute-done | bytes 1081376 | tf_op jit(solution)/shard_map/ppermute | solution.py:230
  638.0 20.4 %collective-permute-done.44 = bf16[264,2048]{1,0:T(8,128)(2,1)} collective-permute-done((bf16[264,2048]{1,0:T(8,128)(2,1)}, bf16[264,2048]{1,0:T(8,128)(2,1)}, u32[]{:S(2)}, u32[]{:S(2)}) %collective-permute-start.44) | collective-permute-done | bytes 1081376 | tf_op jit(solution)/shard_map/ppermute | solution.py:230
  665.6 18.5 %attend_back.1 = (bf16[1024,512]{1,0:T(8,128)(2,1)S(1)}, bf16[1024,512]{1,0:T(8,128)(2,1)S(1)}, bf16[1024,512]{1,0:T(8,128)(2,1)S(1)}) custom-call(bf16[1024,1536]{1,0:T(8,128)(2,1)} %copy-done.2, bf16[1024,1536]{1,0:T(8,128)(2,1)} %copy-done.2, bf16[1024,1536]{1,0:T(8,128)(2,1)} %copy-done.2, bf16[1024,512]{1,0:T(8,128)(2,1)S(1)} %convolution_convert_fusion.14.g_ref, ...), custom_call_target="tpu_custom_call" | custom-call | flops 5368709120 | bytes 8388608 | tf_op jit(solution)/shard_map/attend_back/pallas_call | solution.py:160
  764.8 10.9 %collective-permute-start.49 = (bf16[256,2048]{1,0:T(8,128)(2,1)}, bf16[256,2048]{1,0:T(8,128)(2,1)S(1)}, u32[]{:S(2)}, u32[]{:S(2)}) collective-permute-start(bf16[256,2048]{1,0:T(8,128)(2,1)} %add_convert_fusion.2), channel_id=1, source_target_pairs={{0,2},{2,0},{4,6},{6,4},{1,3},{3,1},{5,7},{7,5},{8,10},{10,8},{12,... | collective-permute-start | bytes 3145736 | tf_op jit(solution)/shard_map/ppermute | solution.py:230
  786.3 15.7 %collective-permute-done.49 = bf16[256,2048]{1,0:T(8,128)(2,1)S(1)} collective-permute-done((bf16[256,2048]{1,0:T(8,128)(2,1)}, bf16[256,2048]{1,0:T(8,128)(2,1)S(1)}, u32[]{:S(2)}, u32[]{:S(2)}) %collective-permute-start.49) | collective-permute-done | bytes 1048608 | tf_op jit(solution)/shard_map/ppermute | solution.py:230
  (535 shorter events, 468.3 us)
Async XLA Ops:
  7.2 86.3 %all-gather.5.cloned.1.call-start = ((), (), s32[]{:S(2)}) async-start(), calls=%async_computation.2 | async-start | bytes 7962624 | tf_op jit(solution)/shard_map/all_gather | solution.py:363
  39.4 114.3 %all-gather.7.cloned.1.call-start = ((), (), s32[]{:S(2)}) async-start(), calls=%async_computation.3 | async-start | bytes 2359296 | tf_op jit(solution)/shard_map/all_gather | solution.py:395
  69.3 170.4 %all-gather.9.cloned.1.call-start = ((), (), s32[]{:S(2)}) async-start(), calls=%async_computation.4 | async-start | bytes 9437184 | tf_op jit(solution)/shard_map/all_gather | solution.py:363
  120.9 28.2 %collective-permute-start.10 = (bf16[64,2048]{1,0:T(8,128)(2,1)S(1)}, bf16[64,2048]{1,0:T(8,128)(2,1)S(1)}, u32[]{:S(2)}, u32[]{:S(2)}) collective-permute-start(bf16[64,2048]{1,0:T(8,128)(2,1)S(1)} %get-tuple-element.311), channel_id=1, source_target_pairs={{0,2},{2,0},{4,6},{6,4},{1,3},{3,1},{5,7},{7,5},{8,10},{10,8},{12,... | collective-permute-start | bytes 786440 | tf_op jit(solution)/shard_map/ppermute | solution.py:186
  121.0 28.1 %collective-permute-start.11 = (bf16[64,2048]{1,0:T(8,128)(2,1)S(1)}, bf16[64,2048]{1,0:T(8,128)(2,1)S(1)}, u32[]{:S(2)}, u32[]{:S(2)}) collective-permute-start(bf16[64,2048]{1,0:T(8,128)(2,1)S(1)} %get-tuple-element.310), channel_id=1, source_target_pairs={{0,4},{2,6},{4,0},{6,2},{1,5},{3,7},{5,1},{7,3},{8,12},{10,14},{12... | collective-permute-start | bytes 786440 | tf_op jit(solution)/shard_map/ppermute | solution.py:186
  150.8 110.7 %all-gather.11.cloned.1.call-start = ((), (), s32[]{:S(2)}) async-start(), calls=%async_computation.5 | async-start | bytes 9437184 | tf_op jit(solution)/shard_map/all_gather | solution.py:401
  153.6 542.4 %reduce-scatter.3.cloned.1.call-start = ((), (), s32[]{:S(2)}) async-start(), calls=%async_computation.6 | async-start | bytes 9437184 | tf_op jit(solution)/shard_map/reduce_scatter | solution.py:485
  160.4 42.5 %collective-permute-start.13 = (bf16[256,2048]{1,0:T(8,128)(2,1)S(1)}, bf16[256,2048]{1,0:T(8,128)(2,1)S(1)}, u32[]{:S(2)}, u32[]{:S(2)}) collective-permute-start(bf16[256,2048]{1,0:T(8,128)(2,1)S(1)} %get-tuple-element.260), channel_id=1, source_target_pairs={{0,2},{6,4},{1,3},{7,5},{8,10},{14,12},{9,11},{15,13},{16,18},{22,... | collective-permute-start | bytes 3145736 | tf_op jit(solution)/shard_map/ppermute | solution.py:230
  186.2 26.6 %collective-permute-start.9 = (f32[128,2048]{1,0:T(8,128)S(1)}, f32[128,2048]{1,0:T(8,128)S(1)}, u32[]{:S(2)}, u32[]{:S(2)}) collective-permute-start(f32[128,2048]{1,0:T(8,128)S(1)} %get-tuple-element.280), channel_id=1, source_target_pairs={{0,1},{1,0},{2,3},{3,2},{4,5},{5,4},{6,7},{7,6},{8,9},{9,8},{10,11... | collective-permute-start | bytes 3145736 | tf_op jit(solution)/shard_map/ppermute | solution.py:186
  262.3 28.9 %collective-permute-start.21 = (bf16[256,2048]{1,0:T(8,128)(2,1)}, bf16[256,2048]{1,0:T(8,128)(2,1)S(1)}, u32[]{:S(2)}, u32[]{:S(2)}) collective-permute-start(bf16[256,2048]{1,0:T(8,128)(2,1)} %collective-permute-done.19), channel_id=1, source_target_pairs={{2,0},{4,6},{3,1},{5,7},{10,8},{12,14},{11,9},{13,15},{18,16},{20,... | collective-permute-start | bytes 3145736 | tf_op jit(solution)/shard_map/ppermute | solution.py:230
  297.3 26.4 %collective-permute-start.22 = (bf16[256,2048]{1,0:T(8,128)(2,1)S(1)}, bf16[256,2048]{1,0:T(8,128)(2,1)S(1)}, u32[]{:S(2)}, u32[]{:S(2)}) collective-permute-start(bf16[256,2048]{1,0:T(8,128)(2,1)S(1)} %collective-permute-done.20), channel_id=1, source_target_pairs={{2,0},{4,6},{3,1},{5,7},{10,8},{12,14},{11,9},{13,15},{18,16},{20,... | collective-permute-start | bytes 3145736 | tf_op jit(solution)/shard_map/ppermute | solution.py:230
  341.0 36.9 %collective-permute-start.23 = (bf16[256,2048]{1,0:T(8,128)(2,1)S(1)}, bf16[256,2048]{1,0:T(8,128)(2,1)S(1)}, u32[]{:S(2)}, u32[]{:S(2)}) collective-permute-start(bf16[256,2048]{1,0:T(8,128)(2,1)S(1)} %convolution_convert_fusion.10), channel_id=1, source_target_pairs={{0,2},{6,4},{1,3},{7,5},{8,10},{14,12},{9,11},{15,13},{16,18},{22,... | collective-permute-start | bytes 3145736 | tf_op jit(solution)/shard_map/ppermute | solution.py:230
  449.1 36.4 %collective-permute-start.35 = (bf16[256,2048]{1,0:T(8,128)(2,1)S(1)}, bf16[256,2048]{1,0:T(8,128)(2,1)S(1)}, u32[]{:S(2)}, u32[]{:S(2)}) collective-permute-start(bf16[256,2048]{1,0:T(8,128)(2,1)S(1)} %collective-permute-done.31), channel_id=1, source_target_pairs={{2,0},{4,6},{3,1},{5,7},{10,8},{12,14},{11,9},{13,15},{18,16},{20,... | collective-permute-start | bytes 3145736 | tf_op jit(solution)/shard_map/ppermute | solution.py:230
  507.5 31.0 %collective-permute-start.34 = (bf16[256,2048]{1,0:T(8,128)(2,1)}, bf16[256,2048]{1,0:T(8,128)(2,1)}, u32[]{:S(2)}, u32[]{:S(2)}) collective-permute-start(bf16[256,2048]{1,0:T(8,128)(2,1)} %convolution_convert_fusion.7), channel_id=1, source_target_pairs={{0,2},{6,4},{1,3},{7,5},{8,10},{14,12},{9,11},{15,13},{16,18},{22,... | collective-permute-start | bytes 3145736 | tf_op jit(solution)/shard_map/ppermute | solution.py:230
  543.9 220.2 %reduce-scatter.5.cloned.1.call-start = ((), (), s32[]{:S(2)}) async-start(), calls=%async_computation.7 | async-start | bytes 9437184 | tf_op jit(solution)/shard_map/reduce_scatter | solution.py:509
  606.1 29.3 %collective-permute-start.43 = (bf16[264,2048]{1,0:T(8,128)(2,1)}, bf16[264,2048]{1,0:T(8,128)(2,1)}, u32[]{:S(2)}, u32[]{:S(2)}) collective-permute-start(bf16[264,2048]{1,0:T(8,128)(2,1)} %collective-permute-done.41), channel_id=1, source_target_pairs={{2,0},{4,6},{3,1},{5,7},{10,8},{12,14},{11,9},{13,15},{18,16},{20,... | collective-permute-start | bytes 3244040 | tf_op jit(solution)/shard_map/ppermute | solution.py:230
  614.9 43.5 %collective-permute-start.44 = (bf16[264,2048]{1,0:T(8,128)(2,1)}, bf16[264,2048]{1,0:T(8,128)(2,1)}, u32[]{:S(2)}, u32[]{:S(2)}) collective-permute-start(bf16[264,2048]{1,0:T(8,128)(2,1)} %collective-permute-done.42), channel_id=1, source_target_pairs={{2,0},{4,6},{3,1},{5,7},{10,8},{12,14},{11,9},{13,15},{18,16},{20,... | collective-permute-start | bytes 3244040 | tf_op jit(solution)/shard_map/ppermute | solution.py:230
  716.4 43.7 %collective-permute-start.45 = (bf16[256,2048]{1,0:T(8,128)(2,1)S(1)}, bf16[256,2048]{1,0:T(8,128)(2,1)}, u32[]{:S(2)}, u32[]{:S(2)}) collective-permute-start(bf16[256,2048]{1,0:T(8,128)(2,1)S(1)} %copy-done.22), channel_id=1, source_target_pairs={{0,2},{6,4},{1,3},{7,5},{8,10},{14,12},{9,11},{15,13},{16,18},{22,... | collective-permute-start | bytes 3145736 | tf_op jit(solution)/shard_map/ppermute | solution.py:230
  723.4 55.8 %collective-permute-start.51 = (bf16[4,4,64,1536]{3,2,1,0:T(8,128)(2,1)}, bf16[4,4,64,1536]{3,2,1,0:T(8,128)(2,1)}, u32[]{:S(2)}, u32[]{:S(2)}) collective-permute-start(bf16[4,4,64,1536]{3,2,1,0:T(8,128)(2,1)} %dynamic-slice_bitcast_fusion), channel_id=1, source_target_pairs={{0,1},{1,0},{2,3},{3,2},{4,5},{5,4},{6,7},{7,6},{8,9},{9,8},{10,11... | collective-permute-start | bytes 9437192 | tf_op jit(solution)/shard_map/ppermute | solution.py:186
  764.8 37.2 %collective-permute-start.49 = (bf16[256,2048]{1,0:T(8,128)(2,1)}, bf16[256,2048]{1,0:T(8,128)(2,1)S(1)}, u32[]{:S(2)}, u32[]{:S(2)}) collective-permute-start(bf16[256,2048]{1,0:T(8,128)(2,1)} %add_convert_fusion.2), channel_id=1, source_target_pairs={{0,2},{2,0},{4,6},{6,4},{1,3},{3,1},{5,7},{7,5},{8,10},{10,8},{12,... | collective-permute-start | bytes 3145736 | tf_op jit(solution)/shard_map/ppermute | solution.py:230
  776.9 37.1 %collective-permute-start.70 = (bf16[64,2048]{1,0:T(8,128)(2,1)S(1)}, bf16[64,2048]{1,0:T(8,128)(2,1)S(1)}, u32[]{:S(2)}, u32[]{:S(2)}) collective-permute-start(bf16[64,2048]{1,0:T(8,128)(2,1)S(1)} %get-tuple-element.298), channel_id=1, source_target_pairs={{0,2},{2,0},{4,6},{6,4},{1,3},{3,1},{5,7},{7,5},{8,10},{10,8},{12,... | collective-permute-start | bytes 786440 | tf_op jit(solution)/shard_map/ppermute | solution.py:186
  776.9 39.5 %collective-permute-start.71 = (bf16[64,2048]{1,0:T(8,128)(2,1)S(1)}, bf16[64,2048]{1,0:T(8,128)(2,1)S(1)}, u32[]{:S(2)}, u32[]{:S(2)}) collective-permute-start(bf16[64,2048]{1,0:T(8,128)(2,1)S(1)} %get-tuple-element.296), channel_id=1, source_target_pairs={{0,4},{2,6},{4,0},{6,2},{1,5},{3,7},{5,1},{7,3},{8,12},{10,14},{12... | collective-permute-start | bytes 786440 | tf_op jit(solution)/shard_map/ppermute | solution.py:186
  779.2 37.2 %collective-permute-start.72 = (bf16[64,2048]{1,0:T(8,128)(2,1)S(1)}, bf16[64,2048]{1,0:T(8,128)(2,1)S(1)}, u32[]{:S(2)}, u32[]{:S(2)}) collective-permute-start(bf16[64,2048]{1,0:T(8,128)(2,1)S(1)} %get-tuple-element.297), channel_id=1, source_target_pairs={{0,6},{2,4},{4,2},{6,0},{1,7},{3,5},{5,3},{7,1},{8,14},{10,12},{12... | collective-permute-start | bytes 786440 | tf_op jit(solution)/shard_map/ppermute | solution.py:186
  805.3 27.8 %collective-permute-start.50 = (f32[128,2048]{1,0:T(8,128)}, f32[128,2048]{1,0:T(8,128)}, u32[]{:S(2)}, u32[]{:S(2)}) collective-permute-start(f32[128,2048]{1,0:T(8,128)} %slice.328), channel_id=1, source_target_pairs={{0,1},{1,0},{2,3},{3,2},{4,5},{5,4},{6,7},{7,6},{8,9},{9,8},{10,11... | collective-permute-start | bytes 3145736 | tf_op jit(solution)/shard_map/ppermute | solution.py:186
  (137 other events, 1781.9 us)
Sparse Core Ops, SparseCore 0:
  39.5 51.1 all-gather.4
  93.1 27.8 all-gather.6
  151.0 54.3 all-gather.8
  207.1 54.3 all-gather.10
  544.0 73.0 reduce-scatter.2
  622.5 80.0 reduce-scatter.4

commit v3 on v2

--- a/solution.py
+++ b/solution.py
@@ -180,6 +180,60 @@
         compiler_params=pltpu.CompilerParams(vmem_limit_bytes=48 * 2**20),
         name="attend_back",
     )(qkv, qkv, qkv, grad_mixed, totals, row_ids, col_ids)
+
+
+def branch_kernel(*refs):
+    *mixed_refs, w_ref, x_ref, own_ref, vector_ref = refs[:-4]
+    low_ref, hidden_ref, normed_ref, inverse_ref = refs[-4:]
+    branch = vector_ref[0:1, :]
+    for k, mixed_ref in enumerate(mixed_refs):
+        branch = branch + jnp.dot(mixed_ref[...], w_ref[k], preferred_element_type=wide)
+    here = pl.program_id(0) == 0
+    tokens = jnp.where(here, own_ref[...], x_ref[...].astype(wide))
+    hidden, normed, inverse = normalize_forward(
+        tokens + branch, vector_ref[1:2, :], vector_ref[2:3, :]
+    )
+    low_ref[...] = hidden.astype(low)
+
+    @pl.when(here)
+    def _():
+        hidden_ref[...] = hidden
+        normed_ref[...] = normed
+        inverse_ref[...] = inverse
+
+
+def branch_norm(mixed_slots, weights, x_all, own, vectors):
+    size = len(mixed_slots)
+    block, width = own.shape
+    fed = mixed_slots[0].shape[1]
+    row = pl.BlockSpec((block, width), lambda i: (i, 0))
+    kept = pl.BlockSpec((block, width), lambda i: (0, 0))
+    specs = [pl.BlockSpec((block, fed), lambda i, k=k: (i ^ k, 0)) for k in range(size)]
+    return pl.pallas_call(
+        branch_kernel,
+        grid=(size,),
+        in_specs=[
+            *specs,
+            pl.BlockSpec((size, fed, width), lambda i: (0, 0, 0)),
+            row,
+            kept,
+            pl.BlockSpec(vectors.shape, lambda i: (0, 0)),
+        ],
+        out_specs=[row, kept, kept, pl.BlockSpec((block, 1), lambda i: (0, 0))],
+        out_shape=[
+            jax.ShapeDtypeStruct((size * block, width), low),
+            jax.ShapeDtypeStruct((block, width), wide),
+            jax.ShapeDtypeStruct((block, width), wide),
+            jax.ShapeDtypeStruct((block, 1), wide),
+        ],
+        cost_estimate=pl.CostEstimate(
+            flops=2 * size * block * size * fed * width,
+            bytes_accessed=2 * size * fed * width + 16 * size * block * width,
+            transcendentals=size * block,
+        ),
+        compiler_params=pltpu.CompilerParams(vmem_limit_bytes=52 * 2**20),
+        name="branch_norm",
+    )(*mixed_slots, weights, x_all, own, vectors)
 
 
 def swap(value, axis, size, bit):
@@ -391,14 +445,11 @@
     vectors = gathered[:, :, :, rows].reshape(devices, width)[:, : own_vectors.shape[0]]
     vectors = vectors.astype(wide)
 
-    if whole_heads:
-        output_matrix = lax.all_gather(
-            output_weight.astype(low), ("seq", "c"), axis=0, tiled=True
-        )
-    else:
-        output_matrix = lax.all_gather(output_weight.astype(low), ALL, axis=0, tiled=True)
-        output_matrix = pick(output_matrix.reshape(heads, Z, DH, D), 1, z).reshape(heads * DH, D)
-    down_matrix = lax.all_gather(down_weight.astype(low), ("seq", "c"), axis=0, tiled=True)
+    square = Z == 4 and S == 4 and whole_heads
+    output_whole = lax.all_gather(output_weight.astype(low), ALL, axis=0, tiled=True)
+    output_whole = output_whole.reshape(heads, Z, DH, D)
+    output_matrix = pick(output_whole, 1, z).reshape(heads * DH, D)
+    down_local = down_weight.astype(low)
 
     up_local = up_weight.astype(low).reshape(rows, S, Z, C * share).transpose(2, 0, 1, 3)
     up_local = up_local.reshape(Z, rows, slice_width)
@@ -406,6 +457,19 @@
         x_slots, up_local, layer_in, out_grad, qkv_matrix, vectors
     )
     inputs, grad_output = to_core(layer_in), to_core(out_grad)
+    if square:
+        down_local, x_last = together(down_local, x_slots[-1])
+        x_slots = [*x_slots[:-1], x_last]
+        down_slots = gather_slots(down_local, "seq", S)
+        down_matrix = jnp.zeros((S * C, share, D), low)
+        for k, block in enumerate(down_slots):
+            for i, value in enumerate((block, cross(block))):
+                down_matrix = lax.dynamic_update_slice_in_dim(
+                    down_matrix, value[None], (s * C + c) ^ (k * C + i), 0
+                )
+        down_matrix = down_matrix.reshape(slice_width, D)
+    else:
+        down_matrix = lax.all_gather(down_local, ("seq", "c"), axis=0, tiled=True)
     up_came = trade(up_local, "z", Z)
 
     vector = lambda i: vectors[:, i * rows : (i + 1) * rows].reshape(D)
@@ -434,28 +498,30 @@
     mixed, totals = attend(qkv, row_ids, col_ids, heads)
     up_came, mixed = together(up_came, mixed)
     up_matrix = gather_rows(ordered(up_came, "z")).reshape(D, slice_width)
-    branch_parts = split_slots(matmul(mixed, output_matrix).astype(low), Z)
-    branch = scatter_slots(branch_parts, "z", Z) + output_offset
-    hidden, first_normed, first_inverse = normalize_forward(
-        inputs + branch, first_scale, first_offset
-    )
-    hidden_low = hidden.astype(low)
+    if square:
+        slot_weights = [pick(output_whole, 1, z ^ k).reshape(heads * DH, D) for k in range(Z)]
+        h_all, hidden, first_normed, first_inverse = branch_norm(
+            gather_slots(mixed, "z", Z),
+            jnp.stack(slot_weights),
+            x_all,
+            inputs,
+            jnp.stack([output_offset, first_scale, first_offset]),
+        )
+        h_slots = split_slots(h_all, Z)
+    else:
+        branch_parts = split_slots(matmul(mixed, output_matrix).astype(low), Z)
+        branch = scatter_slots(branch_parts, "z", Z) + output_offset
+        hidden, first_normed, first_inverse = normalize_forward(
+            inputs + branch, first_scale, first_offset
+        )
+        h_slots = gather_slots(hidden.astype(low), "z", Z)
 
     def forward(h_slot):
         active, slope = gelu_both(matmul(h_slot, up_matrix) + up_offset)
         active = active.astype(low)
         return active, slope, lax.optimization_barrier(matmul(active, down_matrix).astype(low))
 
-    if Z == 4:
-        h_blocks, up_matrix, down_matrix = together(
-            spread_1(hidden_low), up_matrix, down_matrix
-        )
-        h_blocks, done_0 = together(spread_2(*h_blocks), forward(hidden_low))
-        h_slots, done_1 = together(spread_3(*h_blocks), forward(h_blocks[1]))
-        done = [done_0, done_1, forward(h_slots[2]), forward(h_slots[3])]
-    else:
-        h_slots = gather_slots(hidden_low, "z", Z)
-        done = [forward(h_slot) for h_slot in h_slots]
+    done = [forward(h_slot) for h_slot in h_slots]
     actives, slopes, downs = zip(*done, strict=True)
     down = scatter_slots(downs, "z", Z) + down_offset
     result, second_normed, second_inverse = normalize_forward(
@@ -503,9 +569,11 @@
     sent = jnp.concatenate([grad_branch, terms], axis=0)
     if Z == 4:
         b_blocks, up_term = together(spread_1(sent), by_owner(up_term))
-        b_slots = spread_3(*spread_2(*b_blocks))
+        b_blocks, layer_out = together(spread_2(*b_blocks), from_core(result))
+        b_slots = spread_3(*b_blocks)
     else:
         b_slots, up_term = gather_slots(sent, "z", Z), by_owner(up_term)
+        layer_out = from_core(result)
     up_mine = lax.psum_scatter(up_term, ("seq", "c"), scatter_dimension=0, tiled=True)
     b_all = joined([v[:-below] for v in b_slots])
     term_sums = sum(v[-below:].astype(wide) for v in b_slots)
@@ -525,12 +593,9 @@
         in_sum = sum_2(*in_parts)
     else:
         in_sum = scatter_slots(in_parts, "z", Z)
-    layer_out = from_core(result)
     input_grad = from_core(grad_first + in_sum)
     down_weight_grad = down_mine.astype(wide)
-    up_mine = exchange(up_mine.reshape(Z, rows, slice_width), "z", Z)
-    up_mine = up_mine.reshape(Z, rows, S, C * share)
-    up_weight_grad = up_mine.transpose(1, 2, 0, 3).reshape(rows, hidden_units).astype(wide)
+    up_came = trade(up_mine.reshape(Z, rows, slice_width), "z", Z)
 
     def in_plane(term, rest):
         term = term.reshape(S, -1, C, rows, rest)
@@ -547,8 +612,11 @@
             output_term.reshape(D, D), ALL, scatter_dimension=0, tiled=True
         ).astype(wide)
     qkv_mine = in_plane(transposed(x_all, grad_qkv_late).astype(low), width).astype(low)
-    qkv_mine = exchange(qkv_mine.reshape(Z, rows, width), "z", Z)
-    qkv_grads = qkv_mine.reshape(Z, rows, 3, heads, DH).transpose(2, 1, 3, 0, 4)
+    qkv_came = trade(qkv_mine.reshape(Z, rows, width), "z", Z)
+    up_came, qkv_came = together(up_came, qkv_came)
+    up_mine = ordered(up_came, "z").reshape(Z, rows, S, C * share)
+    up_weight_grad = up_mine.transpose(1, 2, 0, 3).reshape(rows, hidden_units).astype(wide)
+    qkv_grads = ordered(qkv_came, "z").reshape(Z, rows, 3, heads, DH).transpose(2, 1, 3, 0, 4)
     qkv_grads = qkv_grads.reshape(3, rows, D).astype(wide)
 
     sums = sum_over(term_sums, ("c", "seq"), sizes)

time: 873 us -> 831 us (0.952)
  waiting for transfers between devices: 385 us -> 301 us
  local copies, waits for them, and re-layouts: 74.2 us -> 102 us
  Pallas kernels: 30.3 us -> 50 us
  other arithmetic: 99.1 us -> 88 us
  matrix products: 135 us -> 144 us
    ppermute x40 -> x35, waiting for transfers between devices: 329 us -> 228 us  [send(): return lax.ppermute(value, 'z', pairs)]
    ppermute x36 -> x44, waiting for transfers between devices: 41.5 us -> 72.4 us  [swap(): return lax.ppermute(value, axis, [(i, i ^ bit) for i in range(size)])]
    pallas_call x0 -> x1, Pallas kernels: none -> 19.7 us  [branch_norm(): pl.pallas_call(branch_kernel, grid=(size,), in_specs=[*specs, pl.BlockSpe...]
    dynamic_update_slice x0 -> x8, local copies, waits for them, and re-layouts: none -> 17.5 us  [shards(): lax.dynamic_update_slice_in_dim(down_matrix, value[None], s * C + c ^ k *...]
    all_gather x2 -> x1, waiting for transfers between devices: 13.5 us -> 0.01 us  [shards(): lax.all_gather(output_weight.astype(low), ALL, axis=0, tiled=True)]
    ppermute x40 -> x35, starting transfers between devices: 87.5 us -> 81.7 us  [send(): return lax.ppermute(value, 'z', pairs)]
    dot_general x10 -> x9, matrix products: 48 us -> 52 us  [matmul(): return jnp.dot(left, right, preferred_element_type=wide)]
    convert_element_type x15 -> x13, other arithmetic: 25.2 us -> 21.5 us  [add(): return (left.astype(wide) + right.astype(wide)).astype(low)]
  transfers between devices with their start and end apart: 82 -> 84, of which waited for: 34 -> 33; matrix products, arithmetic and copies ran while one was open for 29% -> 35% of each run, Pallas kernels for 3% -> 6%
where the time goes in v3:
time: 831 us; the launch traced here: 823 us
  waiting for transfers between devices  301 us (36%)
  matrix products  144 us (17%)
  starting transfers between devices  123 us (15%)
  local copies, waits for them, and re-layouts  102 us (12%)
  other arithmetic  88 us (11%)
  Pallas kernels  50 us (6%)
  between operations  16.1 us (2%)
    ppermute x35, waiting for transfers between devices, send(): return lax.ppermute(value, 'z', pairs)  228 us
    ppermute x35, starting transfers between devices, send(): return lax.ppermute(value, 'z', pairs)  81.7 us
    ppermute x44, waiting for transfers between devices, swap(): return lax.ppermute(value, axis, [(i, i ^ bit) for i in range(size)])  72.4 us
    dot_general x10, matrix products, against(): return jnp.einsum('ti,ji->tj', left, right, preferred_element_type=wide)  54.5 us
    dot_general x9, matrix products, matmul(): return jnp.dot(left, right, preferred_element_type=wide)  52 us
    ppermute x44, starting transfers between devices, swap(): return lax.ppermute(value, axis, [(i, i ^ bit) for i in range(size)])  40.7 us
    dot_general x4, matrix products, transposed(): return jnp.einsum('ti,tj->ij', left, right, preferred_element_type=wide)  37.6 us
    convert_element_type x13, other arithmetic, add(): return (left.astype(wide) + right.astype(wide)).astype(low)  21.5 us
  transfers between devices with their start and end apart: 84, of which 33 were waited for; matrix products, arithmetic and copies ran while one was open for 35% of the time, Pallas kernels for 6%

profile of v3, /device:TPU:0, one launch (start us, length us, event | category | flops | bytes accessed | tf_op | source)
XLA Modules:
  0.0 823.2 jit_solution(605201626326320581)
XLA Ops:
  46.5 21.2 %collective-permute-done.1 = bf16[256,2048]{1,0:T(8,128)(2,1)} collective-permute-done((bf16[256,2048]{1,0:T(8,128)(2,1)S(1)}, bf16[256,2048]{1,0:T(8,128)(2,1)}, u32[]{:S(2)}, u32[]{:S(2)}) %collective-permute-start.1) | collective-permute-done | bytes 1048608 | tf_op jit(solution)/shard_map/ppermute | solution.py:284
  81.1 14.9 %collective-permute-done.4 = bf16[256,2048]{1,0:T(8,128)(2,1)} collective-permute-done((bf16[256,2048]{1,0:T(8,128)(2,1)}, bf16[256,2048]{1,0:T(8,128)(2,1)}, u32[]{:S(2)}, u32[]{:S(2)}) %collective-permute-start.4) | collective-permute-done | bytes 1048608 | tf_op jit(solution)/shard_map/ppermute | solution.py:284
  108.9 25.9 %collective-permute-done.8 = bf16[256,2048]{1,0:T(8,128)(2,1)} collective-permute-done((bf16[256,2048]{1,0:T(8,128)(2,1)}, bf16[256,2048]{1,0:T(8,128)(2,1)}, u32[]{:S(2)}, u32[]{:S(2)}) %collective-permute-start.8) | collective-permute-done | bytes 1048608 | tf_op jit(solution)/shard_map/ppermute | solution.py:284
  143.0 10.3 %add_convert_fusion.q_ref.k_ref.v_ref = bf16[1024,1536]{1,0:T(8,128)(2,1)S(1)} fusion(bf16[1024,2048]{1,0:T(8,128)(2,1)S(1)} %constant_dynamic-update-slice_fusion.refs_5_, bf16[2048,1536]{1,0:T(8,128)(2,1)} %bitcast.304, f32[1536]{0:T(1024)S(1)} %pad_maximum_fusion.18), kind=kOutput, calls=%fused_computation.9 | convolution fusion | flops 6445596672 | bytes 13637632 | tf_op jit(solution)/shard_map/dot_general | solution.py:42
  153.3 11.7 %attend.1 = (bf16[1024,512]{1,0:T(8,128)(2,1)S(1)}, f32[4,1024,1]{2,1,0:T(8,128)S(1)}) custom-call(bf16[1024,1536]{1,0:T(8,128)(2,1)S(1)} %add_convert_fusion.q_ref.k_ref.v_ref, bf16[1024,1536]{1,0:T(8,128)(2,1)S(1)} %add_convert_fusion.q_ref.k_ref.v_ref, bf16[1024,1536]{1,0:T(8,128)(2,1)S(1)} %add_convert_fusion.q_ref.k_ref.v_ref, ...), custom_call_target="tpu_custom_call" | custom-call | flops 2147483648 | bytes 4194304 | tf_op jit(solution)/shard_map/attend/pallas_call | solution.py:126
  207.8 10.3 %collective-permute-done.23 = bf16[128,2048]{1,0:T(8,128)(2,1)S(1)} collective-permute-done((bf16[128,2048]{1,0:T(8,128)(2,1)S(1)}, bf16[128,2048]{1,0:T(8,128)(2,1)S(1)}, u32[]{:S(2)}, u32[]{:S(2)}) %collective-permute-start.23) | collective-permute-done | bytes 524320 | tf_op jit(solution)/shard_map/ppermute | solution.py:240
  242.8 8.9 %collective-permute-done.15 = bf16[1024,512]{1,0:T(8,128)(2,1)} collective-permute-done((bf16[1024,512]{1,0:T(8,128)(2,1)}, bf16[1024,512]{1,0:T(8,128)(2,1)}, u32[]{:S(2)}, u32[]{:S(2)}) %collective-permute-start.15) | collective-permute-done | bytes 1048608 | tf_op jit(solution)/shard_map/ppermute | solution.py:284
  255.0 18.5 %collective-permute-done.16 = bf16[1024,512]{1,0:T(8,128)(2,1)S(1)} collective-permute-done((bf16[1024,512]{1,0:T(8,128)(2,1)}, bf16[1024,512]{1,0:T(8,128)(2,1)S(1)}, u32[]{:S(2)}, u32[]{:S(2)}) %collective-permute-start.16) | collective-permute-done | bytes 1048608 | tf_op jit(solution)/shard_map/ppermute | solution.py:284
  274.7 19.7 %branch_norm.1 = (bf16[1024,2048]{1,0:T(8,128)(2,1)}, f32[256,2048]{1,0:T(8,128)}, f32[256,2048]{1,0:T(8,128)}, f32[256,1]{1,0:T(8,128)S(1)}) custom-call(bf16[1024,512]{1,0:T(8,128)(2,1)S(1)} %get-tuple-element.156.refs_0_, bf16[1024,512]{1,0:T(8,128)(2,1)} %collective-permute-done.12.refs_1_, bf16[1024,512]{1,0:T(8,128)(2,1)} %broadcast_select_fusion.3.refs_2_, ...), custom_call_target="tpu_custom_call" | custom-call | flops 8589934592 | bytes 41943040 | tf_op jit(solution)/shard_map/branch_norm/pallas_call | solution.py:212
  329.9 12.2 %collective-permute-done.27 = bf16[256,2048]{1,0:T(8,128)(2,1)S(1)} collective-permute-done((bf16[256,2048]{1,0:T(8,128)(2,1)S(1)}, bf16[256,2048]{1,0:T(8,128)(2,1)S(1)}, u32[]{:S(2)}, u32[]{:S(2)}) %collective-permute-start.27) | collective-permute-done | bytes 1048608 | tf_op jit(solution)/shard_map/ppermute | solution.py:284
  405.0 10.1 %collective-permute-done.32 = bf16[256,2048]{1,0:T(8,128)(2,1)S(1)} collective-permute-done((bf16[256,2048]{1,0:T(8,128)(2,1)S(1)}, bf16[256,2048]{1,0:T(8,128)(2,1)S(1)}, u32[]{:S(2)}, u32[]{:S(2)}) %collective-permute-start.32) | collective-permute-done | bytes 1048608 | tf_op jit(solution)/shard_map/ppermute | solution.py:284
  440.5 21.6 %collective-permute-done.37 = bf16[256,2048]{1,0:T(8,128)(2,1)S(1)} collective-permute-done((bf16[256,2048]{1,0:T(8,128)(2,1)S(1)}, bf16[256,2048]{1,0:T(8,128)(2,1)S(1)}, u32[]{:S(2)}, u32[]{:S(2)}) %collective-permute-start.37) | collective-permute-done | bytes 1048608 | tf_op jit(solution)/shard_map/ppermute | solution.py:284
  486.9 10.5 %collective-permute-done.38 = bf16[256,2048]{1,0:T(8,128)(2,1)S(1)} collective-permute-done((bf16[256,2048]{1,0:T(8,128)(2,1)S(1)}, bf16[256,2048]{1,0:T(8,128)(2,1)S(1)}, u32[]{:S(2)}, u32[]{:S(2)}) %collective-permute-start.38) | collective-permute-done | bytes 1048608 | tf_op jit(solution)/shard_map/ppermute | solution.py:284
  501.7 11.2 %convolution_convert_fusion.2 = bf16[2048,2048]{1,0:T(8,128)(2,1)} fusion(bf16[256,2048]{1,0:T(8,128)(2,1)S(1)} %copy-done.65, bf16[256,2048]{1,0:T(8,128)(2,1)S(1)} %copy-done.67, bf16[256,2048]{1,0:T(8,128)(2,1)S(1)} %copy-done.69, bf16[256,2048]{1,0:T(8,128)(2,1)S(1)} %copy-done.71, bf16[256,2048]{1,0:T(8,128)(2,1)S(1)} %broadcast_select_fusion.4, ...), kind=kOutput, calls=%fused_computation.5 | convolution fusion | flops 8627683328 | bytes 16777216 | tf_op jit(solution)/shard_map/ti,tj->ij/dot_general | solution.py:46
  522.2 9.6 %collective-permute-start.41 = (bf16[256,2048]{1,0:T(8,128)(2,1)S(1)}, bf16[256,2048]{1,0:T(8,128)(2,1)}, u32[]{:S(2)}, u32[]{:S(2)}) collective-permute-start(bf16[256,2048]{1,0:T(8,128)(2,1)S(1)} %copy-done.28), channel_id=1, source_target_pairs={{0,2},{2,0},{4,6},{6,4},{1,3},{3,1},{5,7},{7,5},{8,10},{10,8},{12,... | collective-permute-start | bytes 3145736 | tf_op jit(solution)/shard_map/ppermute | solution.py:284
  536.0 11.8 %collective-permute-done.41 = bf16[256,2048]{1,0:T(8,128)(2,1)} collective-permute-done((bf16[256,2048]{1,0:T(8,128)(2,1)S(1)}, bf16[256,2048]{1,0:T(8,128)(2,1)}, u32[]{:S(2)}, u32[]{:S(2)}) %collective-permute-start.41) | collective-permute-done | bytes 1048608 | tf_op jit(solution)/shard_map/ppermute | solution.py:284
  558.2 14.1 %convolution_convert_fusion.1 = bf16[2048,2048]{1,0:T(8,128)(2,1)} fusion(bf16[1024,2048]{1,0:T(8,128)(2,1)} %get-tuple-element.111, bf16[256,2048]{1,0:T(8,128)(2,1)} %copy-done.40, bf16[256,2048]{1,0:T(8,128)(2,1)} %copy-done.42, bf16[256,2048]{1,0:T(8,128)(2,1)} %copy-done.38, bf16[256,2048]{1,0:T(8,128)(2,1)} %copy-done.36), kind=kOutput, calls=%fused_computation.4 | convolution fusion | flops 8610906112 | bytes 16777216 | tf_op jit(solution)/shard_map/ti,tj->ij/dot_general | solution.py:46
  589.2 20.6 %collective-permute-done.45 = bf16[264,2048]{1,0:T(8,128)(2,1)} collective-permute-done((bf16[264,2048]{1,0:T(8,128)(2,1)}, bf16[264,2048]{1,0:T(8,128)(2,1)}, u32[]{:S(2)}, u32[]{:S(2)}) %collective-permute-start.45) | collective-permute-done | bytes 1081376 | tf_op jit(solution)/shard_map/ppermute | solution.py:284
  637.8 18.5 %attend_back.1 = (bf16[1024,512]{1,0:T(8,128)(2,1)S(1)}, bf16[1024,512]{1,0:T(8,128)(2,1)S(1)}, bf16[1024,512]{1,0:T(8,128)(2,1)S(1)}) custom-call(bf16[1024,1536]{1,0:T(8,128)(2,1)} %copy-done.2, bf16[1024,1536]{1,0:T(8,128)(2,1)} %copy-done.2, bf16[1024,1536]{1,0:T(8,128)(2,1)} %copy-done.2, bf16[1024,512]{1,0:T(8,128)(2,1)S(1)} %convolution_convert_fusion.13.g_ref, ...), custom_call_target="tpu_custom_call" | custom-call | flops 5368709120 | bytes 8388608 | tf_op jit(solution)/shard_map/attend_back/pallas_call | solution.py:160
  656.6 10.0 %convolution_convert_fusion.3 = bf16[1024,2048]{1,0:T(8,128)(2,1)S(1)} fusion(bf16[1024,1536]{1,0:T(8,128)(2,1)S(1)} %constant_dynamic-update-slice_fusion.6, bf16[2048,1536]{1,0:T(8,128)(2,1)} %bitcast.305), kind=kOutput, calls=%fused_computation.26 | convolution fusion | flops 6444548096 | bytes 13631488 | tf_op jit(solution)/shard_map/ti,ji->tj/dot_general | solution.py:50
  674.6 9.7 %convolution_convert_fusion = bf16[2048,1536]{1,0:T(8,128)(2,1)S(1)} fusion(bf16[1024,2048]{1,0:T(8,128)(2,1)} %copy-done.48, bf16[1024,1536]{1,0:T(8,128)(2,1)S(1)} %copy-done.14), kind=kOutput, calls=%fused_computation.3 | convolution fusion | flops 6445596672 | bytes 13631488 | tf_op jit(solution)/shard_map/ti,tj->ij/dot_general | solution.py:46
  742.4 16.5 %collective-permute-done.52 = bf16[256,2048]{1,0:T(8,128)(2,1)S(1)} collective-permute-done((bf16[256,2048]{1,0:T(8,128)(2,1)}, bf16[256,2048]{1,0:T(8,128)(2,1)S(1)}, u32[]{:S(2)}, u32[]{:S(2)}) %collective-permute-start.52) | collective-permute-done | bytes 1048608 | tf_op jit(solution)/shard_map/ppermute | solution.py:284
  766.3 14.1 %collective-permute-done.59 = bf16[256,1536]{1,0:T(8,128)(2,1)S(1)} collective-permute-done((bf16[256,1536]{1,0:T(8,128)(2,1)S(1)}, bf16[256,1536]{1,0:T(8,128)(2,1)S(1)}, u32[]{:S(2)}, u32[]{:S(2)}) %collective-permute-start.59) | collective-permute-done | bytes 786464 | tf_op jit(solution)/shard_map/ppermute | solution.py:240
  788.6 14.5 %collective-permute-done.63 = bf16[64,1536]{1,0:T(8,128)(2,1)S(1)} collective-permute-done((bf16[64,1536]{1,0:T(8,128)(2,1)S(1)}, bf16[64,1536]{1,0:T(8,128)(2,1)S(1)}, u32[]{:S(2)}, u32[]{:S(2)}) %collective-permute-start.63) | collective-permute-done | bytes 196640 | tf_op jit(solution)/shard_map/ppermute | solution.py:240
  (536 shorter events, 460.5 us)
Async XLA Ops:
  7.2 88.8 %all-gather.4.cloned.1.call-start = ((), (), s32[]{:S(2)}) async-start(), calls=%async_computation.2 | async-start | bytes 7962624 | tf_op jit(solution)/shard_map/all_gather | solution.py:417
  39.9 183.6 %all-gather.6.cloned.1.call-start = ((), (), s32[]{:S(2)}) async-start(), calls=%async_computation.3 | async-start | bytes 8650752 | tf_op jit(solution)/shard_map/all_gather | solution.py:449
  40.7 253.8 %all-gather.8.cloned.1.call-start = ((), (), s32[]{:S(2)}) async-start(), calls=%async_computation.4 | async-start | bytes 9437184 | tf_op jit(solution)/shard_map/all_gather | solution.py:417
  40.8 26.9 %collective-permute-start.1 = (bf16[256,2048]{1,0:T(8,128)(2,1)S(1)}, bf16[256,2048]{1,0:T(8,128)(2,1)}, u32[]{:S(2)}, u32[]{:S(2)}) collective-permute-start(bf16[256,2048]{1,0:T(8,128)(2,1)S(1)} %pad_maximum_fusion.6), channel_id=1, source_target_pairs={{0,2},{2,0},{4,6},{6,4},{1,3},{3,1},{5,7},{7,5},{8,10},{10,8},{12,... | collective-permute-start | bytes 3145736 | tf_op jit(solution)/shard_map/ppermute | solution.py:284
  69.3 26.7 %collective-permute-start.4 = (bf16[256,2048]{1,0:T(8,128)(2,1)}, bf16[256,2048]{1,0:T(8,128)(2,1)}, u32[]{:S(2)}, u32[]{:S(2)}) collective-permute-start(bf16[256,2048]{1,0:T(8,128)(2,1)} %collective-permute-done.3), channel_id=1, source_target_pairs={{2,0},{4,6},{3,1},{5,7},{10,8},{12,14},{11,9},{13,15},{18,16},{20,... | collective-permute-start | bytes 3145736 | tf_op jit(solution)/shard_map/ppermute | solution.py:284
  96.0 38.8 %collective-permute-start.8 = (bf16[256,2048]{1,0:T(8,128)(2,1)}, bf16[256,2048]{1,0:T(8,128)(2,1)}, u32[]{:S(2)}, u32[]{:S(2)}) collective-permute-start(bf16[256,2048]{1,0:T(8,128)(2,1)} %collective-permute-done.2), channel_id=1, source_target_pairs={{2,0},{4,6},{3,1},{5,7},{10,8},{12,14},{11,9},{13,15},{18,16},{20,... | collective-permute-start | bytes 3145736 | tf_op jit(solution)/shard_map/ppermute | solution.py:284
  137.5 27.6 %collective-permute-start.10 = (bf16[64,2048]{1,0:T(8,128)(2,1)S(1)}, bf16[64,2048]{1,0:T(8,128)(2,1)S(1)}, u32[]{:S(2)}, u32[]{:S(2)}) collective-permute-start(bf16[64,2048]{1,0:T(8,128)(2,1)S(1)} %get-tuple-element.296), channel_id=1, source_target_pairs={{0,4},{2,6},{4,0},{6,2},{1,5},{3,7},{5,1},{7,3},{8,12},{10,14},{12... | collective-permute-start | bytes 786440 | tf_op jit(solution)/shard_map/ppermute | solution.py:240
  137.6 27.6 %collective-permute-start.11 = (bf16[64,2048]{1,0:T(8,128)(2,1)S(1)}, bf16[64,2048]{1,0:T(8,128)(2,1)S(1)}, u32[]{:S(2)}, u32[]{:S(2)}) collective-permute-start(bf16[64,2048]{1,0:T(8,128)(2,1)S(1)} %get-tuple-element.295), channel_id=1, source_target_pairs={{0,6},{2,4},{4,2},{6,0},{1,7},{3,5},{5,3},{7,1},{8,14},{10,12},{12... | collective-permute-start | bytes 786440 | tf_op jit(solution)/shard_map/ppermute | solution.py:240
  166.9 501.6 %reduce-scatter.3.cloned.1.call-start = ((), (), s32[]{:S(2)}) async-start(), calls=%async_computation.5 | async-start | bytes 9437184 | tf_op jit(solution)/shard_map/reduce_scatter | solution.py:551
  167.0 31.6 %collective-permute-start.18 = (bf16[256,2048]{1,0:T(8,128)(2,1)}, bf16[256,2048]{1,0:T(8,128)(2,1)}, u32[]{:S(2)}, u32[]{:S(2)}) collective-permute-start(bf16[256,2048]{1,0:T(8,128)(2,1)} %convert_element_type.408), channel_id=1, source_target_pairs={{0,1},{1,0},{2,3},{3,2},{4,5},{5,4},{6,7},{7,6},{8,9},{9,8},{10,11... | collective-permute-start | bytes 3145736 | tf_op jit(solution)/shard_map/ppermute | solution.py:240
  168.8 26.9 %collective-permute-start.21 = (bf16[256,2048]{1,0:T(8,128)(2,1)}, bf16[256,2048]{1,0:T(8,128)(2,1)}, u32[]{:S(2)}, u32[]{:S(2)}) collective-permute-start(bf16[256,2048]{1,0:T(8,128)(2,1)} %convert_element_type.408), channel_id=1, source_target_pairs={{0,16},{8,24},{16,0},{24,8},{1,17},{9,25},{17,1},{25,9},{2,18},{10... | collective-permute-start | bytes 3145736 | tf_op jit(solution)/shard_map/ppermute | solution.py:240
  174.0 31.1 %collective-permute-start.17 = (f32[128,2048]{1,0:T(8,128)}, f32[128,2048]{1,0:T(8,128)}, u32[]{:S(2)}, u32[]{:S(2)}) collective-permute-start(f32[128,2048]{1,0:T(8,128)} %get-tuple-element.269), channel_id=1, source_target_pairs={{0,1},{1,0},{2,3},{3,2},{4,5},{5,4},{6,7},{7,6},{8,9},{9,8},{10,11... | collective-permute-start | bytes 3145736 | tf_op jit(solution)/shard_map/ppermute | solution.py:240
  184.5 34.4 %collective-permute-start.12 = (bf16[1024,512]{1,0:T(8,128)(2,1)S(1)}, bf16[1024,512]{1,0:T(8,128)(2,1)}, u32[]{:S(2)}, u32[]{:S(2)}) collective-permute-start(bf16[1024,512]{1,0:T(8,128)(2,1)S(1)} %get-tuple-element.156.refs_0_), channel_id=1, source_target_pairs={{0,2},{2,0},{4,6},{6,4},{1,3},{3,1},{5,7},{7,5},{8,10},{10,8},{12,... | collective-permute-start | bytes 3145736 | tf_op jit(solution)/shard_map/ppermute | solution.py:284
  205.0 184.0 %collective-permute-start.31 = (f32[128,2048]{1,0:T(8,128)}, f32[128,2048]{1,0:T(8,128)}, u32[]{:S(2)}, u32[]{:S(2)}) collective-permute-start(f32[128,2048]{1,0:T(8,128)} %get-tuple-element.266), channel_id=1, source_target_pairs={{0,1},{1,0},{2,3},{3,2},{4,5},{5,4},{6,7},{7,6},{8,9},{9,8},{10,11... | collective-permute-start | bytes 3145736 | tf_op jit(solution)/shard_map/ppermute | solution.py:240
  221.1 30.5 %collective-permute-start.15 = (bf16[1024,512]{1,0:T(8,128)(2,1)}, bf16[1024,512]{1,0:T(8,128)(2,1)}, u32[]{:S(2)}, u32[]{:S(2)}) collective-permute-start(bf16[1024,512]{1,0:T(8,128)(2,1)} %collective-permute-done.14), channel_id=1, source_target_pairs={{2,0},{4,6},{3,1},{5,7},{10,8},{12,14},{11,9},{13,15},{18,16},{20,... | collective-permute-start | bytes 3145736 | tf_op jit(solution)/shard_map/ppermute | solution.py:284
  239.1 34.5 %collective-permute-start.16 = (bf16[1024,512]{1,0:T(8,128)(2,1)}, bf16[1024,512]{1,0:T(8,128)(2,1)S(1)}, u32[]{:S(2)}, u32[]{:S(2)}) collective-permute-start(bf16[1024,512]{1,0:T(8,128)(2,1)} %collective-permute-done.13), channel_id=1, source_target_pairs={{2,0},{4,6},{3,1},{5,7},{10,8},{12,14},{11,9},{13,15},{18,16},{20,... | collective-permute-start | bytes 3145736 | tf_op jit(solution)/shard_map/ppermute | solution.py:284
  328.6 31.7 %collective-permute-start.26 = (bf16[256,2048]{1,0:T(8,128)(2,1)S(1)}, bf16[256,2048]{1,0:T(8,128)(2,1)S(1)}, u32[]{:S(2)}, u32[]{:S(2)}) collective-permute-start(bf16[256,2048]{1,0:T(8,128)(2,1)S(1)} %convolution_convert_fusion.10), channel_id=1, source_target_pairs={{0,2},{6,4},{1,3},{7,5},{8,10},{14,12},{9,11},{15,13},{16,18},{22,... | collective-permute-start | bytes 3145736 | tf_op jit(solution)/shard_map/ppermute | solution.py:284
  427.9 34.2 %collective-permute-start.37 = (bf16[256,2048]{1,0:T(8,128)(2,1)S(1)}, bf16[256,2048]{1,0:T(8,128)(2,1)S(1)}, u32[]{:S(2)}, u32[]{:S(2)}) collective-permute-start(bf16[256,2048]{1,0:T(8,128)(2,1)S(1)} %collective-permute-done.33), channel_id=1, source_target_pairs={{2,0},{4,6},{3,1},{5,7},{10,8},{12,14},{11,9},{13,15},{18,16},{20,... | collective-permute-start | bytes 3145736 | tf_op jit(solution)/shard_map/ppermute | solution.py:284
  484.3 30.4 %collective-permute-start.36 = (bf16[256,2048]{1,0:T(8,128)(2,1)}, bf16[256,2048]{1,0:T(8,128)(2,1)}, u32[]{:S(2)}, u32[]{:S(2)}) collective-permute-start(bf16[256,2048]{1,0:T(8,128)(2,1)} %convolution_convert_fusion.6), channel_id=1, source_target_pairs={{0,2},{6,4},{1,3},{7,5},{8,10},{14,12},{9,11},{15,13},{16,18},{22,... | collective-permute-start | bytes 3145736 | tf_op jit(solution)/shard_map/ppermute | solution.py:284
  520.3 207.2 %reduce-scatter.5.cloned.1.call-start = ((), (), s32[]{:S(2)}) async-start(), calls=%async_computation.6 | async-start | bytes 9437184 | tf_op jit(solution)/shard_map/reduce_scatter | solution.py:577
  535.8 50.0 %collective-permute-start.46 = (f32[128,2048]{1,0:T(8,128)}, f32[128,2048]{1,0:T(8,128)}, u32[]{:S(2)}, u32[]{:S(2)}) collective-permute-start(f32[128,2048]{1,0:T(8,128)} %slice.321), channel_id=1, source_target_pairs={{0,1},{1,0},{2,3},{3,2},{4,5},{5,4},{6,7},{7,6},{8,9},{9,8},{10,11... | collective-permute-start | bytes 3145736 | tf_op jit(solution)/shard_map/ppermute | solution.py:240
  668.5 36.1 %collective-permute-start.49 = (bf16[256,2048]{1,0:T(8,128)(2,1)}, bf16[256,2048]{1,0:T(8,128)(2,1)}, u32[]{:S(2)}, u32[]{:S(2)}) collective-permute-start(bf16[256,2048]{1,0:T(8,128)(2,1)} %get-tuple-element.143), channel_id=1, source_target_pairs={{0,2},{6,4},{1,3},{7,5},{8,10},{14,12},{9,11},{15,13},{16,18},{22,... | collective-permute-start | bytes 3145736 | tf_op jit(solution)/shard_map/ppermute | solution.py:284
  696.9 41.0 %collective-permute-start.57 = (bf16[4,4,64,1536]{3,2,1,0:T(8,128)(2,1)}, bf16[4,4,64,1536]{3,2,1,0:T(8,128)(2,1)}, u32[]{:S(2)}, u32[]{:S(2)}) collective-permute-start(bf16[4,4,64,1536]{3,2,1,0:T(8,128)(2,1)} %dynamic-slice_bitcast_fusion), channel_id=1, source_target_pairs={{0,1},{1,0},{2,3},{3,2},{4,5},{5,4},{6,7},{7,6},{8,9},{9,8},{10,11... | collective-permute-start | bytes 9437192 | tf_op jit(solution)/shard_map/ppermute | solution.py:240
  728.4 30.6 %collective-permute-start.52 = (bf16[256,2048]{1,0:T(8,128)(2,1)}, bf16[256,2048]{1,0:T(8,128)(2,1)S(1)}, u32[]{:S(2)}, u32[]{:S(2)}) collective-permute-start(bf16[256,2048]{1,0:T(8,128)(2,1)} %add_convert_fusion.2), channel_id=1, source_target_pairs={{0,2},{2,0},{4,6},{6,4},{1,3},{3,1},{5,7},{7,5},{8,10},{10,8},{12,... | collective-permute-start | bytes 3145736 | tf_op jit(solution)/shard_map/ppermute | solution.py:284
  (134 other events, 1787.5 us)
Sparse Core Ops, SparseCore 0:
  40.0 51.5 all-gather.3
  95.1 88.8 all-gather.5
  185.9 63.1 all-gather.7
  520.4 80.4 reduce-scatter.2
  621.7 73.3 reduce-scatter.4

commit v4 on v3

--- a/solution.py
+++ b/solution.py
@@ -446,9 +446,15 @@
     vectors = vectors.astype(wide)
 
     square = Z == 4 and S == 4 and whole_heads
-    output_whole = lax.all_gather(output_weight.astype(low), ALL, axis=0, tiled=True)
-    output_whole = output_whole.reshape(heads, Z, DH, D)
-    output_matrix = pick(output_whole, 1, z).reshape(heads * DH, D)
+    if square:
+        output_slots = jnp.concatenate(gather_slots(output_weight.astype(low), "z", Z), axis=0)
+        output_whole = lax.all_gather(output_slots, ("seq", "c"), axis=0, tiled=False)
+        output_whole = output_whole.reshape(S * C, Z, rows, D).transpose(1, 0, 2, 3)
+        output_whole = output_whole.reshape(Z, heads * DH, D)
+        output_matrix = output_whole[0]
+    else:
+        output_whole = lax.all_gather(output_weight.astype(low), ALL, axis=0, tiled=True)
+        output_matrix = pick(output_whole.reshape(heads, Z, DH, D), 1, z).reshape(heads * DH, D)
     down_local = down_weight.astype(low)
 
     up_local = up_weight.astype(low).reshape(rows, S, Z, C * share).transpose(2, 0, 1, 3)
@@ -499,10 +505,9 @@
     up_came, mixed = together(up_came, mixed)
     up_matrix = gather_rows(ordered(up_came, "z")).reshape(D, slice_width)
     if square:
-        slot_weights = [pick(output_whole, 1, z ^ k).reshape(heads * DH, D) for k in range(Z)]
         h_all, hidden, first_normed, first_inverse = branch_norm(
             gather_slots(mixed, "z", Z),
-            jnp.stack(slot_weights),
+            output_whole,
             x_all,
             inputs,
             jnp.stack([output_offset, first_scale, first_offset]),

time: 831 us -> 852 us (1.025)
  waiting for transfers between devices: 301 us -> 324 us
    ppermute x35 -> x40, waiting for transfers between devices: 228 us -> 241 us  [send(): return lax.ppermute(value, 'z', pairs)]
    ppermute x44, waiting for transfers between devices: 72.4 us -> 82.4 us  [swap(): return lax.ppermute(value, axis, [(i, i ^ bit) for i in range(size)])]
    ppermute x35 -> x40, starting transfers between devices: 81.7 us -> 78.7 us  [send(): return lax.ppermute(value, 'z', pairs)]
  transfers between devices with their start and end apart: 84 -> 89, of which waited for: 33 -> 36; matrix products, arithmetic and copies ran while one was open for 35% -> 34% of each run, Pallas kernels for 6% -> 6%
where the time goes in v4:
time: 852 us; the launch traced here: 844 us
  waiting for transfers between devices  324 us (38%)
  matrix products  144 us (17%)
  starting transfers between devices  119 us (14%)
  local copies, waits for them, and re-layouts  108 us (13%)
  other arithmetic  82.4 us (10%)
  Pallas kernels  49.8 us (6%)
  between operations  16.2 us (2%)
    ppermute x40, waiting for transfers between devices, send(): return lax.ppermute(value, 'z', pairs)  241 us
    ppermute x44, waiting for transfers between devices, swap(): return lax.ppermute(value, axis, [(i, i ^ bit) for i in range(size)])  82.4 us
    ppermute x40, starting transfers between devices, send(): return lax.ppermute(value, 'z', pairs)  78.7 us
    dot_general x10, matrix products, against(): return jnp.einsum('ti,ji->tj', left, right, preferred_element_type=wide)  54.3 us
    dot_general x9, matrix products, matmul(): return jnp.dot(left, right, preferred_element_type=wide)  52 us
    ppermute x44, starting transfers between devices, swap(): return lax.ppermute(value, axis, [(i, i ^ bit) for i in range(size)])  40.4 us
    dot_general x4, matrix products, transposed(): return jnp.einsum('ti,tj->ij', left, right, preferred_element_type=wide)  37.8 us
    convert_element_type x13, other arithmetic, add(): return (left.astype(wide) + right.astype(wide)).astype(low)  21.4 us
  transfers between devices with their start and end apart: 89, of which 36 were waited for; matrix products, arithmetic and copies ran while one was open for 34% of the time, Pallas kernels for 6%

profile of v4, /device:TPU:0, one launch (start us, length us, event | category | flops | bytes accessed | tf_op | source)
XLA Modules:
  0.0 843.7 jit_solution(6508301562864472872)
XLA Ops:
  69.6 21.6 %collective-permute-done.1 = bf16[256,2048]{1,0:T(8,128)(2,1)} collective-permute-done((bf16[256,2048]{1,0:T(8,128)(2,1)S(1)}, bf16[256,2048]{1,0:T(8,128)(2,1)}, u32[]{:S(2)}, u32[]{:S(2)}) %collective-permute-start.1) | collective-permute-done | bytes 1048608 | tf_op jit(solution)/shard_map/ppermute | solution.py:284
  104.9 12.5 %collective-permute-done.4 = bf16[256,2048]{1,0:T(8,128)(2,1)} collective-permute-done((bf16[256,2048]{1,0:T(8,128)(2,1)}, bf16[256,2048]{1,0:T(8,128)(2,1)}, u32[]{:S(2)}, u32[]{:S(2)}) %collective-permute-start.4) | collective-permute-done | bytes 1048608 | tf_op jit(solution)/shard_map/ppermute | solution.py:284
  148.9 10.3 %add_convert_fusion.q_ref.k_ref.v_ref = bf16[1024,1536]{1,0:T(8,128)(2,1)S(1)} fusion(bf16[1024,2048]{1,0:T(8,128)(2,1)S(1)} %constant_dynamic-update-slice_fusion.refs_5_, bf16[2048,1536]{1,0:T(8,128)(2,1)} %bitcast.293, f32[1536]{0:T(1024)S(1)} %pad_maximum_fusion.18), kind=kOutput, calls=%fused_computation.8 | convolution fusion | flops 6445596672 | bytes 13637632 | tf_op jit(solution)/shard_map/dot_general | solution.py:42
  159.2 11.7 %attend.1 = (bf16[1024,512]{1,0:T(8,128)(2,1)S(1)}, f32[4,1024,1]{2,1,0:T(8,128)S(1)}) custom-call(bf16[1024,1536]{1,0:T(8,128)(2,1)S(1)} %add_convert_fusion.q_ref.k_ref.v_ref, bf16[1024,1536]{1,0:T(8,128)(2,1)S(1)} %add_convert_fusion.q_ref.k_ref.v_ref, bf16[1024,1536]{1,0:T(8,128)(2,1)S(1)} %add_convert_fusion.q_ref.k_ref.v_ref, ...), custom_call_target="tpu_custom_call" | custom-call | flops 2147483648 | bytes 4194304 | tf_op jit(solution)/shard_map/attend/pallas_call | solution.py:126
  190.2 19.7 %collective-permute-done.24 = bf16[256,2048]{1,0:T(8,128)(2,1)} collective-permute-done((bf16[256,2048]{1,0:T(8,128)(2,1)}, bf16[256,2048]{1,0:T(8,128)(2,1)}, u32[]{:S(2)}, u32[]{:S(2)}) %collective-permute-start.24) | collective-permute-done | bytes 1048608 | tf_op jit(solution)/shard_map/ppermute | solution.py:240
  252.4 17.9 %collective-permute-done.15 = bf16[1024,512]{1,0:T(8,128)(2,1)S(1)} collective-permute-done((bf16[1024,512]{1,0:T(8,128)(2,1)}, bf16[1024,512]{1,0:T(8,128)(2,1)S(1)}, u32[]{:S(2)}, u32[]{:S(2)}) %collective-permute-start.15) | collective-permute-done | bytes 1048608 | tf_op jit(solution)/shard_map/ppermute | solution.py:284
  272.4 21.5 %collective-permute-done.16 = bf16[1024,512]{1,0:T(8,128)(2,1)S(1)} collective-permute-done((bf16[1024,512]{1,0:T(8,128)(2,1)S(1)}, bf16[1024,512]{1,0:T(8,128)(2,1)S(1)}, u32[]{:S(2)}, u32[]{:S(2)}) %collective-permute-start.16) | collective-permute-done | bytes 1048608 | tf_op jit(solution)/shard_map/ppermute | solution.py:284
  295.0 19.7 %branch_norm.1 = (bf16[1024,2048]{1,0:T(8,128)(2,1)}, f32[256,2048]{1,0:T(8,128)}, f32[256,2048]{1,0:T(8,128)}, f32[256,1]{1,0:T(8,128)S(1)}) custom-call(bf16[1024,512]{1,0:T(8,128)(2,1)S(1)} %get-tuple-element.156.refs_0_, bf16[1024,512]{1,0:T(8,128)(2,1)} %collective-permute-done.12.refs_1_, bf16[1024,512]{1,0:T(8,128)(2,1)} %broadcast_select_fusion.3.refs_2_, ...), custom_call_target="tpu_custom_call" | custom-call | flops 8589934592 | bytes 41943040 | tf_op jit(solution)/shard_map/branch_norm/pallas_call | solution.py:212
  349.9 12.4 %collective-permute-done.32 = bf16[256,2048]{1,0:T(8,128)(2,1)S(1)} collective-permute-done((bf16[256,2048]{1,0:T(8,128)(2,1)S(1)}, bf16[256,2048]{1,0:T(8,128)(2,1)S(1)}, u32[]{:S(2)}, u32[]{:S(2)}) %collective-permute-start.32) | collective-permute-done | bytes 1048608 | tf_op jit(solution)/shard_map/ppermute | solution.py:284
  426.7 10.2 %collective-permute-done.37 = bf16[256,2048]{1,0:T(8,128)(2,1)S(1)} collective-permute-done((bf16[256,2048]{1,0:T(8,128)(2,1)S(1)}, bf16[256,2048]{1,0:T(8,128)(2,1)S(1)}, u32[]{:S(2)}, u32[]{:S(2)}) %collective-permute-start.37) | collective-permute-done | bytes 1048608 | tf_op jit(solution)/shard_map/ppermute | solution.py:284
  453.4 10.1 %collective-permute-done.40 = bf16[256,2048]{1,0:T(8,128)(2,1)S(1)} collective-permute-done((bf16[256,2048]{1,0:T(8,128)(2,1)S(1)}, bf16[256,2048]{1,0:T(8,128)(2,1)S(1)}, u32[]{:S(2)}, u32[]{:S(2)}) %collective-permute-start.40) | collective-permute-done | bytes 1048608 | tf_op jit(solution)/shard_map/ppermute | solution.py:284
  463.6 21.0 %collective-permute-done.42 = bf16[256,2048]{1,0:T(8,128)(2,1)S(1)} collective-permute-done((bf16[256,2048]{1,0:T(8,128)(2,1)S(1)}, bf16[256,2048]{1,0:T(8,128)(2,1)S(1)}, u32[]{:S(2)}, u32[]{:S(2)}) %collective-permute-start.42) | collective-permute-done | bytes 1048608 | tf_op jit(solution)/shard_map/ppermute | solution.py:284
  509.0 10.7 %collective-permute-done.43 = bf16[256,2048]{1,0:T(8,128)(2,1)S(1)} collective-permute-done((bf16[256,2048]{1,0:T(8,128)(2,1)S(1)}, bf16[256,2048]{1,0:T(8,128)(2,1)S(1)}, u32[]{:S(2)}, u32[]{:S(2)}) %collective-permute-start.43) | collective-permute-done | bytes 1048608 | tf_op jit(solution)/shard_map/ppermute | solution.py:284
  524.0 11.2 %convolution_convert_fusion.2 = bf16[2048,2048]{1,0:T(8,128)(2,1)} fusion(bf16[256,2048]{1,0:T(8,128)(2,1)S(1)} %copy-done.64, bf16[256,2048]{1,0:T(8,128)(2,1)S(1)} %copy-done.66, bf16[256,2048]{1,0:T(8,128)(2,1)S(1)} %copy-done.68, bf16[256,2048]{1,0:T(8,128)(2,1)S(1)} %copy-done.70, bf16[256,2048]{1,0:T(8,128)(2,1)S(1)} %broadcast_select_fusion.4, ...), kind=kOutput, calls=%fused_computation.4 | convolution fusion | flops 8627683328 | bytes 16777216 | tf_op jit(solution)/shard_map/ti,tj->ij/dot_general | solution.py:46
  556.6 11.5 %collective-permute-done.46 = bf16[256,2048]{1,0:T(8,128)(2,1)} collective-permute-done((bf16[256,2048]{1,0:T(8,128)(2,1)S(1)}, bf16[256,2048]{1,0:T(8,128)(2,1)}, u32[]{:S(2)}, u32[]{:S(2)}) %collective-permute-start.46) | collective-permute-done | bytes 1048608 | tf_op jit(solution)/shard_map/ppermute | solution.py:284
  578.3 14.4 %convolution_convert_fusion.1 = bf16[2048,2048]{1,0:T(8,128)(2,1)} fusion(bf16[1024,2048]{1,0:T(8,128)(2,1)} %get-tuple-element.111, bf16[256,2048]{1,0:T(8,128)(2,1)} %copy-done.39, bf16[256,2048]{1,0:T(8,128)(2,1)} %copy-done.41, bf16[256,2048]{1,0:T(8,128)(2,1)} %copy-done.37, bf16[256,2048]{1,0:T(8,128)(2,1)} %copy-done.35), kind=kOutput, calls=%fused_computation.3 | convolution fusion | flops 8610906112 | bytes 16777216 | tf_op jit(solution)/shard_map/ti,tj->ij/dot_general | solution.py:46
  609.3 20.5 %collective-permute-done.50 = bf16[264,2048]{1,0:T(8,128)(2,1)} collective-permute-done((bf16[264,2048]{1,0:T(8,128)(2,1)}, bf16[264,2048]{1,0:T(8,128)(2,1)}, u32[]{:S(2)}, u32[]{:S(2)}) %collective-permute-start.50) | collective-permute-done | bytes 1081376 | tf_op jit(solution)/shard_map/ppermute | solution.py:284
  658.3 18.4 %attend_back.1 = (bf16[1024,512]{1,0:T(8,128)(2,1)S(1)}, bf16[1024,512]{1,0:T(8,128)(2,1)S(1)}, bf16[1024,512]{1,0:T(8,128)(2,1)S(1)}) custom-call(bf16[1024,1536]{1,0:T(8,128)(2,1)} %copy-done.2, bf16[1024,1536]{1,0:T(8,128)(2,1)} %copy-done.2, bf16[1024,1536]{1,0:T(8,128)(2,1)} %copy-done.2, bf16[1024,512]{1,0:T(8,128)(2,1)S(1)} %convolution_convert_fusion.13.g_ref, ...), custom_call_target="tpu_custom_call" | custom-call | flops 5368709120 | bytes 8388608 | tf_op jit(solution)/shard_map/attend_back/pallas_call | solution.py:160
  676.9 10.0 %convolution_convert_fusion.3 = bf16[1024,2048]{1,0:T(8,128)(2,1)S(1)} fusion(bf16[1024,1536]{1,0:T(8,128)(2,1)S(1)} %constant_dynamic-update-slice_fusion.6, bf16[2048,1536]{1,0:T(8,128)(2,1)} %bitcast.294), kind=kOutput, calls=%fused_computation.25 | convolution fusion | flops 6444548096 | bytes 13631488 | tf_op jit(solution)/shard_map/ti,ji->tj/dot_general | solution.py:50
  695.5 9.7 %convolution_convert_fusion = bf16[2048,1536]{1,0:T(8,128)(2,1)S(1)} fusion(bf16[1024,2048]{1,0:T(8,128)(2,1)} %copy-done.47, bf16[1024,1536]{1,0:T(8,128)(2,1)S(1)} %copy-done.13), kind=kOutput, calls=%fused_computation.2 | convolution fusion | flops 6445596672 | bytes 13631488 | tf_op jit(solution)/shard_map/ti,tj->ij/dot_general | solution.py:46
  747.3 9.6 %collective-permute-start.57 = (bf16[256,2048]{1,0:T(8,128)(2,1)}, bf16[256,2048]{1,0:T(8,128)(2,1)S(1)}, u32[]{:S(2)}, u32[]{:S(2)}) collective-permute-start(bf16[256,2048]{1,0:T(8,128)(2,1)} %add_convert_fusion.2), channel_id=1, source_target_pairs={{0,2},{2,0},{4,6},{6,4},{1,3},{3,1},{5,7},{7,5},{8,10},{10,8},{12,... | collective-permute-start | bytes 3145736 | tf_op jit(solution)/shard_map/ppermute | solution.py:284
  763.8 15.1 %collective-permute-done.57 = bf16[256,2048]{1,0:T(8,128)(2,1)S(1)} collective-permute-done((bf16[256,2048]{1,0:T(8,128)(2,1)}, bf16[256,2048]{1,0:T(8,128)(2,1)S(1)}, u32[]{:S(2)}, u32[]{:S(2)}) %collective-permute-start.57) | collective-permute-done | bytes 1048608 | tf_op jit(solution)/shard_map/ppermute | solution.py:284
  786.8 13.6 %collective-permute-done.64 = bf16[256,1536]{1,0:T(8,128)(2,1)S(1)} collective-permute-done((bf16[256,1536]{1,0:T(8,128)(2,1)S(1)}, bf16[256,1536]{1,0:T(8,128)(2,1)S(1)}, u32[]{:S(2)}, u32[]{:S(2)}) %collective-permute-start.64) | collective-permute-done | bytes 786464 | tf_op jit(solution)/shard_map/ppermute | solution.py:240
  808.4 15.1 %collective-permute-done.68 = bf16[64,1536]{1,0:T(8,128)(2,1)S(1)} collective-permute-done((bf16[64,1536]{1,0:T(8,128)(2,1)S(1)}, bf16[64,1536]{1,0:T(8,128)(2,1)S(1)}, u32[]{:S(2)}, u32[]{:S(2)}) %collective-permute-start.68) | collective-permute-done | bytes 196640 | tf_op jit(solution)/shard_map/ppermute | solution.py:240
  (547 shorter events, 479.2 us)
Async XLA Ops:
  7.2 110.2 %all-gather.5.cloned.1.call-start = ((), (), s32[]{:S(2)}) async-start(), calls=%async_computation.2 | async-start | bytes 7962624 | tf_op jit(solution)/shard_map/all_gather | solution.py:417
  39.9 186.1 %all-gather.9.cloned.1.call-start = ((), (), s32[]{:S(2)}) async-start(), calls=%async_computation.6 | async-start | bytes 9437184 | tf_op jit(solution)/shard_map/all_gather | solution.py:451
  67.9 246.9 %all-gather.7.cloned.1.call-start = ((), (), s32[]{:S(2)}) async-start(), calls=%async_computation.3 | async-start | bytes 9437184 | tf_op jit(solution)/shard_map/all_gather | solution.py:417
  143.3 27.7 %collective-permute-start.10 = (bf16[64,2048]{1,0:T(8,128)(2,1)S(1)}, bf16[64,2048]{1,0:T(8,128)(2,1)S(1)}, u32[]{:S(2)}, u32[]{:S(2)}) collective-permute-start(bf16[64,2048]{1,0:T(8,128)(2,1)S(1)} %get-tuple-element.294), channel_id=1, source_target_pairs={{0,4},{2,6},{4,0},{6,2},{1,5},{3,7},{5,1},{7,3},{8,12},{10,14},{12... | collective-permute-start | bytes 786440 | tf_op jit(solution)/shard_map/ppermute | solution.py:240
  143.3 27.7 %collective-permute-start.11 = (bf16[64,2048]{1,0:T(8,128)(2,1)S(1)}, bf16[64,2048]{1,0:T(8,128)(2,1)S(1)}, u32[]{:S(2)}, u32[]{:S(2)}) collective-permute-start(bf16[64,2048]{1,0:T(8,128)(2,1)S(1)} %get-tuple-element.293), channel_id=1, source_target_pairs={{0,6},{2,4},{4,2},{6,0},{1,7},{3,5},{5,3},{7,1},{8,14},{10,12},{12... | collective-permute-start | bytes 786440 | tf_op jit(solution)/shard_map/ppermute | solution.py:240
  172.7 516.0 %reduce-scatter.3.cloned.1.call-start = ((), (), s32[]{:S(2)}) async-start(), calls=%async_computation.4 | async-start | bytes 9437184 | tf_op jit(solution)/shard_map/reduce_scatter | solution.py:556
  172.8 44.2 %collective-permute-start.23 = (bf16[256,2048]{1,0:T(8,128)(2,1)}, bf16[256,2048]{1,0:T(8,128)(2,1)}, u32[]{:S(2)}, u32[]{:S(2)}) collective-permute-start(bf16[256,2048]{1,0:T(8,128)(2,1)} %convert_element_type.408), channel_id=1, source_target_pairs={{0,1},{1,0},{2,3},{3,2},{4,5},{5,4},{6,7},{7,6},{8,9},{9,8},{10,11... | collective-permute-start | bytes 3145736 | tf_op jit(solution)/shard_map/ppermute | solution.py:240
  172.9 37.1 %collective-permute-start.24 = (bf16[256,2048]{1,0:T(8,128)(2,1)}, bf16[256,2048]{1,0:T(8,128)(2,1)}, u32[]{:S(2)}, u32[]{:S(2)}) collective-permute-start(bf16[256,2048]{1,0:T(8,128)(2,1)} %convert_element_type.408), channel_id=1, source_target_pairs={{0,8},{8,0},{16,24},{24,16},{1,9},{9,1},{17,25},{25,17},{2,10},{10... | collective-permute-start | bytes 3145736 | tf_op jit(solution)/shard_map/ppermute | solution.py:240
  174.4 39.1 %collective-permute-start.26 = (bf16[256,2048]{1,0:T(8,128)(2,1)}, bf16[256,2048]{1,0:T(8,128)(2,1)}, u32[]{:S(2)}, u32[]{:S(2)}) collective-permute-start(bf16[256,2048]{1,0:T(8,128)(2,1)} %convert_element_type.408), channel_id=1, source_target_pairs={{0,16},{8,24},{16,0},{24,8},{1,17},{9,25},{17,1},{25,9},{2,18},{10... | collective-permute-start | bytes 3145736 | tf_op jit(solution)/shard_map/ppermute | solution.py:240
  179.2 41.6 %collective-permute-start.22 = (f32[128,2048]{1,0:T(8,128)}, f32[128,2048]{1,0:T(8,128)}, u32[]{:S(2)}, u32[]{:S(2)}) collective-permute-start(f32[128,2048]{1,0:T(8,128)} %get-tuple-element.267), channel_id=1, source_target_pairs={{0,1},{1,0},{2,3},{3,2},{4,5},{5,4},{6,7},{7,6},{8,9},{9,8},{10,11... | collective-permute-start | bytes 3145736 | tf_op jit(solution)/shard_map/ppermute | solution.py:240
  189.6 50.9 %collective-permute-start.12 = (bf16[1024,512]{1,0:T(8,128)(2,1)S(1)}, bf16[1024,512]{1,0:T(8,128)(2,1)}, u32[]{:S(2)}, u32[]{:S(2)}) collective-permute-start(bf16[1024,512]{1,0:T(8,128)(2,1)S(1)} %get-tuple-element.156.refs_0_), channel_id=1, source_target_pairs={{0,2},{2,0},{4,6},{6,4},{1,3},{3,1},{5,7},{7,5},{8,10},{10,8},{12,... | collective-permute-start | bytes 3145736 | tf_op jit(solution)/shard_map/ppermute | solution.py:284
  210.0 31.1 %collective-permute-start.14 = (bf16[1024,512]{1,0:T(8,128)(2,1)S(1)}, bf16[1024,512]{1,0:T(8,128)(2,1)}, u32[]{:S(2)}, u32[]{:S(2)}) collective-permute-start(bf16[1024,512]{1,0:T(8,128)(2,1)S(1)} %get-tuple-element.156.refs_0_), channel_id=1, source_target_pairs={{2,4},{4,2},{3,5},{5,3},{10,12},{12,10},{11,13},{13,11},{18,20},{2... | collective-permute-start | bytes 3145736 | tf_op jit(solution)/shard_map/ppermute | solution.py:284
  239.5 171.4 %collective-permute-start.36 = (f32[128,2048]{1,0:T(8,128)}, f32[128,2048]{1,0:T(8,128)}, u32[]{:S(2)}, u32[]{:S(2)}) collective-permute-start(f32[128,2048]{1,0:T(8,128)} %get-tuple-element.264), channel_id=1, source_target_pairs={{0,1},{1,0},{2,3},{3,2},{4,5},{5,4},{6,7},{7,6},{8,9},{9,8},{10,11... | collective-permute-start | bytes 3145736 | tf_op jit(solution)/shard_map/ppermute | solution.py:240
  242.7 27.6 %collective-permute-start.15 = (bf16[1024,512]{1,0:T(8,128)(2,1)}, bf16[1024,512]{1,0:T(8,128)(2,1)S(1)}, u32[]{:S(2)}, u32[]{:S(2)}) collective-permute-start(bf16[1024,512]{1,0:T(8,128)(2,1)} %collective-permute-done.14), channel_id=1, source_target_pairs={{2,0},{4,6},{3,1},{5,7},{10,8},{12,14},{11,9},{13,15},{18,16},{20,... | collective-permute-start | bytes 3145736 | tf_op jit(solution)/shard_map/ppermute | solution.py:284
  244.0 27.3 %collective-permute-start.30 = (bf16[256,2048]{1,0:T(8,128)(2,1)S(1)}, bf16[256,2048]{1,0:T(8,128)(2,1)S(1)}, u32[]{:S(2)}, u32[]{:S(2)}) collective-permute-start(bf16[256,2048]{1,0:T(8,128)(2,1)S(1)} %constant_dynamic-update-slice_fusion.4), channel_id=1, source_target_pairs={{0,1},{1,0},{2,3},{3,2},{4,5},{5,4},{6,7},{7,6},{8,9},{9,8},{10,11... | collective-permute-start | bytes 3145736 | tf_op jit(solution)/shard_map/ppermute | solution.py:240
  249.9 44.0 %collective-permute-start.16 = (bf16[1024,512]{1,0:T(8,128)(2,1)S(1)}, bf16[1024,512]{1,0:T(8,128)(2,1)S(1)}, u32[]{:S(2)}, u32[]{:S(2)}) collective-permute-start(bf16[1024,512]{1,0:T(8,128)(2,1)S(1)} %collective-permute-done.13), channel_id=1, source_target_pairs={{2,0},{4,6},{3,1},{5,7},{10,8},{12,14},{11,9},{13,15},{18,16},{20,... | collective-permute-start | bytes 3145736 | tf_op jit(solution)/shard_map/ppermute | solution.py:284
  348.6 33.7 %collective-permute-start.31 = (bf16[256,2048]{1,0:T(8,128)(2,1)S(1)}, bf16[256,2048]{1,0:T(8,128)(2,1)S(1)}, u32[]{:S(2)}, u32[]{:S(2)}) collective-permute-start(bf16[256,2048]{1,0:T(8,128)(2,1)S(1)} %convolution_convert_fusion.10), channel_id=1, source_target_pairs={{0,2},{6,4},{1,3},{7,5},{8,10},{14,12},{9,11},{15,13},{16,18},{22,... | collective-permute-start | bytes 3145736 | tf_op jit(solution)/shard_map/ppermute | solution.py:284
  449.7 34.9 %collective-permute-start.42 = (bf16[256,2048]{1,0:T(8,128)(2,1)S(1)}, bf16[256,2048]{1,0:T(8,128)(2,1)S(1)}, u32[]{:S(2)}, u32[]{:S(2)}) collective-permute-start(bf16[256,2048]{1,0:T(8,128)(2,1)S(1)} %collective-permute-done.38), channel_id=1, source_target_pairs={{2,0},{4,6},{3,1},{5,7},{10,8},{12,14},{11,9},{13,15},{18,16},{20,... | collective-permute-start | bytes 3145736 | tf_op jit(solution)/shard_map/ppermute | solution.py:284
  506.4 31.3 %collective-permute-start.41 = (bf16[256,2048]{1,0:T(8,128)(2,1)}, bf16[256,2048]{1,0:T(8,128)(2,1)}, u32[]{:S(2)}, u32[]{:S(2)}) collective-permute-start(bf16[256,2048]{1,0:T(8,128)(2,1)} %convolution_convert_fusion.6), channel_id=1, source_target_pairs={{0,2},{6,4},{1,3},{7,5},{8,10},{14,12},{9,11},{15,13},{16,18},{22,... | collective-permute-start | bytes 3145736 | tf_op jit(solution)/shard_map/ppermute | solution.py:284
  543.2 203.1 %reduce-scatter.5.cloned.1.call-start = ((), (), s32[]{:S(2)}) async-start(), calls=%async_computation.5 | async-start | bytes 9437184 | tf_op jit(solution)/shard_map/reduce_scatter | solution.py:582
  556.4 49.6 %collective-permute-start.51 = (f32[128,2048]{1,0:T(8,128)}, f32[128,2048]{1,0:T(8,128)}, u32[]{:S(2)}, u32[]{:S(2)}) collective-permute-start(f32[128,2048]{1,0:T(8,128)} %slice.326), channel_id=1, source_target_pairs={{0,1},{1,0},{2,3},{3,2},{4,5},{5,4},{6,7},{7,6},{8,9},{9,8},{10,11... | collective-permute-start | bytes 3145736 | tf_op jit(solution)/shard_map/ppermute | solution.py:240
  688.7 34.8 %collective-permute-start.54 = (bf16[256,2048]{1,0:T(8,128)(2,1)}, bf16[256,2048]{1,0:T(8,128)(2,1)}, u32[]{:S(2)}, u32[]{:S(2)}) collective-permute-start(bf16[256,2048]{1,0:T(8,128)(2,1)} %get-tuple-element.143), channel_id=1, source_target_pairs={{0,2},{6,4},{1,3},{7,5},{8,10},{14,12},{9,11},{15,13},{16,18},{22,... | collective-permute-start | bytes 3145736 | tf_op jit(solution)/shard_map/ppermute | solution.py:284
  715.8 42.0 %collective-permute-start.62 = (bf16[4,4,64,1536]{3,2,1,0:T(8,128)(2,1)}, bf16[4,4,64,1536]{3,2,1,0:T(8,128)(2,1)}, u32[]{:S(2)}, u32[]{:S(2)}) collective-permute-start(bf16[4,4,64,1536]{3,2,1,0:T(8,128)(2,1)} %dynamic-slice_bitcast_fusion), channel_id=1, source_target_pairs={{0,1},{1,0},{2,3},{3,2},{4,5},{5,4},{6,7},{7,6},{8,9},{9,8},{10,11... | collective-permute-start | bytes 9437192 | tf_op jit(solution)/shard_map/ppermute | solution.py:240
  747.3 31.5 %collective-permute-start.57 = (bf16[256,2048]{1,0:T(8,128)(2,1)}, bf16[256,2048]{1,0:T(8,128)(2,1)S(1)}, u32[]{:S(2)}, u32[]{:S(2)}) collective-permute-start(bf16[256,2048]{1,0:T(8,128)(2,1)} %add_convert_fusion.2), channel_id=1, source_target_pairs={{0,2},{2,0},{4,6},{6,4},{1,3},{3,1},{5,7},{7,5},{8,10},{10,8},{12,... | collective-permute-start | bytes 3145736 | tf_op jit(solution)/shard_map/ppermute | solution.py:284
  (138 other events, 1797.5 us)
Sparse Core Ops, SparseCore 0:
  40.0 51.5 all-gather.4
  94.0 54.3 all-gather.8
  172.8 75.6 all-gather.6
  543.3 75.7 reduce-scatter.2
  642.2 72.6 reduce-scatter.4
